TPU v7x, 32 devices: a whole 2x2x4 slice. The times are simulated.
32 devices in a mesh: dom: 8 (over z, y), ka: 4 (over x, core).
Axes of the slice: x: 2, y: 2, z: 4, core: 2. Of those that a mesh axis runs over, the one named last changes fastest.
Arguments:
- x_blocks: bfloat16 [64, 64, 2048], P('dom', None, 'ka'), may hold values from -0.29882812 to 0.29882812
- col_index: int32 [64, 32], P('dom'), may hold values from 0 to 63, as said below
- prod_index: int32 [64, 32], P('dom'), may hold values from 0 to 63, as said below
Outputs:
- purified: bfloat16 [64, 64, 2048], P('dom', None, 'ka')
Inputs may be any that keep to these rules, and one draw needn't show every extreme that they name: `col_index`: row i lists 32 distinct block columns (i + o) mod 64 with offsets o between -16 and 16, in ascending order of o; the offsets 0, -16 and 16 are always among them. `prod_index`: row i lists 32 distinct block columns (i + o) mod 64 with offsets o between -16 and 16, in ascending order of o; the offsets 0, -16 and 16 are always among them.
All inputs are finite; a program needn't handle non-finite values.
Results may differ from a plain program's by a relative error of at most 0.013.
Values may be sent and summed in bfloat16 or wider, within the bound.
No kernel may reach another device: no remote copies, remote signals or barrier semaphores. Data moves between devices by JAX's collectives and lax.ppermute only.
A program may use at most 128 MiB of HBM per device.

v0:
```python
import jax
import jax.numpy as jnp
from jax import lax
from jax.experimental import pallas as pl
from jax.experimental.pallas import tpu as pltpu
from jax.sharding import PartitionSpec as P


WINDOWS = 5
PIECES = 3


def permuted(value, pairs):
    return lax.ppermute(value, ("dom", "ka"), pairs)


def routes(dom_count, ka_count):
    def pairs(target):
        out = []
        for dom in range(dom_count):
            for group in range(ka_count):
                to = target(dom, group, group // 2, dom % 2)
                if to is not None:
                    out.append((dom * ka_count + group, (to[0] % dom_count) * ka_count + to[1]))
        return out

    def core(takers):
        return pairs(lambda d, g, x, y: (d, g ^ 1) if (g ^ 1) in takers(x, y) else None)

    return {
        "za": pairs(lambda d, g, x, y: (d + 2 if x else d - 2, g)),
        "zb": pairs(lambda d, g, x, y: (d - 2 if x else d + 2, g)),
        "x": pairs(lambda d, g, x, y: (d, g ^ 2)),
        "y": pairs(lambda d, g, x, y: (d ^ 1, g)),
        "dd": pairs(lambda d, g, x, y: (d + 1 if x else d - 1, g ^ 2)),
        "core": core(lambda x, y: (0, 1, 2, 3)),
        "core_dd": core(lambda x, y: (1, 2)),
        "core_oy": core(lambda x, y: ((1, 0), (3, 2))[x][y:y + 1]),
        "core_by": core(lambda x, y: ((0, 1), (2, 3))[x][y:y + 1]),
    }


def spread(pieces, shift, width, threshold):
    wide = jnp.concatenate(pieces, axis=1)
    low = wide[:, shift * 64:(shift + width) * 64]
    high = wide[:, (shift - 1) * 64:(shift - 1 + width) * 64]
    place = lax.broadcasted_iota(jnp.int32, low.shape, 1)
    zero = jnp.zeros_like(low)
    return jnp.where(place < threshold * 64, low, jnp.where(place >= threshold * 64 + 64, high, zero))


def kept(total, row, threshold, width):
    low = total[:, row * 64:row * 64 + width]
    high = total[:, (row + 1) * 64:(row + 1) * 64 + width]
    place = lax.broadcasted_iota(jnp.int32, low.shape, 1)
    return jnp.where(place < threshold * 64, low, high)


def fill_left(left_ref, rows_of, threshold, order, row_count):
    for row in range(row_count):
        blocks = rows_of(row)
        pad = jnp.zeros((64, 512), blocks[0].dtype)
        dense = spread([pad] + blocks + [pad], 8 - row, WINDOWS * 8, threshold(row))
        for window in range(WINDOWS):
            at = pl.ds(pl.multiple_of(order(window) * 512, 512), 512)
            left_ref[row * 64:(row + 1) * 64, at] = dense[:, window * 512:(window + 1) * 512]


def collect(store, items, dest, valid):
    for number, item in enumerate(items):
        @pl.when(dest(number) >= 0)
        def _():
            store[dest(number)] = item[...]
    for place in range(store.shape[0]):
        @pl.when(valid(place) == 0)
        def _():
            store[place] = jnp.zeros(store.shape[1:], store.dtype)


def zero_invalid(store, valid):
    for place in range(store.shape[0]):
        @pl.when(valid(place) == 0)
        def _():
            store[place] = jnp.zeros(store.shape[1:], store.dtype)


def collected(items, store, sems, dest):
    copies = []
    for number, item in enumerate(items):
        place = dest(number)
        copy = pltpu.make_async_copy(item, store.at[jnp.maximum(place, 0)], sems.at[number])
        copies.append((place >= 0, copy))
    return copies


def start_all(copies):
    for needed, copy in copies:
        pl.when(needed)(copy.start)


def wait_all(copies):
    for needed, copy in copies:
        pl.when(needed)(copy.wait)


def windows(store, table_ref, count, threshold):
    row_count = store.shape[1]
    for window in range(count):
        for row in range(row_count):
            blocks = [store[window * PIECES + piece, row] for piece in range(PIECES)]
            at = window * 512 + row * 64
            table_ref[at:at + 64, :] = spread(blocks, 8 - row, 16, threshold(window * 8 + row))


def product(left_ref, table_ref, total_ref, before_ref=None):
    depth = table_ref.shape[0]

    def step(tile, carry):
        cols = pl.ds(pl.multiple_of(tile * 256, 256), 256)
        value = jnp.dot(left_ref[:, :depth], table_ref[:, cols], preferred_element_type=jnp.float32)
        total_ref[:, cols] = value if before_ref is None else before_ref[:, cols] + value
        return carry

    lax.fori_loop(0, table_ref.shape[1] // 256, step, 0)


def near_kernel(meta_ref, dest_ref, *refs):
    items = refs[:8]
    left_out, table_out, total_out, left_store, store, left, left_far, table, total, sems, left_sems, out_sems = refs[8:]
    row_count = left_store.shape[1]
    left_in = [
        pltpu.make_async_copy(items[n], left_store.at[dest_ref[8 + n]], left_sems.at[n]) for n in range(4)
    ]
    for copy in left_in:
        copy.start()
    copies = collected(items, store, sems, lambda n: dest_ref[n])
    start_all(copies)
    zero_invalid(store, lambda p: dest_ref[16 + p])
    for copy in left_in:
        copy.wait()
    for row in range(row_count):
        pad = jnp.zeros((64, 512), left.dtype)
        blocks = [pad] + [left_store[h, row] for h in range(4)] + [pad]
        dense = spread(blocks, 8 - row, WINDOWS * 8, meta_ref[row])
        rows = slice(row * 64, (row + 1) * 64)
        left[rows, :512] = dense[:, 1024:1536]
        left_far[rows, 512:1024] = dense[:, :512]
        left_far[rows, 1024:] = dense[:, 2048:]

        @pl.when(meta_ref[30] > 0)
        def _():
            left[rows, 512:] = dense[:, 1536:2048]
            left_far[rows, :512] = dense[:, 512:1024]

        @pl.when(meta_ref[30] < 0)
        def _():
            left[rows, 512:] = dense[:, 512:1024]
            left_far[rows, :512] = dense[:, 1536:2048]
    outs = [pltpu.make_async_copy(*pair, out_sems.at[n]) for n, pair in enumerate(
        ((left_far, left_out), (table, table_out), (total, total_out)))]
    outs[0].start()
    wait_all(copies)
    windows(store, table, 2, lambda at: dest_ref[22 + at])
    outs[1].start()
    product(left, table, total)
    outs[2].start()
    for copy in outs:
        copy.wait()


def far_kernel(meta_ref, dest_ref, left_ref, before_ref, *refs):
    items = refs[:9]
    table_ref, square_ref, low_ref, store, total_ref = refs[9:]
    row_count = items[0].shape[0]
    collect(store, items, lambda n: dest_ref[n], lambda p: dest_ref[9 + p])
    for window in range(3):
        for row in range(row_count):
            blocks = [store[window * PIECES + piece, row] for piece in range(PIECES)]
            at = window * 512 + row * 64
            table_ref[at:at + 64, :] = spread(blocks, 8 - row, 16, dest_ref[18 + window * 8 + row])

    def step(tile, carry):
        cols = pl.ds(pl.multiple_of(tile * 256, 256), 256)
        total_ref[:, cols] = before_ref[:, cols] + jnp.dot(
            left_ref[...], table_ref[:, cols], preferred_element_type=jnp.float32
        )
        return carry

    lax.fori_loop(0, 4, step, 0)
    for row in range(row_count):
        picked = kept(total_ref[row * 64:(row + 1) * 64, :], row, meta_ref[8 + row], 512)
        square_ref[row] = picked
        low_ref[row] = picked.astype(low_ref.dtype)


def cube_kernel(meta_ref, own_ref, core_ref, x_ref, far_ref, table_a, table_b, square_ref, out_ref,
                store, left_ref, total_ref):
    row_count = out_ref.shape[0]
    group = meta_ref[29]
    for bits, ref in enumerate((own_ref, core_ref, x_ref, far_ref)):
        store[group ^ bits] = ref[...]
    fill_left(left_ref, lambda row: [store[h, row] for h in range(4)],
              lambda row: meta_ref[16 + row], lambda chunk: meta_ref[24 + chunk], row_count)

    def step(tile, carry):
        cols = pl.ds(pl.multiple_of(tile * 256, 256), 256)
        total_ref[:, cols] = (
            jnp.dot(left_ref[:, :1024], table_a[:, cols], preferred_element_type=jnp.float32)
            + jnp.dot(left_ref[:, 1024:], table_b[:, cols], preferred_element_type=jnp.float32)
        )
        return carry

    lax.fori_loop(0, 4, step, 0)
    for row in range(row_count):
        cube = kept(total_ref[row * 64:(row + 1) * 64, :], row, meta_ref[8 + row], 512)
        out_ref[row] = (3.0 * square_ref[row] - 2.0 * cube).astype(out_ref.dtype)


def missing_places(index, rows, total_rows, reach):
    places = (index - rows[:, None] + reach) % total_rows
    slots = jnp.arange(index.shape[1], dtype=jnp.int32)[None, :]
    return jnp.sum((places == slots).astype(jnp.int32), axis=1)


def per_device(dom_count, ka_count, x_blocks, col_index, prod_index):
    row_count, block, width = x_blocks.shape
    reach = 2 * row_count
    total_rows = row_count * dom_count
    dom = lax.axis_index("dom")
    group = lax.axis_index("ka")
    x_side, y_side = group // 2, dom % 2
    sign = 2 * x_side - 1
    same = x_side == y_side
    other = jnp.logical_not(same)
    near = 1 - 2 * y_side
    route = routes(dom_count, ka_count)
    steps = jnp.arange(row_count, dtype=jnp.int32)

    def missing(index, delta):
        there = (dom + delta) % dom_count * row_count + steps
        return missing_places(index, there, total_rows, reach)

    def along(value, source):
        return lax.ppermute(value, "dom", [(source(d) % dom_count, d) for d in range(dom_count)])

    from_near = along(col_index, lambda d: d ^ 1)
    from_far = along(col_index, lambda d: d + 1 if d % 2 else d - 1)
    from_before = along(col_index, lambda d: d - 2)
    from_after = along(col_index, lambda d: d + 2)
    own = x_blocks
    za = permuted(own, route["za"])
    zb = permuted(own, route["zb"])
    ox = permuted(own, route["x"])
    oy = permuted(own, route["y"])
    dd = permuted(own, route["dd"])
    own_core = permuted(own, route["core"])
    ox_core = permuted(ox, route["core"])
    oy_core = permuted(oy, route["core_oy"])
    dd_core = permuted(dd, route["core_dd"])
    bx = permuted(za, route["x"])
    by = permuted(jnp.where(same, za, zb), route["y"])
    z_core = permuted(jnp.where((group == 0) | (group == 3), za, zb), route["core"])
    from_near, from_far, from_before, from_after, bx = lax.optimization_barrier(
        (from_near, from_far, from_before, from_after, bx)
    )
    bx_core = permuted(bx, route["core"])
    by_core = permuted(by, route["core_by"])

    place = {0: missing(col_index, 0), "near": missing(from_near, near), "far": missing(from_far, -near),
             -2: missing(from_before, -2), 2: missing(from_after, 2)}
    prod_place = missing(prod_index, 0)

    def dest_of(entries, window_of):
        out = []
        for delta, shard, valid in entries:
            piece = shard - group + delta + 1
            ok = valid & (piece >= 0) & (piece < PIECES)
            out.append(jnp.where(ok, window_of(delta) * PIECES + piece, -1))
        return out

    def valid_of(delta):
        shards = [group - delta - 1 + piece for piece in range(PIECES)]
        return [((shard >= 0) & (shard < ka_count)).astype(jnp.int32) for shard in shards]

    def threshold(delta, key):
        return place[key] - 8 * (group - delta) + steps

    def table_of(scalars, vectors):
        return jnp.concatenate([jnp.stack(scalars)] + vectors).astype(jnp.int32)

    order = [jnp.int32(3), 2 - (near == -1), jnp.int32(0), 2 - (near == 1), jnp.int32(4)]
    meta = jnp.concatenate(
        [place[0] + steps, prod_place - 8 * group, prod_place + steps, jnp.stack(order + [group, near])]
    ).astype(jnp.int32)

    yes = jnp.bool_(True)
    near_items = (own, own_core, ox, ox_core, oy, oy_core, dd, dd_core)
    near_dest = dest_of(
        [(0, group ^ bits, yes) for bits in range(4)]
        + [(near, group, yes), (near, group ^ 1, yes), (near, group ^ 2, other), (near, group ^ 3, other)],
        lambda delta: 0 if isinstance(delta, int) else 1,
    )
    near_table = table_of(
        near_dest + [group ^ bits for bits in range(4)] + [group * 0] * 4 + valid_of(0) + valid_of(near),
        [threshold(0, 0), threshold(near, "near")],
    )
    far_items = (za, zb, z_core, bx, bx_core, by, by_core, dd, dd_core)
    far_dest = dest_of(
        [
            (-2 * sign, group, yes),
            (2 * sign, group, yes),
            (jnp.where((group == 0) | (group == 2), -2, 2), group ^ 1, yes),
            (2 * sign, group ^ 2, yes),
            (2 * sign, group ^ 3, yes),
            (-near, group, yes),
            (-near, group ^ 1, yes),
            (-near, group ^ 2, same),
            (-near, group ^ 3, same),
        ],
        lambda delta: jnp.where(delta == -2, 1, jnp.where(delta == 2, 2, 0)),
    )
    far_table = table_of(
        far_dest + valid_of(-near) + valid_of(-2) + valid_of(2),
        [threshold(-near, "far"), threshold(-2, -2), threshold(2, 2)],
    )

    smem = pl.BlockSpec(memory_space=pltpu.SMEM)
    vmem = pl.BlockSpec(memory_space=pltpu.VMEM)
    hbm = pl.BlockSpec(memory_space=pltpu.HBM)
    shards = (row_count, block, width)
    rows, depth, columns = row_count * block, WINDOWS * 8 * block, 16 * block
    shape = jax.ShapeDtypeStruct
    bf16, f32 = jnp.bfloat16, jnp.float32

    small = pltpu.CompilerParams(vmem_limit_bytes=28 << 20)

    def cost(k):
        return pl.CostEstimate(flops=2 * rows * k * columns * 2, bytes_accessed=12 << 20, transcendentals=0)

    left_far, table_a, total = pl.pallas_call(
        near_kernel,
        out_shape=(pltpu.HBM((rows, 1536), bf16), pltpu.HBM((1024, columns), bf16), pltpu.HBM((rows, columns), f32)),
        in_specs=[smem, smem] + [hbm] * 8,
        out_specs=(hbm,) * 3,
        scratch_shapes=[
            pltpu.VMEM((ka_count,) + shards, bf16),
            pltpu.VMEM((2 * PIECES,) + shards, bf16),
            pltpu.VMEM((rows, 1024), bf16),
            pltpu.VMEM((rows, 1536), bf16),
            pltpu.VMEM((1024, columns), bf16),
            pltpu.VMEM((rows, columns), f32),
            pltpu.SemaphoreType.DMA((8,)),
            pltpu.SemaphoreType.DMA((4,)),
            pltpu.SemaphoreType.DMA((3,)),
        ],
        compiler_params=small,
        cost_estimate=cost(1024),
    )(meta, near_table, *[pltpu.with_memory_space_constraint(v, pltpu.HBM) for v in near_items])

    table_b, square, low = pl.pallas_call(
        far_kernel,
        out_shape=(
            shape((1536, columns), bf16),
            shape((row_count, block, width), f32),
            shape((row_count, block, width), bf16),
        ),
        in_specs=[smem, smem] + [vmem] * 11,
        out_specs=(vmem, vmem, vmem),
        scratch_shapes=[
            pltpu.VMEM((3 * PIECES, row_count, block, width), bf16),
            pltpu.VMEM((rows, columns), f32),
        ],
        compiler_params=small,
        cost_estimate=cost(1536),
    )(meta, far_table, *[pltpu.with_memory_space_constraint(v, pltpu.HBM) for v in (left_far, total, za, zb)],
      *far_items[2:7], *[pltpu.with_memory_space_constraint(v, pltpu.HBM) for v in (dd, dd_core)])

    low_x = permuted(low, route["x"])
    low_core = permuted(low, route["core"])
    low_far = permuted(low_x, route["core"])
    return pl.pallas_call(
        cube_kernel,
        out_shape=shape((row_count, block, width), bf16),
        in_specs=[smem] + [vmem] * 7,
        out_specs=vmem,
        scratch_shapes=[
            pltpu.VMEM((ka_count, row_count, block, width), bf16),
            pltpu.VMEM((rows, depth), bf16),
            pltpu.VMEM((rows, columns), f32),
        ],
        compiler_params=small,
    )(meta, low, low_core, low_x, low_far, table_a, table_b, square)


def solution(mesh):
    def body(*args):
        return per_device(mesh.shape["dom"], mesh.shape["ka"], *args)

    return jax.shard_map(
        body,
        mesh=mesh,
        in_specs=(P("dom", None, "ka"), P("dom", None), P("dom", None)),
        out_specs=P("dom", None, "ka"),
        check_vma=False,
    )
```

profile of v0, /device:TPU:0, one launch (start us, length us, event | category | flops | bytes accessed | tf_op | source)
XLA Modules:
  0.0 97.3 jit_solution(14992248850962492359)
XLA Ops:
  0.0 6.0 %collective-permute-start.1 = (s32[8,32]{1,0:T(8,128)}, s32[8,32]{1,0:T(8,128)S(1)}, u32[]{:S(2)}, u32[]{:S(2)}) collective-permute-start(s32[8,32]{1,0:T(8,128)} %param.4), channel_id=1, source_target_pairs={{28,0},{8,4},{4,8},{16,12},{12,16},{24,20},{20,24},{0,28},{29,1},{... | collective-permute-start | bytes 3080 | tf_op jit(solution)/shard_map/ppermute | solution.py:244
  6.0 0.6 collective-permute-start.3
  6.7 1.9 %collective-permute-start.4 = (bf16[8,64,512]{2,1,0:T(8,128)(2,1)}, bf16[8,64,512]{2,1,0:T(8,128)(2,1)S(1)}, u32[]{:S(2)}, u32[]{:S(2)}) collective-permute-start(bf16[8,64,512]{2,1,0:T(8,128)(2,1)} %refs_0_.1), channel_id=1, source_target_pairs={{0,24},{1,25},{2,10},{3,11},{4,28},{5,29},{6,14},{7,15},{8,0},{9,1... | collective-permute-start | bytes 1572872 | tf_op jit(solution)/shard_map/ppermute | solution.py:14
  8.6 0.1 collective-permute-start.13
  8.7 0.9 convert_reduce_fusion.4
  9.7 4.1 %collective-permute-start.11 = (bf16[8,64,512]{2,1,0:T(8,128)(2,1)}, bf16[8,64,512]{2,1,0:T(8,128)(2,1)}, u32[]{:S(2)}, u32[]{:S(2)}) collective-permute-start(bf16[8,64,512]{2,1,0:T(8,128)(2,1)} %refs_0_.1), channel_id=1, source_target_pairs={{0,30},{1,31},{2,4},{3,5},{4,2},{5,3},{6,8},{7,9},{8,6},{9,7},{10,... | collective-permute-start | bytes 1572872 | tf_op jit(solution)/shard_map/ppermute | solution.py:14
  13.8 0.8 collective-permute-start.9
  14.6 0.4 collective-permute-start.7
  15.0 17.5 %collective-permute-done.4.refs_0_ = bf16[8,64,512]{2,1,0:T(8,128)(2,1)S(1)} collective-permute-done((bf16[8,64,512]{2,1,0:T(8,128)(2,1)}, bf16[8,64,512]{2,1,0:T(8,128)(2,1)S(1)}, u32[]{:S(2)}, u32[]{:S(2)}) %collective-permute-start.4) | collective-permute-done | bytes 524320 | tf_op jit(solution)/shard_map/ppermute | solution.py:14
  33.1 0.2 collective-permute-done.13.refs_1_
  33.3 1.7 %collective-permute-start.2 = (s32[8,32]{1,0:T(8,128)}, s32[8,32]{1,0:T(8,128)S(1)}, u32[]{:S(2)}, u32[]{:S(2)}) collective-permute-start(s32[8,32]{1,0:T(8,128)} %param.4), channel_id=1, source_target_pairs={{24,0},{28,4},{0,8},{4,12},{8,16},{12,20},{16,24},{20,28},{25,1},{... | collective-permute-start | bytes 3080 | tf_op jit(solution)/shard_map/ppermute | solution.py:244
  35.0 0.9 broadcast_select_fusion
  35.9 7.0 %collective-permute-done.2 = s32[8,32]{1,0:T(8,128)S(1)} collective-permute-done((s32[8,32]{1,0:T(8,128)}, s32[8,32]{1,0:T(8,128)S(1)}, u32[]{:S(2)}, u32[]{:S(2)}) %collective-permute-start.2) | collective-permute-done | bytes 1056 | tf_op jit(solution)/shard_map/ppermute | solution.py:244
  42.8 3.6 %collective-permute-done.11.refs_6_.refs_7_ = bf16[8,64,512]{2,1,0:T(8,128)(2,1)} collective-permute-done((bf16[8,64,512]{2,1,0:T(8,128)(2,1)}, bf16[8,64,512]{2,1,0:T(8,128)(2,1)}, u32[]{:S(2)}, u32[]{:S(2)}) %collective-permute-start.11) | collective-permute-done | bytes 524320 | tf_op jit(solution)/shard_map/ppermute | solution.py:14
  46.4 1.3 %collective-permute-start.12 = (bf16[8,64,512]{2,1,0:T(8,128)(2,1)}, bf16[8,64,512]{2,1,0:T(8,128)(2,1)S(1)}, u32[]{:S(2)}, u32[]{:S(2)}) collective-permute-start(bf16[8,64,512]{2,1,0:T(8,128)(2,1)} %collective-permute-done.11.refs_6_.refs_7_), channel_id=1, source_target_pairs={{0,1},{3,2},{4,5},{7,6},{8,9},{11,10},{12,13},{15,14},{16,17},{19,... | collective-permute-start | bytes 1572872 | tf_op jit(solution)/shard_map/ppermute | solution.py:14
  47.8 2.1 %collective-permute-start.10 = (bf16[8,64,512]{2,1,0:T(8,128)(2,1)}, bf16[8,64,512]{2,1,0:T(8,128)(2,1)}, u32[]{:S(2)}, u32[]{:S(2)}) collective-permute-start(bf16[8,64,512]{2,1,0:T(8,128)(2,1)} %collective-permute-done.9.refs_4_), channel_id=1, source_target_pairs={{0,1},{2,3},{5,4},{7,6},{8,9},{10,11},{13,12},{15,14},{16,17},{18,... | collective-permute-start | bytes 1572872 | tf_op jit(solution)/shard_map/ppermute | solution.py:14
  49.9 0.2 convert_reduce_fusion.2
  50.2 0.2 convert_reduce_fusion
  50.4 0.6 collective-permute-start.14
  51.0 0.1 collective-permute-start.15
  51.1 7.3 %collective-permute-done.16.refs_5_ = bf16[8,64,512]{2,1,0:T(8,128)(2,1)S(1)} collective-permute-done((bf16[8,64,512]{2,1,0:T(8,128)(2,1)S(1)}, bf16[8,64,512]{2,1,0:T(8,128)(2,1)S(1)}, u32[]{:S(2)}, u32[]{:S(2)}) %collective-permute-start.16) | collective-permute-done | bytes 524320 | tf_op jit(solution)/shard_map/ppermute | solution.py:14
  58.3 1.3 %collective-permute-start.17 = (bf16[8,64,512]{2,1,0:T(8,128)(2,1)S(1)}, bf16[8,64,512]{2,1,0:T(8,128)(2,1)S(1)}, u32[]{:S(2)}, u32[]{:S(2)}) collective-permute-start(bf16[8,64,512]{2,1,0:T(8,128)(2,1)S(1)} %collective-permute-done.16.refs_5_), channel_id=1, source_target_pairs={{1,0},{3,2},{4,5},{6,7},{9,8},{11,10},{12,13},{14,15},{17,16},{19,... | collective-permute-start | bytes 1572872 | tf_op jit(solution)/shard_map/ppermute | solution.py:14
  59.7 0.1 concatenate.11.dest_ref
  59.8 0.1 concatenate.10.dest_ref
  59.9 7.7 %shard_map.37 = (bf16[512,1536]{1,0:T(8,128)(2,1)}, bf16[1024,1024]{1,0:T(8,128)(2,1)}, f32[512,1024]{1,0:T(8,128)}) custom-call(s32[31]{0:T(128)S(1)} %concatenate.9.meta_ref, s32[38]{0:T(128)S(1)} %concatenate.11.dest_ref, bf16[8,64,512]{2,1,0:T(8,128)(2,1)} %refs_0_.1, bf16[8,64,512]{2,1,0:T(8,128)(2,1)} %copy-done.5, ...), custom_call_target="tpu_custom_call" | custom-call | flops 2147483648 | bytes 12582912 | tf_op jit(solution)/shard_map/pallas_call | solution.py:340
  67.7 7.0 %shard_map.38 = (bf16[1536,1024]{1,0:T(8,128)(2,1)S(1)}, f32[8,64,512]{2,1,0:T(8,128)S(1)}, bf16[8,64,512]{2,1,0:T(8,128)(2,1)S(1)}) custom-call(s32[31]{0:T(128)S(1)} %concatenate.9.meta_ref, s32[42]{0:T(128)S(1)} %concatenate.10.dest_ref, bf16[512,1536]{1,0:T(8,128)(2,1)} %get-tuple-element.20.left_ref, f32[512,1024]{1,0:T(8,128)} %get-tuple-element.21.before_ref, ...), custom_call_target="tpu_custom_call" | custom-call | flops 3221225472 | bytes 12582912 | tf_op jit(solution)/shard_map/pallas_call | solution.py:360
  74.6 2.2 %collective-permute-start.19 = (bf16[8,64,512]{2,1,0:T(8,128)(2,1)S(1)}, bf16[8,64,512]{2,1,0:T(8,128)(2,1)S(1)}, u32[]{:S(2)}, u32[]{:S(2)}) collective-permute-start(bf16[8,64,512]{2,1,0:T(8,128)(2,1)S(1)} %get-tuple-element.23.own_ref), channel_id=1, source_target_pairs={{0,2},{1,3},{2,0},{3,1},{4,6},{5,7},{6,4},{7,5},{8,10},{9,11},{10,... | collective-permute-start | bytes 1572872 | tf_op jit(solution)/shard_map/ppermute | solution.py:14
  76.9 0.8 collective-permute-start.18
  77.6 11.6 %collective-permute-done.19.x_ref = bf16[8,64,512]{2,1,0:T(8,128)(2,1)S(1)} collective-permute-done((bf16[8,64,512]{2,1,0:T(8,128)(2,1)S(1)}, bf16[8,64,512]{2,1,0:T(8,128)(2,1)S(1)}, u32[]{:S(2)}, u32[]{:S(2)}) %collective-permute-start.19) | collective-permute-done | bytes 524320 | tf_op jit(solution)/shard_map/ppermute | solution.py:14
  89.3 0.2 collective-permute-start.20
  89.5 1.7 %collective-permute-done.20.far_ref = bf16[8,64,512]{2,1,0:T(8,128)(2,1)S(1)} collective-permute-done((bf16[8,64,512]{2,1,0:T(8,128)(2,1)S(1)}, bf16[8,64,512]{2,1,0:T(8,128)(2,1)S(1)}, u32[]{:S(2)}, u32[]{:S(2)}) %collective-permute-start.20) | collective-permute-done | bytes 524320 | tf_op jit(solution)/shard_map/ppermute | solution.py:14
  91.2 6.2 %shard_map.39 = bf16[8,64,512]{2,1,0:T(8,128)(2,1)} custom-call(s32[31]{0:T(128)S(1)} %concatenate.9.meta_ref, bf16[8,64,512]{2,1,0:T(8,128)(2,1)S(1)} %get-tuple-element.23.own_ref, bf16[8,64,512]{2,1,0:T(8,128)(2,1)S(1)} %collective-permute-done.18.core_ref, bf16[8,64,512]{2,1,0:T(8,128)(2,1)S(1)} %collective-permute-done.19.x_ref, ...), custom_call_target="tpu_custom_call" | custom-call | tf_op jit(solution)/shard_map/pallas_call | solution.py:381
  (43 shorter events, 0.2 us)
Async XLA Ops:
  0.0 42.8 %copy-start.3 = (bf16[8,64,512]{2,1,0:T(8,128)(2,1)S(1)}, bf16[8,64,512]{2,1,0:T(8,128)(2,1)}, u32[]{:S(2)}) copy-start(bf16[8,64,512]{2,1,0:T(8,128)(2,1)} %refs_0_.1) | copy-start | bytes 1572868
  0.0 9.7 %collective-permute-start.1 = (s32[8,32]{1,0:T(8,128)}, s32[8,32]{1,0:T(8,128)S(1)}, u32[]{:S(2)}, u32[]{:S(2)}) collective-permute-start(s32[8,32]{1,0:T(8,128)} %param.4), channel_id=1, source_target_pairs={{28,0},{8,4},{4,8},{16,12},{12,16},{24,20},{20,24},{0,28},{29,1},{... | collective-permute-start | bytes 3080 | tf_op jit(solution)/shard_map/ppermute | solution.py:244
  6.0 7.7 %collective-permute-start = (s32[8,32]{1,0:T(8,128)}, s32[8,32]{1,0:T(8,128)S(1)}, u32[]{:S(2)}, u32[]{:S(2)}) collective-permute-start(s32[8,32]{1,0:T(8,128)} %param.4), channel_id=1, source_target_pairs={{4,0},{0,4},{12,8},{8,12},{20,16},{16,20},{28,24},{24,28},{5,1},{1... | collective-permute-start | bytes 3080 | tf_op jit(solution)/shard_map/ppermute | solution.py:244
  6.0 8.6 %collective-permute-start.3 = (s32[8,32]{1,0:T(8,128)}, s32[8,32]{1,0:T(8,128)S(1)}, u32[]{:S(2)}, u32[]{:S(2)}) collective-permute-start(s32[8,32]{1,0:T(8,128)} %param.4), channel_id=1, source_target_pairs={{8,0},{12,4},{16,8},{20,12},{24,16},{28,20},{0,24},{4,28},{9,1},{1... | collective-permute-start | bytes 3080 | tf_op jit(solution)/shard_map/ppermute | solution.py:244
  6.7 25.9 %collective-permute-start.4 = (bf16[8,64,512]{2,1,0:T(8,128)(2,1)}, bf16[8,64,512]{2,1,0:T(8,128)(2,1)S(1)}, u32[]{:S(2)}, u32[]{:S(2)}) collective-permute-start(bf16[8,64,512]{2,1,0:T(8,128)(2,1)} %refs_0_.1), channel_id=1, source_target_pairs={{0,24},{1,25},{2,10},{3,11},{4,28},{5,29},{6,14},{7,15},{8,0},{9,1... | collective-permute-start | bytes 1572872 | tf_op jit(solution)/shard_map/ppermute | solution.py:14
  8.6 24.7 %collective-permute-start.13 = (bf16[8,64,512]{2,1,0:T(8,128)(2,1)}, bf16[8,64,512]{2,1,0:T(8,128)(2,1)S(1)}, u32[]{:S(2)}, u32[]{:S(2)}) collective-permute-start(bf16[8,64,512]{2,1,0:T(8,128)(2,1)} %refs_0_.1), channel_id=1, source_target_pairs={{0,8},{1,9},{2,26},{3,27},{4,12},{5,13},{6,30},{7,31},{8,16},{9,17... | collective-permute-start | bytes 1572872 | tf_op jit(solution)/shard_map/ppermute | solution.py:14
  9.7 36.7 %collective-permute-start.11 = (bf16[8,64,512]{2,1,0:T(8,128)(2,1)}, bf16[8,64,512]{2,1,0:T(8,128)(2,1)}, u32[]{:S(2)}, u32[]{:S(2)}) collective-permute-start(bf16[8,64,512]{2,1,0:T(8,128)(2,1)} %refs_0_.1), channel_id=1, source_target_pairs={{0,30},{1,31},{2,4},{3,5},{4,2},{5,3},{6,8},{7,9},{8,6},{9,7},{10,... | collective-permute-start | bytes 1572872 | tf_op jit(solution)/shard_map/ppermute | solution.py:14
  13.8 32.7 %collective-permute-start.9 = (bf16[8,64,512]{2,1,0:T(8,128)(2,1)}, bf16[8,64,512]{2,1,0:T(8,128)(2,1)}, u32[]{:S(2)}, u32[]{:S(2)}) collective-permute-start(bf16[8,64,512]{2,1,0:T(8,128)(2,1)} %refs_0_.1), channel_id=1, source_target_pairs={{0,4},{1,5},{2,6},{3,7},{4,0},{5,1},{6,2},{7,3},{8,12},{9,13},{10,... | collective-permute-start | bytes 1572872 | tf_op jit(solution)/shard_map/ppermute | solution.py:14
  14.6 33.1 %collective-permute-start.7 = (bf16[8,64,512]{2,1,0:T(8,128)(2,1)}, bf16[8,64,512]{2,1,0:T(8,128)(2,1)}, u32[]{:S(2)}, u32[]{:S(2)}) collective-permute-start(bf16[8,64,512]{2,1,0:T(8,128)(2,1)} %refs_0_.1), channel_id=1, source_target_pairs={{0,2},{1,3},{2,0},{3,1},{4,6},{5,7},{6,4},{7,5},{8,10},{9,11},{10,... | collective-permute-start | bytes 1572872 | tf_op jit(solution)/shard_map/ppermute | solution.py:14
  32.5 35.1 %copy-start.1 = (bf16[8,64,512]{2,1,0:T(8,128)(2,1)}, bf16[8,64,512]{2,1,0:T(8,128)(2,1)S(1)}, u32[]{:S(2)}) copy-start(bf16[8,64,512]{2,1,0:T(8,128)(2,1)S(1)} %collective-permute-done.4.refs_0_) | copy-start | bytes 1572868
  32.5 17.4 %collective-permute-start.5 = (bf16[8,64,512]{2,1,0:T(8,128)(2,1)S(1)}, bf16[8,64,512]{2,1,0:T(8,128)(2,1)S(1)}, u32[]{:S(2)}, u32[]{:S(2)}) collective-permute-start(bf16[8,64,512]{2,1,0:T(8,128)(2,1)S(1)} %collective-permute-done.4.refs_0_), channel_id=1, source_target_pairs={{0,2},{1,3},{2,0},{3,1},{4,6},{5,7},{6,4},{7,5},{8,10},{9,11},{10,... | collective-permute-start | bytes 1572872 | tf_op jit(solution)/shard_map/ppermute | solution.py:14
  33.3 13.1 %copy-start.2 = (bf16[8,64,512]{2,1,0:T(8,128)(2,1)}, bf16[8,64,512]{2,1,0:T(8,128)(2,1)S(1)}, u32[]{:S(2)}) copy-start(bf16[8,64,512]{2,1,0:T(8,128)(2,1)S(1)} %collective-permute-done.13.refs_1_) | copy-start | bytes 1572868
  33.3 9.5 %collective-permute-start.2 = (s32[8,32]{1,0:T(8,128)}, s32[8,32]{1,0:T(8,128)S(1)}, u32[]{:S(2)}, u32[]{:S(2)}) collective-permute-start(s32[8,32]{1,0:T(8,128)} %param.4), channel_id=1, source_target_pairs={{24,0},{28,4},{0,8},{4,12},{8,16},{12,20},{16,24},{20,28},{25,1},{... | collective-permute-start | bytes 3080 | tf_op jit(solution)/shard_map/ppermute | solution.py:244
  42.8 7.6 %collective-permute-start.6 = (bf16[8,64,512]{2,1,0:T(8,128)(2,1)S(1)}, bf16[8,64,512]{2,1,0:T(8,128)(2,1)S(1)}, u32[]{:S(2)}, u32[]{:S(2)}) collective-permute-start(bf16[8,64,512]{2,1,0:T(8,128)(2,1)S(1)} %copy-done.3), channel_id=1, source_target_pairs={{0,1},{1,0},{2,3},{3,2},{4,5},{5,4},{6,7},{7,6},{8,9},{9,8},{10,11... | collective-permute-start | bytes 1572872 | tf_op jit(solution)/shard_map/ppermute | solution.py:14
  46.4 11.9 %collective-permute-start.16 = (bf16[8,64,512]{2,1,0:T(8,128)(2,1)S(1)}, bf16[8,64,512]{2,1,0:T(8,128)(2,1)S(1)}, u32[]{:S(2)}, u32[]{:S(2)}) collective-permute-start(bf16[8,64,512]{2,1,0:T(8,128)(2,1)S(1)} %get-tuple-element.29), channel_id=1, source_target_pairs={{0,4},{1,5},{2,6},{3,7},{4,0},{5,1},{6,2},{7,3},{8,12},{9,13},{10,... | collective-permute-start | bytes 1572872 | tf_op jit(solution)/shard_map/ppermute | solution.py:14
  46.4 4.5 %collective-permute-start.12 = (bf16[8,64,512]{2,1,0:T(8,128)(2,1)}, bf16[8,64,512]{2,1,0:T(8,128)(2,1)S(1)}, u32[]{:S(2)}, u32[]{:S(2)}) collective-permute-start(bf16[8,64,512]{2,1,0:T(8,128)(2,1)} %collective-permute-done.11.refs_6_.refs_7_), channel_id=1, source_target_pairs={{0,1},{3,2},{4,5},{7,6},{8,9},{11,10},{12,13},{15,14},{16,17},{19,... | collective-permute-start | bytes 1572872 | tf_op jit(solution)/shard_map/ppermute | solution.py:14
  47.8 12.1 %collective-permute-start.10 = (bf16[8,64,512]{2,1,0:T(8,128)(2,1)}, bf16[8,64,512]{2,1,0:T(8,128)(2,1)}, u32[]{:S(2)}, u32[]{:S(2)}) collective-permute-start(bf16[8,64,512]{2,1,0:T(8,128)(2,1)} %collective-permute-done.9.refs_4_), channel_id=1, source_target_pairs={{0,1},{2,3},{5,4},{7,6},{8,9},{10,11},{13,12},{15,14},{16,17},{18,... | collective-permute-start | bytes 1572872 | tf_op jit(solution)/shard_map/ppermute | solution.py:14
  49.9 10.0 %collective-permute-start.8 = (bf16[8,64,512]{2,1,0:T(8,128)(2,1)}, bf16[8,64,512]{2,1,0:T(8,128)(2,1)}, u32[]{:S(2)}, u32[]{:S(2)}) collective-permute-start(bf16[8,64,512]{2,1,0:T(8,128)(2,1)} %collective-permute-done.7.refs_2_), channel_id=1, source_target_pairs={{0,1},{1,0},{2,3},{3,2},{4,5},{5,4},{6,7},{7,6},{8,9},{9,8},{10,11... | collective-permute-start | bytes 1572872 | tf_op jit(solution)/shard_map/ppermute | solution.py:14
  50.4 9.3 %copy-start.5 = (bf16[8,64,512]{2,1,0:T(8,128)(2,1)}, bf16[8,64,512]{2,1,0:T(8,128)(2,1)S(1)}, u32[]{:S(2)}) copy-start(bf16[8,64,512]{2,1,0:T(8,128)(2,1)S(1)} %collective-permute-done.6.refs_1_) | copy-start | bytes 1572868
  50.4 17.2 %collective-permute-start.14 = (bf16[8,64,512]{2,1,0:T(8,128)(2,1)}, bf16[8,64,512]{2,1,0:T(8,128)(2,1)S(1)}, u32[]{:S(2)}, u32[]{:S(2)}) collective-permute-start(bf16[8,64,512]{2,1,0:T(8,128)(2,1)} %get-tuple-element.30), channel_id=1, source_target_pairs={{0,1},{1,0},{2,3},{3,2},{4,5},{5,4},{6,7},{7,6},{8,9},{9,8},{10,11... | collective-permute-start | bytes 1572872 | tf_op jit(solution)/shard_map/ppermute | solution.py:14
  51.0 8.7 %copy-start.4 = (bf16[8,64,512]{2,1,0:T(8,128)(2,1)}, bf16[8,64,512]{2,1,0:T(8,128)(2,1)S(1)}, u32[]{:S(2)}) copy-start(bf16[8,64,512]{2,1,0:T(8,128)(2,1)S(1)} %collective-permute-done.12.refs_7_.refs_8_) | copy-start | bytes 1572868
  51.0 16.7 %collective-permute-start.15 = (bf16[8,64,512]{2,1,0:T(8,128)(2,1)S(1)}, bf16[8,64,512]{2,1,0:T(8,128)(2,1)S(1)}, u32[]{:S(2)}, u32[]{:S(2)}) collective-permute-start(bf16[8,64,512]{2,1,0:T(8,128)(2,1)S(1)} %collective-permute-done.5.refs_3_), channel_id=1, source_target_pairs={{0,1},{1,0},{2,3},{3,2},{4,5},{5,4},{6,7},{7,6},{8,9},{9,8},{10,11... | collective-permute-start | bytes 1572872 | tf_op jit(solution)/shard_map/ppermute | solution.py:14
  58.3 9.3 %collective-permute-start.17 = (bf16[8,64,512]{2,1,0:T(8,128)(2,1)S(1)}, bf16[8,64,512]{2,1,0:T(8,128)(2,1)S(1)}, u32[]{:S(2)}, u32[]{:S(2)}) collective-permute-start(bf16[8,64,512]{2,1,0:T(8,128)(2,1)S(1)} %collective-permute-done.16.refs_5_), channel_id=1, source_target_pairs={{1,0},{3,2},{4,5},{6,7},{9,8},{11,10},{12,13},{14,15},{17,16},{19,... | collective-permute-start | bytes 1572872 | tf_op jit(solution)/shard_map/ppermute | solution.py:14
  67.7 23.5 %copy-start = (bf16[1024,1024]{1,0:T(8,128)(2,1)S(1)}, bf16[1024,1024]{1,0:T(8,128)(2,1)}, u32[]{:S(2)}) copy-start(bf16[1024,1024]{1,0:T(8,128)(2,1)} %get-tuple-element.24.table_a) | copy-start | bytes 6291460
  74.6 14.6 %collective-permute-start.19 = (bf16[8,64,512]{2,1,0:T(8,128)(2,1)S(1)}, bf16[8,64,512]{2,1,0:T(8,128)(2,1)S(1)}, u32[]{:S(2)}, u32[]{:S(2)}) collective-permute-start(bf16[8,64,512]{2,1,0:T(8,128)(2,1)S(1)} %get-tuple-element.23.own_ref), channel_id=1, source_target_pairs={{0,2},{1,3},{2,0},{3,1},{4,6},{5,7},{6,4},{7,5},{8,10},{9,11},{10,... | collective-permute-start | bytes 1572872 | tf_op jit(solution)/shard_map/ppermute | solution.py:14
  76.9 12.6 %collective-permute-start.18 = (bf16[8,64,512]{2,1,0:T(8,128)(2,1)S(1)}, bf16[8,64,512]{2,1,0:T(8,128)(2,1)S(1)}, u32[]{:S(2)}, u32[]{:S(2)}) collective-permute-start(bf16[8,64,512]{2,1,0:T(8,128)(2,1)S(1)} %get-tuple-element.23.own_ref), channel_id=1, source_target_pairs={{0,1},{1,0},{2,3},{3,2},{4,5},{5,4},{6,7},{7,6},{8,9},{9,8},{10,11... | collective-permute-start | bytes 1572872 | tf_op jit(solution)/shard_map/ppermute | solution.py:14
  89.3 1.9 %collective-permute-start.20 = (bf16[8,64,512]{2,1,0:T(8,128)(2,1)S(1)}, bf16[8,64,512]{2,1,0:T(8,128)(2,1)S(1)}, u32[]{:S(2)}, u32[]{:S(2)}) collective-permute-start(bf16[8,64,512]{2,1,0:T(8,128)(2,1)S(1)} %collective-permute-done.19.x_ref), channel_id=1, source_target_pairs={{0,1},{1,0},{2,3},{3,2},{4,5},{5,4},{6,7},{7,6},{8,9},{9,8},{10,11... | collective-permute-start | bytes 1572872 | tf_op jit(solution)/shard_map/ppermute | solution.py:14
where the time goes:
time: 97.6 us; the launch traced here: 97.3 us
  waiting for transfers between devices  48.9 us (50%)
  starting transfers between devices  24.2 us (25%)
  Pallas kernels  20.8 us (21%)
  other arithmetic  2.31 us (2%)
    ppermute x17, waiting for transfers between devices, permuted(): return lax.ppermute(value, ('dom', 'ka'), pairs)  41.9 us
    ppermute x17, starting transfers between devices, permuted(): return lax.ppermute(value, ('dom', 'ka'), pairs)  15.9 us
    ppermute x4, starting transfers between devices, along(): lax.ppermute(value, 'dom', [(source(d) % dom_count, d) for d in range(dom...  8.33 us
    pallas_call x1, Pallas kernels, per_device(): pl.pallas_call(near_kernel, out_shape=(pltpu.HBM((rows, 1536), bf16), plt...  7.7 us
    ppermute x4, waiting for transfers between devices, along(): lax.ppermute(value, 'dom', [(source(d) % dom_count, d) for d in range(dom...  6.97 us
    pallas_call x1, Pallas kernels, per_device(): pl.pallas_call(far_kernel, out_shape=(shape((1536, columns), bf16), shape...  6.95 us
    pallas_call x1, Pallas kernels, per_device(): pl.pallas_call(cube_kernel, out_shape=shape((row_count, block, width), bf...  6.17 us
  transfers between devices with their start and end apart: 21, of which 7 were waited for; matrix products, arithmetic and copies ran while one was open for 3% of the time, Pallas kernels for 8%

commit v1 on v0

--- a/solution.py
+++ b/solution.py
@@ -29,7 +29,7 @@
 
     return {
         "za": pairs(lambda d, g, x, y: (d + 2 if x else d - 2, g)),
-        "zb": pairs(lambda d, g, x, y: (d - 2 if x else d + 2, g)),
+        "zb": pairs(lambda d, g, x, y: (d - 2 if x else d + 2, g) if x != y or g in (1, 2) else None),
         "x": pairs(lambda d, g, x, y: (d, g ^ 2)),
         "y": pairs(lambda d, g, x, y: (d ^ 1, g)),
         "dd": pairs(lambda d, g, x, y: (d + 1 if x else d - 1, g ^ 2)),
@@ -124,51 +124,74 @@
     lax.fori_loop(0, table_ref.shape[1] // 256, step, 0)
 
 
-def near_kernel(meta_ref, dest_ref, *refs):
-    items = refs[:8]
-    left_out, table_out, total_out, left_store, store, left, left_far, table, total, sems, left_sems, out_sems = refs[8:]
+def transfers(pairs, sems):
+    copies = [pltpu.make_async_copy(source, target, sems.at[n]) for n, (source, target) in enumerate(pairs)]
+    for copy in copies:
+        copy.start()
+    return copies
+
+
+def own_kernel(meta_ref, dest_ref, *refs):
+    items = refs[:4]
+    left_near_out, left_far_out, table_out, total_out = refs[4:8]
+    left_store, left, left_near, left_far, store, table, total, sems, out_sems = refs[8:]
     row_count = left_store.shape[1]
-    left_in = [
-        pltpu.make_async_copy(items[n], left_store.at[dest_ref[8 + n]], left_sems.at[n]) for n in range(4)
-    ]
-    for copy in left_in:
-        copy.start()
-    copies = collected(items, store, sems, lambda n: dest_ref[n])
-    start_all(copies)
-    zero_invalid(store, lambda p: dest_ref[16 + p])
-    for copy in left_in:
+    copies = transfers([(items[n], left_store.at[dest_ref[4 + n]]) for n in range(4)], sems)
+    zero_invalid(store, lambda p: dest_ref[8 + p])
+    for copy in copies:
         copy.wait()
+    for number in range(4):
+        @pl.when(dest_ref[number] >= 0)
+        def _():
+            store[dest_ref[number]] = left_store[dest_ref[4 + number]]
     for row in range(row_count):
         pad = jnp.zeros((64, 512), left.dtype)
         blocks = [pad] + [left_store[h, row] for h in range(4)] + [pad]
         dense = spread(blocks, 8 - row, WINDOWS * 8, meta_ref[row])
         rows = slice(row * 64, (row + 1) * 64)
-        left[rows, :512] = dense[:, 1024:1536]
+        left[rows, :] = dense[:, 1024:1536]
         left_far[rows, 512:1024] = dense[:, :512]
         left_far[rows, 1024:] = dense[:, 2048:]
 
         @pl.when(meta_ref[30] > 0)
         def _():
-            left[rows, 512:] = dense[:, 1536:2048]
+            left_near[rows, :] = dense[:, 1536:2048]
             left_far[rows, :512] = dense[:, 512:1024]
 
         @pl.when(meta_ref[30] < 0)
         def _():
-            left[rows, 512:] = dense[:, 512:1024]
+            left_near[rows, :] = dense[:, 512:1024]
             left_far[rows, :512] = dense[:, 1536:2048]
-    outs = [pltpu.make_async_copy(*pair, out_sems.at[n]) for n, pair in enumerate(
-        ((left_far, left_out), (table, table_out), (total, total_out)))]
-    outs[0].start()
-    wait_all(copies)
-    windows(store, table, 2, lambda at: dest_ref[22 + at])
-    outs[1].start()
+    outs = transfers([(left_near, left_near_out), (left_far, left_far_out)], out_sems)
+    windows(store, table, 1, lambda at: dest_ref[11 + at])
+    outs += transfers([(table, table_out)], out_sems.at[pl.ds(2, 1)])
     product(left, table, total)
-    outs[2].start()
+    outs += transfers([(total, total_out)], out_sems.at[pl.ds(3, 1)])
     for copy in outs:
         copy.wait()
 
 
-def far_kernel(meta_ref, dest_ref, left_ref, before_ref, *refs):
+def near_kernel(meta_ref, dest_ref, left_in, before_in, *refs):
+    items = refs[:4]
+    table_out, base_out, store, left, before, table, total, base, sems, in_sems, out_sems = refs[4:]
+    copies = collected(items, store, sems, lambda n: dest_ref[n])
+    start_all(copies)
+    ins = transfers([(left_in, left), (before_in, before)], in_sems)
+    zero_invalid(store, lambda p: dest_ref[4 + p])
+    wait_all(copies)
+    windows(store, table, 1, lambda at: dest_ref[7 + at])
+    outs = transfers([(table, table_out)], out_sems)
+    for copy in ins:
+        copy.wait()
+    product(left, table, total, before)
+    for row in range(base.shape[0]):
+        base[row] = kept(total[row * 64:(row + 1) * 64, :], row, meta_ref[8 + row], 512)
+    outs += transfers([(base, base_out)], out_sems.at[pl.ds(1, 1)])
+    for copy in outs:
+        copy.wait()
+
+
+def far_kernel(meta_ref, dest_ref, left_ref, base_ref, *refs):
     items = refs[:9]
     table_ref, square_ref, low_ref, store, total_ref = refs[9:]
     row_count = items[0].shape[0]
@@ -181,19 +204,19 @@
 
     def step(tile, carry):
         cols = pl.ds(pl.multiple_of(tile * 256, 256), 256)
-        total_ref[:, cols] = before_ref[:, cols] + jnp.dot(
+        total_ref[:, cols] = jnp.dot(
             left_ref[...], table_ref[:, cols], preferred_element_type=jnp.float32
         )
         return carry
 
     lax.fori_loop(0, 4, step, 0)
     for row in range(row_count):
-        picked = kept(total_ref[row * 64:(row + 1) * 64, :], row, meta_ref[8 + row], 512)
+        picked = base_ref[row] + kept(total_ref[row * 64:(row + 1) * 64, :], row, meta_ref[8 + row], 512)
         square_ref[row] = picked
         low_ref[row] = picked.astype(low_ref.dtype)
 
 
-def cube_kernel(meta_ref, own_ref, core_ref, x_ref, far_ref, table_a, table_b, square_ref, out_ref,
+def cube_kernel(meta_ref, own_ref, core_ref, x_ref, far_ref, table_own, table_near, table_b, square_ref, out_ref,
                 store, left_ref, total_ref):
     row_count = out_ref.shape[0]
     group = meta_ref[29]
@@ -205,7 +228,8 @@
     def step(tile, carry):
         cols = pl.ds(pl.multiple_of(tile * 256, 256), 256)
         total_ref[:, cols] = (
-            jnp.dot(left_ref[:, :1024], table_a[:, cols], preferred_element_type=jnp.float32)
+            jnp.dot(left_ref[:, :512], table_own[:, cols], preferred_element_type=jnp.float32)
+            + jnp.dot(left_ref[:, 512:1024], table_near[:, cols], preferred_element_type=jnp.float32)
             + jnp.dot(left_ref[:, 1024:], table_b[:, cols], preferred_element_type=jnp.float32)
         )
         return carry
@@ -256,13 +280,14 @@
     own_core = permuted(own, route["core"])
     ox_core = permuted(ox, route["core"])
     oy_core = permuted(oy, route["core_oy"])
+    from_near, dd = lax.optimization_barrier((from_near, dd))
     dd_core = permuted(dd, route["core_dd"])
     bx = permuted(za, route["x"])
-    by = permuted(jnp.where(same, za, zb), route["y"])
-    z_core = permuted(jnp.where((group == 0) | (group == 3), za, zb), route["core"])
-    from_near, from_far, from_before, from_after, bx = lax.optimization_barrier(
-        (from_near, from_far, from_before, from_after, bx)
-    )
+    by_source = jnp.where(same, za, zb)
+    z_source = jnp.where((group == 0) | (group == 3), za, zb)
+    by = permuted(by_source, route["y"])
+    z_core = permuted(z_source, route["core"])
+    from_far, from_before, from_after, bx = lax.optimization_barrier((from_far, from_before, from_after, bx))
     bx_core = permuted(bx, route["core"])
     by_core = permuted(by, route["core_by"])
 
@@ -294,15 +319,20 @@
     ).astype(jnp.int32)
 
     yes = jnp.bool_(True)
-    near_items = (own, own_core, ox, ox_core, oy, oy_core, dd, dd_core)
-    near_dest = dest_of(
-        [(0, group ^ bits, yes) for bits in range(4)]
-        + [(near, group, yes), (near, group ^ 1, yes), (near, group ^ 2, other), (near, group ^ 3, other)],
-        lambda delta: 0 if isinstance(delta, int) else 1,
+    own_items = (own, own_core, ox, ox_core)
+    own_table = table_of(
+        dest_of([(0, group ^ bits, yes) for bits in range(4)], lambda delta: 0)
+        + [group ^ bits for bits in range(4)] + valid_of(0),
+        [threshold(0, 0)],
     )
+    near_items = (oy, oy_core, dd, dd_core)
     near_table = table_of(
-        near_dest + [group ^ bits for bits in range(4)] + [group * 0] * 4 + valid_of(0) + valid_of(near),
-        [threshold(0, 0), threshold(near, "near")],
+        dest_of(
+            [(near, group, yes), (near, group ^ 1, yes), (near, group ^ 2, other), (near, group ^ 3, other)],
+            lambda delta: 0,
+        )
+        + valid_of(near),
+        [threshold(near, "near")],
     )
     far_items = (za, zb, z_core, bx, bx_core, by, by_core, dd, dd_core)
     far_dest = dest_of(
@@ -337,25 +367,54 @@
     def cost(k):
         return pl.CostEstimate(flops=2 * rows * k * columns * 2, bytes_accessed=12 << 20, transcendentals=0)
 
-    left_far, table_a, total = pl.pallas_call(
-        near_kernel,
-        out_shape=(pltpu.HBM((rows, 1536), bf16), pltpu.HBM((1024, columns), bf16), pltpu.HBM((rows, columns), f32)),
-        in_specs=[smem, smem] + [hbm] * 8,
-        out_specs=(hbm,) * 3,
+    def in_hbm(*values):
+        return [pltpu.with_memory_space_constraint(value, pltpu.HBM) for value in values]
+
+    dma = pltpu.SemaphoreType.DMA
+    left_near, left_far, table_own, total = pl.pallas_call(
+        own_kernel,
+        out_shape=(
+            pltpu.HBM((rows, 512), bf16),
+            pltpu.HBM((rows, 1536), bf16),
+            pltpu.HBM((512, columns), bf16),
+            pltpu.HBM((rows, columns), f32),
+        ),
+        in_specs=[smem, smem] + [hbm] * 4,
+        out_specs=(hbm,) * 4,
         scratch_shapes=[
             pltpu.VMEM((ka_count,) + shards, bf16),
-            pltpu.VMEM((2 * PIECES,) + shards, bf16),
-            pltpu.VMEM((rows, 1024), bf16),
+            pltpu.VMEM((rows, 512), bf16),
+            pltpu.VMEM((rows, 512), bf16),
             pltpu.VMEM((rows, 1536), bf16),
-            pltpu.VMEM((1024, columns), bf16),
+            pltpu.VMEM((PIECES,) + shards, bf16),
+            pltpu.VMEM((512, columns), bf16),
             pltpu.VMEM((rows, columns), f32),
-            pltpu.SemaphoreType.DMA((8,)),
-            pltpu.SemaphoreType.DMA((4,)),
-            pltpu.SemaphoreType.DMA((3,)),
+            dma((4,)),
+            dma((4,)),
         ],
         compiler_params=small,
-        cost_estimate=cost(1024),
-    )(meta, near_table, *[pltpu.with_memory_space_constraint(v, pltpu.HBM) for v in near_items])
+        cost_estimate=cost(512),
+    )(meta, own_table, *in_hbm(*own_items))
+
+    table_near, base = pl.pallas_call(
+        near_kernel,
+        out_shape=(pltpu.HBM((512, columns), bf16), pltpu.HBM(shards, f32)),
+        in_specs=[smem, smem] + [hbm] * 6,
+        out_specs=(hbm, hbm),
+        scratch_shapes=[
+            pltpu.VMEM((PIECES,) + shards, bf16),
+            pltpu.VMEM((rows, 512), bf16),
+            pltpu.VMEM((rows, columns), f32),
+            pltpu.VMEM((512, columns), bf16),
+            pltpu.VMEM((rows, columns), f32),
+            pltpu.VMEM(shards, f32),
+            dma((4,)),
+            dma((2,)),
+            dma((2,)),
+        ],
+        compiler_params=small,
+        cost_estimate=cost(512),
+    )(meta, near_table, *in_hbm(left_near, total, *near_items))
 
     table_b, square, low = pl.pallas_call(
         far_kernel,
@@ -372,7 +431,7 @@
         ],
         compiler_params=small,
         cost_estimate=cost(1536),
-    )(meta, far_table, *[pltpu.with_memory_space_constraint(v, pltpu.HBM) for v in (left_far, total, za, zb)],
+    )(meta, far_table, *[pltpu.with_memory_space_constraint(v, pltpu.HBM) for v in (left_far, base, za, zb)],
       *far_items[2:7], *[pltpu.with_memory_space_constraint(v, pltpu.HBM) for v in (dd, dd_core)])
 
     low_x = permuted(low, route["x"])
@@ -381,7 +440,7 @@
     return pl.pallas_call(
         cube_kernel,
         out_shape=shape((row_count, block, width), bf16),
-        in_specs=[smem] + [vmem] * 7,
+        in_specs=[smem] + [vmem] * 8,
         out_specs=vmem,
         scratch_shapes=[
             pltpu.VMEM((ka_count, row_count, block, width), bf16),
@@ -389,7 +448,7 @@
             pltpu.VMEM((rows, columns), f32),
         ],
         compiler_params=small,
-    )(meta, low, low_core, low_x, low_far, table_a, table_b, square)
+    )(meta, low, low_core, low_x, low_far, table_own, table_near, table_b, square)
 
 
 def solution(mesh):

time: 97.6 us -> 107 us (1.096)
  starting transfers between devices: 24.2 us -> 30.4 us
  Pallas kernels: 20.8 us -> 24.3 us
    ppermute x17, starting transfers between devices: 15.9 us -> 22.4 us  [permuted(): return lax.ppermute(value, ('dom', 'ka'), pairs)]
    ppermute x4, waiting for transfers between devices: 6.97 us -> 1.62 us  [along(): lax.ppermute(value, 'dom', [(source(d) % dom_count, d) for d in range(dom...]
    ppermute x17, waiting for transfers between devices: 41.9 us -> 46.5 us  [permuted(): return lax.ppermute(value, ('dom', 'ka'), pairs)]
    pallas_call x1 -> x2, Pallas kernels: 7.7 us -> 11.5 us  [the longest x1 6.36 us: per_device(): pl.pallas_call(own_kernel, out_shape=(pltpu.HBM((rows, 512), bf16), pltpu...]
  transfers between devices with their start and end apart: 21 -> 21, of which waited for: 7 -> 7; matrix products, arithmetic and copies ran while one was open for 3% -> 3% of each run, Pallas kernels for 8% -> 11%
where the time goes in v1:
time: 107 us; the launch traced here: 106 us
  waiting for transfers between devices  48.2 us (45%)
  starting transfers between devices  30.4 us (28%)
  Pallas kernels  24.3 us (23%)
  other arithmetic  2.49 us (2%)
    ppermute x17, waiting for transfers between devices, permuted(): return lax.ppermute(value, ('dom', 'ka'), pairs)  46.5 us
    ppermute x17, starting transfers between devices, permuted(): return lax.ppermute(value, ('dom', 'ka'), pairs)  22.4 us
    ppermute x4, starting transfers between devices, along(): lax.ppermute(value, 'dom', [(source(d) % dom_count, d) for d in range(dom...  8.01 us
    pallas_call x1, Pallas kernels, per_device(): pl.pallas_call(far_kernel, out_shape=(shape((1536, columns), bf16), shape...  6.63 us
    pallas_call x1, Pallas kernels, per_device(): pl.pallas_call(own_kernel, out_shape=(pltpu.HBM((rows, 512), bf16), pltpu...  6.36 us
    pallas_call x1, Pallas kernels, per_device(): pl.pallas_call(cube_kernel, out_shape=shape((row_count, block, width), bf...  6.17 us
    pallas_call x1, Pallas kernels, per_device(): pl.pallas_call(near_kernel, out_shape=(pltpu.HBM((512, columns), bf16), p...  5.15 us
  transfers between devices with their start and end apart: 21, of which 7 were waited for; matrix products, arithmetic and copies ran while one was open for 3% of the time, Pallas kernels for 11%

profile of v1, /device:TPU:0, one launch (start us, length us, event | category | flops | bytes accessed | tf_op | source)
XLA Modules:
  0.0 106.4 jit_solution(12469574394060848245)
XLA Ops:
  0.0 7.0 %collective-permute-start.9 = (bf16[8,64,512]{2,1,0:T(8,128)(2,1)}, bf16[8,64,512]{2,1,0:T(8,128)(2,1)S(1)}, u32[]{:S(2)}, u32[]{:S(2)}) collective-permute-start(bf16[8,64,512]{2,1,0:T(8,128)(2,1)} %refs_0_.1), channel_id=1, source_target_pairs={{0,30},{1,31},{2,4},{3,5},{4,2},{5,3},{6,8},{7,9},{8,6},{9,7},{10,... | collective-permute-start | bytes 1572872 | tf_op jit(solution)/shard_map/ppermute | solution.py:14
  7.0 1.1 %collective-permute-start.3 = (bf16[8,64,512]{2,1,0:T(8,128)(2,1)}, bf16[8,64,512]{2,1,0:T(8,128)(2,1)S(1)}, u32[]{:S(2)}, u32[]{:S(2)}) collective-permute-start(bf16[8,64,512]{2,1,0:T(8,128)(2,1)} %refs_0_.1), channel_id=1, source_target_pairs={{0,24},{1,25},{2,10},{3,11},{4,28},{5,29},{6,14},{7,15},{8,0},{9,1... | collective-permute-start | bytes 1572872 | tf_op jit(solution)/shard_map/ppermute | solution.py:14
  8.1 0.7 collective-permute-start.13
  8.8 1.3 %collective-permute-start.8 = (s32[8,32]{1,0:T(8,128)}, s32[8,32]{1,0:T(8,128)S(1)}, u32[]{:S(2)}, u32[]{:S(2)}) collective-permute-start(s32[8,32]{1,0:T(8,128)} %param.4), channel_id=1, source_target_pairs={{4,0},{0,4},{12,8},{8,12},{20,16},{16,20},{28,24},{24,28},{5,1},{1... | collective-permute-start | bytes 3080 | tf_op jit(solution)/shard_map/ppermute | solution.py:268
  10.1 0.9 convert_reduce_fusion.4
  11.7 1.6 %collective-permute-done.8 = s32[8,32]{1,0:T(8,128)S(1)} collective-permute-done((s32[8,32]{1,0:T(8,128)}, s32[8,32]{1,0:T(8,128)S(1)}, u32[]{:S(2)}, u32[]{:S(2)}) %collective-permute-start.8) | collective-permute-done | bytes 1056 | tf_op jit(solution)/shard_map/ppermute | solution.py:268
  13.3 0.6 collective-permute-start.1
  13.9 6.1 %collective-permute-done.9.refs_2_.refs_7_ = bf16[8,64,512]{2,1,0:T(8,128)(2,1)S(1)} collective-permute-done((bf16[8,64,512]{2,1,0:T(8,128)(2,1)}, bf16[8,64,512]{2,1,0:T(8,128)(2,1)S(1)}, u32[]{:S(2)}, u32[]{:S(2)}) %collective-permute-start.9) | collective-permute-done | bytes 524320 | tf_op jit(solution)/shard_map/ppermute | solution.py:14
  20.1 1.9 %collective-permute-start = (s32[8,32]{1,0:T(8,128)}, s32[8,32]{1,0:T(8,128)S(1)}, u32[]{:S(2)}, u32[]{:S(2)}) collective-permute-start(s32[8,32]{1,0:T(8,128)} %param.4), channel_id=1, source_target_pairs={{28,0},{8,4},{4,8},{16,12},{12,16},{24,20},{20,24},{0,28},{29,1},{... | collective-permute-start | bytes 3080 | tf_op jit(solution)/shard_map/ppermute | solution.py:268
  22.0 8.9 %collective-permute-done.3.refs_0_ = bf16[8,64,512]{2,1,0:T(8,128)(2,1)S(1)} collective-permute-done((bf16[8,64,512]{2,1,0:T(8,128)(2,1)}, bf16[8,64,512]{2,1,0:T(8,128)(2,1)S(1)}, u32[]{:S(2)}, u32[]{:S(2)}) %collective-permute-start.3) | collective-permute-done | bytes 524320 | tf_op jit(solution)/shard_map/ppermute | solution.py:14
  30.9 4.2 %collective-permute-start.2 = (s32[8,32]{1,0:T(8,128)}, s32[8,32]{1,0:T(8,128)S(1)}, u32[]{:S(2)}, u32[]{:S(2)}) collective-permute-start(s32[8,32]{1,0:T(8,128)} %param.4), channel_id=1, source_target_pairs={{8,0},{12,4},{16,8},{20,12},{24,16},{28,20},{0,24},{4,28},{9,1},{1... | collective-permute-start | bytes 3080 | tf_op jit(solution)/shard_map/ppermute | solution.py:268
  35.1 0.5 collective-permute-start.4
  35.5 0.9 broadcast_select_fusion
  36.5 0.2 convert_reduce_fusion
  36.6 0.8 collective-permute-start.5
  37.5 2.7 %collective-permute-start.10 = (bf16[8,64,512]{2,1,0:T(8,128)(2,1)}, bf16[8,64,512]{2,1,0:T(8,128)(2,1)}, u32[]{:S(2)}, u32[]{:S(2)}) collective-permute-start(bf16[8,64,512]{2,1,0:T(8,128)(2,1)} %refs_0_.1), channel_id=1, source_target_pairs={{0,4},{1,5},{2,6},{3,7},{4,0},{5,1},{6,2},{7,3},{8,12},{9,13},{10,... | collective-permute-start | bytes 1572872 | tf_op jit(solution)/shard_map/ppermute | solution.py:14
  40.5 9.2 %collective-permute-done.4.refs_3_ = bf16[8,64,512]{2,1,0:T(8,128)(2,1)S(1)} collective-permute-done((bf16[8,64,512]{2,1,0:T(8,128)(2,1)S(1)}, bf16[8,64,512]{2,1,0:T(8,128)(2,1)S(1)}, u32[]{:S(2)}, u32[]{:S(2)}) %collective-permute-start.4) | collective-permute-done | bytes 524320 | tf_op jit(solution)/shard_map/ppermute | solution.py:14
  49.7 3.1 %collective-permute-start.12 = (bf16[8,64,512]{2,1,0:T(8,128)(2,1)S(1)}, bf16[8,64,512]{2,1,0:T(8,128)(2,1)}, u32[]{:S(2)}, u32[]{:S(2)}) collective-permute-start(bf16[8,64,512]{2,1,0:T(8,128)(2,1)S(1)} %collective-permute-done.9.refs_2_.refs_7_), channel_id=1, source_target_pairs={{0,1},{3,2},{4,5},{7,6},{8,9},{11,10},{12,13},{15,14},{16,17},{19,... | collective-permute-start | bytes 1572872 | tf_op jit(solution)/shard_map/ppermute | solution.py:14
  52.8 0.2 convert_reduce_fusion.3
  53.0 0.2 convert_reduce_fusion.1
  53.3 3.2 %collective-permute-start.11 = (bf16[8,64,512]{2,1,0:T(8,128)(2,1)}, bf16[8,64,512]{2,1,0:T(8,128)(2,1)}, u32[]{:S(2)}, u32[]{:S(2)}) collective-permute-start(bf16[8,64,512]{2,1,0:T(8,128)(2,1)} %collective-permute-done.10.refs_0_), channel_id=1, source_target_pairs={{0,1},{2,3},{5,4},{7,6},{8,9},{10,11},{13,12},{15,14},{16,17},{18,... | collective-permute-start | bytes 1572872 | tf_op jit(solution)/shard_map/ppermute | solution.py:14
  56.5 7.6 %collective-permute-done.16.refs_5_ = bf16[8,64,512]{2,1,0:T(8,128)(2,1)S(1)} collective-permute-done((bf16[8,64,512]{2,1,0:T(8,128)(2,1)S(1)}, bf16[8,64,512]{2,1,0:T(8,128)(2,1)S(1)}, u32[]{:S(2)}, u32[]{:S(2)}) %collective-permute-start.16) | collective-permute-done | bytes 524320 | tf_op jit(solution)/shard_map/ppermute | solution.py:14
  64.2 1.3 %collective-permute-start.17 = (bf16[8,64,512]{2,1,0:T(8,128)(2,1)S(1)}, bf16[8,64,512]{2,1,0:T(8,128)(2,1)S(1)}, u32[]{:S(2)}, u32[]{:S(2)}) collective-permute-start(bf16[8,64,512]{2,1,0:T(8,128)(2,1)S(1)} %collective-permute-done.16.refs_5_), channel_id=1, source_target_pairs={{1,0},{3,2},{4,5},{6,7},{9,8},{11,10},{12,13},{14,15},{17,16},{19,... | collective-permute-start | bytes 1572872 | tf_op jit(solution)/shard_map/ppermute | solution.py:14
  65.6 6.4 %shard_map.37 = (bf16[512,512]{1,0:T(8,128)(2,1)}, bf16[512,1536]{1,0:T(8,128)(2,1)}, bf16[512,1024]{1,0:T(8,128)(2,1)}, f32[512,1024]{1,0:T(8,128)}) custom-call(s32[31]{0:T(128)S(1)} %concatenate.12.meta_ref, s32[19]{0:T(128)S(1)} %concatenate.14.dest_ref, bf16[8,64,512]{2,1,0:T(8,128)(2,1)} %refs_0_.1, ...), custom_call_target="tpu_custom_call" | custom-call | flops 1073741824 | bytes 12582912 | tf_op jit(solution)/shard_map/pallas_call | solution.py:374
  72.0 5.1 %shard_map.38 = (bf16[512,1024]{1,0:T(8,128)(2,1)}, f32[8,64,512]{2,1,0:T(8,128)}) custom-call(s32[31]{0:T(128)S(1)} %concatenate.12.meta_ref, s32[15]{0:T(128)S(1)} %concatenate.15.dest_ref, bf16[512,512]{1,0:T(8,128)(2,1)} %get-tuple-element.25.left_in, f32[512,1024]{1,0:T(8,128)} %get-tuple-element.26.before_in, ...), custom_call_target="tpu_custom_call" | custom-call | flops 1073741824 | bytes 12582912 | tf_op jit(solution)/shard_map/pallas_call | solution.py:399
  77.2 6.6 %shard_map.39 = (bf16[1536,1024]{1,0:T(8,128)(2,1)S(1)}, f32[8,64,512]{2,1,0:T(8,128)S(1)}, bf16[8,64,512]{2,1,0:T(8,128)(2,1)S(1)}) custom-call(s32[31]{0:T(128)S(1)} %concatenate.12.meta_ref, s32[42]{0:T(128)S(1)} %concatenate.13.dest_ref, bf16[512,1536]{1,0:T(8,128)(2,1)} %get-tuple-element.23.left_ref, f32[8,64,512]{2,1,0:T(8,128)} %get-tuple-element.28.base_ref, ...), custom_call_target="tpu_custom_call" | custom-call | flops 3221225472 | bytes 12582912 | tf_op jit(solution)/shard_map/pallas_call | solution.py:419
  83.8 1.0 collective-permute-start.19
  84.8 0.5 collective-permute-start.18
  85.4 12.9 %collective-permute-done.19.x_ref = bf16[8,64,512]{2,1,0:T(8,128)(2,1)S(1)} collective-permute-done((bf16[8,64,512]{2,1,0:T(8,128)(2,1)S(1)}, bf16[8,64,512]{2,1,0:T(8,128)(2,1)S(1)}, u32[]{:S(2)}, u32[]{:S(2)}) %collective-permute-start.19) | collective-permute-done | bytes 524320 | tf_op jit(solution)/shard_map/ppermute | solution.py:14
  98.3 0.2 collective-permute-start.20
  98.5 1.7 %collective-permute-done.20.far_ref = bf16[8,64,512]{2,1,0:T(8,128)(2,1)S(1)} collective-permute-done((bf16[8,64,512]{2,1,0:T(8,128)(2,1)S(1)}, bf16[8,64,512]{2,1,0:T(8,128)(2,1)S(1)}, u32[]{:S(2)}, u32[]{:S(2)}) %collective-permute-start.20) | collective-permute-done | bytes 524320 | tf_op jit(solution)/shard_map/ppermute | solution.py:14
  100.2 6.2 %shard_map.40 = bf16[8,64,512]{2,1,0:T(8,128)(2,1)} custom-call(s32[31]{0:T(128)S(1)} %concatenate.12.meta_ref, bf16[8,64,512]{2,1,0:T(8,128)(2,1)S(1)} %get-tuple-element.30.own_ref, bf16[8,64,512]{2,1,0:T(8,128)(2,1)S(1)} %collective-permute-done.18.core_ref, bf16[8,64,512]{2,1,0:T(8,128)(2,1)S(1)} %collective-permute-done.19.x_ref, ...), custom_call_target="tpu_custom_call" | custom-call | tf_op jit(solution)/shard_map/pallas_call | solution.py:440
  (43 shorter events, 0.8 us)
Async XLA Ops:
  0.0 20.1 %collective-permute-start.9 = (bf16[8,64,512]{2,1,0:T(8,128)(2,1)}, bf16[8,64,512]{2,1,0:T(8,128)(2,1)S(1)}, u32[]{:S(2)}, u32[]{:S(2)}) collective-permute-start(bf16[8,64,512]{2,1,0:T(8,128)(2,1)} %refs_0_.1), channel_id=1, source_target_pairs={{0,30},{1,31},{2,4},{3,5},{4,2},{5,3},{6,8},{7,9},{8,6},{9,7},{10,... | collective-permute-start | bytes 1572872 | tf_op jit(solution)/shard_map/ppermute | solution.py:14
  7.0 33.3 %collective-permute-start.6 = (bf16[8,64,512]{2,1,0:T(8,128)(2,1)}, bf16[8,64,512]{2,1,0:T(8,128)(2,1)}, u32[]{:S(2)}, u32[]{:S(2)}) collective-permute-start(bf16[8,64,512]{2,1,0:T(8,128)(2,1)} %refs_0_.1), channel_id=1, source_target_pairs={{0,2},{1,3},{2,0},{3,1},{4,6},{5,7},{6,4},{7,5},{8,10},{9,11},{10,... | collective-permute-start | bytes 1572872 | tf_op jit(solution)/shard_map/ppermute | solution.py:14
  7.0 23.9 %collective-permute-start.3 = (bf16[8,64,512]{2,1,0:T(8,128)(2,1)}, bf16[8,64,512]{2,1,0:T(8,128)(2,1)S(1)}, u32[]{:S(2)}, u32[]{:S(2)}) collective-permute-start(bf16[8,64,512]{2,1,0:T(8,128)(2,1)} %refs_0_.1), channel_id=1, source_target_pairs={{0,24},{1,25},{2,10},{3,11},{4,28},{5,29},{6,14},{7,15},{8,0},{9,1... | collective-permute-start | bytes 1572872 | tf_op jit(solution)/shard_map/ppermute | solution.py:14
  8.1 27.0 %collective-permute-start.13 = (bf16[8,64,512]{2,1,0:T(8,128)(2,1)}, bf16[8,64,512]{2,1,0:T(8,128)(2,1)S(1)}, u32[]{:S(2)}, u32[]{:S(2)}) collective-permute-start(bf16[8,64,512]{2,1,0:T(8,128)(2,1)} %refs_0_.1), channel_id=1, source_target_pairs={{1,9},{2,26},{3,27},{4,12},{5,13},{6,30},{9,17},{10,2},{11,3},{12,... | collective-permute-start | bytes 1572872 | tf_op jit(solution)/shard_map/ppermute | solution.py:14
  8.8 4.6 %collective-permute-start.8 = (s32[8,32]{1,0:T(8,128)}, s32[8,32]{1,0:T(8,128)S(1)}, u32[]{:S(2)}, u32[]{:S(2)}) collective-permute-start(s32[8,32]{1,0:T(8,128)} %param.4), channel_id=1, source_target_pairs={{4,0},{0,4},{12,8},{8,12},{20,16},{16,20},{28,24},{24,28},{5,1},{1... | collective-permute-start | bytes 3080 | tf_op jit(solution)/shard_map/ppermute | solution.py:268
  13.3 23.3 %collective-permute-start.1 = (s32[8,32]{1,0:T(8,128)}, s32[8,32]{1,0:T(8,128)S(1)}, u32[]{:S(2)}, u32[]{:S(2)}) collective-permute-start(s32[8,32]{1,0:T(8,128)} %param.4), channel_id=1, source_target_pairs={{24,0},{28,4},{0,8},{4,12},{8,16},{12,20},{16,24},{20,28},{25,1},{... | collective-permute-start | bytes 3080 | tf_op jit(solution)/shard_map/ppermute | solution.py:268
  20.1 51.9 %copy-start.2 = (bf16[8,64,512]{2,1,0:T(8,128)(2,1)}, bf16[8,64,512]{2,1,0:T(8,128)(2,1)S(1)}, u32[]{:S(2)}) copy-start(bf16[8,64,512]{2,1,0:T(8,128)(2,1)S(1)} %collective-permute-done.9.refs_2_.refs_7_) | copy-start | bytes 1572868
  20.1 17.4 %collective-permute-start = (s32[8,32]{1,0:T(8,128)}, s32[8,32]{1,0:T(8,128)S(1)}, u32[]{:S(2)}, u32[]{:S(2)}) collective-permute-start(s32[8,32]{1,0:T(8,128)} %param.4), channel_id=1, source_target_pairs={{28,0},{8,4},{4,8},{16,12},{12,16},{24,20},{20,24},{0,28},{29,1},{... | collective-permute-start | bytes 3080 | tf_op jit(solution)/shard_map/ppermute | solution.py:268
  30.9 22.3 %copy-start.3 = (bf16[8,64,512]{2,1,0:T(8,128)(2,1)}, bf16[8,64,512]{2,1,0:T(8,128)(2,1)S(1)}, u32[]{:S(2)}) copy-start(bf16[8,64,512]{2,1,0:T(8,128)(2,1)S(1)} %collective-permute-done.3.refs_0_) | copy-start | bytes 1572868
  30.9 9.3 %collective-permute-start.2 = (s32[8,32]{1,0:T(8,128)}, s32[8,32]{1,0:T(8,128)S(1)}, u32[]{:S(2)}, u32[]{:S(2)}) collective-permute-start(s32[8,32]{1,0:T(8,128)} %param.4), channel_id=1, source_target_pairs={{8,0},{12,4},{16,8},{20,12},{24,16},{28,20},{0,24},{4,28},{9,1},{1... | collective-permute-start | bytes 3080 | tf_op jit(solution)/shard_map/ppermute | solution.py:268
  35.1 5.1 %copy-start.4 = (bf16[8,64,512]{2,1,0:T(8,128)(2,1)}, bf16[8,64,512]{2,1,0:T(8,128)(2,1)S(1)}, u32[]{:S(2)}) copy-start(bf16[8,64,512]{2,1,0:T(8,128)(2,1)S(1)} %collective-permute-done.13.refs_1_) | copy-start | bytes 1572868
  35.1 14.6 %collective-permute-start.4 = (bf16[8,64,512]{2,1,0:T(8,128)(2,1)S(1)}, bf16[8,64,512]{2,1,0:T(8,128)(2,1)S(1)}, u32[]{:S(2)}, u32[]{:S(2)}) collective-permute-start(bf16[8,64,512]{2,1,0:T(8,128)(2,1)S(1)} %collective-permute-done.3.refs_0_), channel_id=1, source_target_pairs={{0,2},{1,3},{2,0},{3,1},{4,6},{5,7},{6,4},{7,5},{8,10},{9,11},{10,... | collective-permute-start | bytes 1572872 | tf_op jit(solution)/shard_map/ppermute | solution.py:14
  36.6 16.6 %collective-permute-start.5 = (bf16[8,64,512]{2,1,0:T(8,128)(2,1)}, bf16[8,64,512]{2,1,0:T(8,128)(2,1)}, u32[]{:S(2)}, u32[]{:S(2)}) collective-permute-start(bf16[8,64,512]{2,1,0:T(8,128)(2,1)} %refs_0_.1), channel_id=1, source_target_pairs={{0,1},{1,0},{2,3},{3,2},{4,5},{5,4},{6,7},{7,6},{8,9},{9,8},{10,11... | collective-permute-start | bytes 1572872 | tf_op jit(solution)/shard_map/ppermute | solution.py:14
  37.5 15.9 %collective-permute-start.10 = (bf16[8,64,512]{2,1,0:T(8,128)(2,1)}, bf16[8,64,512]{2,1,0:T(8,128)(2,1)}, u32[]{:S(2)}, u32[]{:S(2)}) collective-permute-start(bf16[8,64,512]{2,1,0:T(8,128)(2,1)} %refs_0_.1), channel_id=1, source_target_pairs={{0,4},{1,5},{2,6},{3,7},{4,0},{5,1},{6,2},{7,3},{8,12},{9,13},{10,... | collective-permute-start | bytes 1572872 | tf_op jit(solution)/shard_map/ppermute | solution.py:14
  40.2 23.9 %collective-permute-start.16 = (bf16[8,64,512]{2,1,0:T(8,128)(2,1)S(1)}, bf16[8,64,512]{2,1,0:T(8,128)(2,1)S(1)}, u32[]{:S(2)}, u32[]{:S(2)}) collective-permute-start(bf16[8,64,512]{2,1,0:T(8,128)(2,1)S(1)} %get-tuple-element.37), channel_id=1, source_target_pairs={{0,4},{1,5},{2,6},{3,7},{4,0},{5,1},{6,2},{7,3},{8,12},{9,13},{10,... | collective-permute-start | bytes 1572872 | tf_op jit(solution)/shard_map/ppermute | solution.py:14
  40.3 16.2 %collective-permute-start.7 = (bf16[8,64,512]{2,1,0:T(8,128)(2,1)}, bf16[8,64,512]{2,1,0:T(8,128)(2,1)}, u32[]{:S(2)}, u32[]{:S(2)}) collective-permute-start(bf16[8,64,512]{2,1,0:T(8,128)(2,1)} %collective-permute-done.6.refs_2_), channel_id=1, source_target_pairs={{0,1},{1,0},{2,3},{3,2},{4,5},{5,4},{6,7},{7,6},{8,9},{9,8},{10,11... | collective-permute-start | bytes 1572872 | tf_op jit(solution)/shard_map/ppermute | solution.py:14
  49.7 22.3 %collective-permute-start.12 = (bf16[8,64,512]{2,1,0:T(8,128)(2,1)S(1)}, bf16[8,64,512]{2,1,0:T(8,128)(2,1)}, u32[]{:S(2)}, u32[]{:S(2)}) collective-permute-start(bf16[8,64,512]{2,1,0:T(8,128)(2,1)S(1)} %collective-permute-done.9.refs_2_.refs_7_), channel_id=1, source_target_pairs={{0,1},{3,2},{4,5},{7,6},{8,9},{11,10},{12,13},{15,14},{16,17},{19,... | collective-permute-start | bytes 1572872 | tf_op jit(solution)/shard_map/ppermute | solution.py:14
  53.2 23.9 %collective-permute-start.14 = (bf16[8,64,512]{2,1,0:T(8,128)(2,1)}, bf16[8,64,512]{2,1,0:T(8,128)(2,1)S(1)}, u32[]{:S(2)}, u32[]{:S(2)}) collective-permute-start(bf16[8,64,512]{2,1,0:T(8,128)(2,1)} %get-tuple-element.38), channel_id=1, source_target_pairs={{0,1},{1,0},{2,3},{3,2},{4,5},{5,4},{6,7},{7,6},{8,9},{9,8},{10,11... | collective-permute-start | bytes 1572872 | tf_op jit(solution)/shard_map/ppermute | solution.py:14
  53.3 18.6 %collective-permute-start.11 = (bf16[8,64,512]{2,1,0:T(8,128)(2,1)}, bf16[8,64,512]{2,1,0:T(8,128)(2,1)}, u32[]{:S(2)}, u32[]{:S(2)}) collective-permute-start(bf16[8,64,512]{2,1,0:T(8,128)(2,1)} %collective-permute-done.10.refs_0_), channel_id=1, source_target_pairs={{0,1},{2,3},{5,4},{7,6},{8,9},{10,11},{13,12},{15,14},{16,17},{18,... | collective-permute-start | bytes 1572872 | tf_op jit(solution)/shard_map/ppermute | solution.py:14
  56.5 20.6 %collective-permute-start.15 = (bf16[8,64,512]{2,1,0:T(8,128)(2,1)S(1)}, bf16[8,64,512]{2,1,0:T(8,128)(2,1)S(1)}, u32[]{:S(2)}, u32[]{:S(2)}) collective-permute-start(bf16[8,64,512]{2,1,0:T(8,128)(2,1)S(1)} %collective-permute-done.4.refs_3_), channel_id=1, source_target_pairs={{0,1},{1,0},{2,3},{3,2},{4,5},{5,4},{6,7},{7,6},{8,9},{9,8},{10,11... | collective-permute-start | bytes 1572872 | tf_op jit(solution)/shard_map/ppermute | solution.py:14
  64.2 13.0 %collective-permute-start.17 = (bf16[8,64,512]{2,1,0:T(8,128)(2,1)S(1)}, bf16[8,64,512]{2,1,0:T(8,128)(2,1)S(1)}, u32[]{:S(2)}, u32[]{:S(2)}) collective-permute-start(bf16[8,64,512]{2,1,0:T(8,128)(2,1)S(1)} %collective-permute-done.16.refs_5_), channel_id=1, source_target_pairs={{1,0},{3,2},{4,5},{6,7},{9,8},{11,10},{12,13},{14,15},{17,16},{19,... | collective-permute-start | bytes 1572872 | tf_op jit(solution)/shard_map/ppermute | solution.py:14
  77.2 23.1 %copy-start = (bf16[512,1024]{1,0:T(8,128)(2,1)S(1)}, bf16[512,1024]{1,0:T(8,128)(2,1)}, u32[]{:S(2)}) copy-start(bf16[512,1024]{1,0:T(8,128)(2,1)} %get-tuple-element.31.table_own) | copy-start | bytes 3145732
  77.2 23.1 %copy-start.1 = (bf16[512,1024]{1,0:T(8,128)(2,1)S(1)}, bf16[512,1024]{1,0:T(8,128)(2,1)}, u32[]{:S(2)}) copy-start(bf16[512,1024]{1,0:T(8,128)(2,1)} %get-tuple-element.32.table_near) | copy-start | bytes 3145732
  83.8 14.5 %collective-permute-start.19 = (bf16[8,64,512]{2,1,0:T(8,128)(2,1)S(1)}, bf16[8,64,512]{2,1,0:T(8,128)(2,1)S(1)}, u32[]{:S(2)}, u32[]{:S(2)}) collective-permute-start(bf16[8,64,512]{2,1,0:T(8,128)(2,1)S(1)} %get-tuple-element.30.own_ref), channel_id=1, source_target_pairs={{0,2},{1,3},{2,0},{3,1},{4,6},{5,7},{6,4},{7,5},{8,10},{9,11},{10,... | collective-permute-start | bytes 1572872 | tf_op jit(solution)/shard_map/ppermute | solution.py:14
  84.8 13.7 %collective-permute-start.18 = (bf16[8,64,512]{2,1,0:T(8,128)(2,1)S(1)}, bf16[8,64,512]{2,1,0:T(8,128)(2,1)S(1)}, u32[]{:S(2)}, u32[]{:S(2)}) collective-permute-start(bf16[8,64,512]{2,1,0:T(8,128)(2,1)S(1)} %get-tuple-element.30.own_ref), channel_id=1, source_target_pairs={{0,1},{1,0},{2,3},{3,2},{4,5},{5,4},{6,7},{7,6},{8,9},{9,8},{10,11... | collective-permute-start | bytes 1572872 | tf_op jit(solution)/shard_map/ppermute | solution.py:14
  98.3 1.9 %collective-permute-start.20 = (bf16[8,64,512]{2,1,0:T(8,128)(2,1)S(1)}, bf16[8,64,512]{2,1,0:T(8,128)(2,1)S(1)}, u32[]{:S(2)}, u32[]{:S(2)}) collective-permute-start(bf16[8,64,512]{2,1,0:T(8,128)(2,1)S(1)} %collective-permute-done.19.x_ref), channel_id=1, source_target_pairs={{0,1},{1,0},{2,3},{3,2},{4,5},{5,4},{6,7},{7,6},{8,9},{9,8},{10,11... | collective-permute-start | bytes 1572872 | tf_op jit(solution)/shard_map/ppermute | solution.py:14

commit v2 on v1

--- a/solution.py
+++ b/solution.py
@@ -1,3 +1,5 @@
+import functools
+
 import jax
 import jax.numpy as jnp
 from jax import lax
@@ -56,11 +58,11 @@
     return jnp.where(place < threshold * 64, low, high)
 
 
-def fill_left(left_ref, rows_of, threshold, order, row_count):
-    for row in range(row_count):
-        blocks = rows_of(row)
-        pad = jnp.zeros((64, 512), blocks[0].dtype)
-        dense = spread([pad] + blocks + [pad], 8 - row, WINDOWS * 8, threshold(row))
+def fill_left(left_ref, store, first_row, threshold, order):
+    for row in range(store.shape[1]):
+        pad = jnp.zeros((64, 512), store.dtype)
+        blocks = [pad] + [store[h, row] for h in range(store.shape[0])] + [pad]
+        dense = spread(blocks, 8 - first_row - row, WINDOWS * 8, threshold(first_row + row))
         for window in range(WINDOWS):
             at = pl.ds(pl.multiple_of(order(window) * 512, 512), 512)
             left_ref[row * 64:(row + 1) * 64, at] = dense[:, window * 512:(window + 1) * 512]
@@ -193,8 +195,9 @@
 
 def far_kernel(meta_ref, dest_ref, left_ref, base_ref, *refs):
     items = refs[:9]
-    table_ref, square_ref, low_ref, store, total_ref = refs[9:]
+    table_ref, square_ref, low_a, low_b, store, total_ref = refs[9:]
     row_count = items[0].shape[0]
+    half = row_count // 2
     collect(store, items, lambda n: dest_ref[n], lambda p: dest_ref[9 + p])
     for window in range(3):
         for row in range(row_count):
@@ -213,17 +216,18 @@
     for row in range(row_count):
         picked = base_ref[row] + kept(total_ref[row * 64:(row + 1) * 64, :], row, meta_ref[8 + row], 512)
         square_ref[row] = picked
-        low_ref[row] = picked.astype(low_ref.dtype)
-
-
-def cube_kernel(meta_ref, own_ref, core_ref, x_ref, far_ref, table_own, table_near, table_b, square_ref, out_ref,
-                store, left_ref, total_ref):
-    row_count = out_ref.shape[0]
+        low_ref = low_a if row < half else low_b
+        low_ref[row % half] = picked.astype(low_ref.dtype)
+
+
+def cube_kernel(part, meta_ref, own_ref, core_ref, x_ref, far_ref, table_own, table_near, table_b, square_ref, *refs):
+    out_ref, store, left_ref, total_ref, result, sem = refs[part:]
+    row_count = result.shape[0]
+    first_row = part * row_count
     group = meta_ref[29]
     for bits, ref in enumerate((own_ref, core_ref, x_ref, far_ref)):
         store[group ^ bits] = ref[...]
-    fill_left(left_ref, lambda row: [store[h, row] for h in range(4)],
-              lambda row: meta_ref[16 + row], lambda chunk: meta_ref[24 + chunk], row_count)
+    fill_left(left_ref, store, first_row, lambda row: meta_ref[16 + row], lambda window: meta_ref[24 + window])
 
     def step(tile, carry):
         cols = pl.ds(pl.multiple_of(tile * 256, 256), 256)
@@ -236,8 +240,12 @@
 
     lax.fori_loop(0, 4, step, 0)
     for row in range(row_count):
-        cube = kept(total_ref[row * 64:(row + 1) * 64, :], row, meta_ref[8 + row], 512)
-        out_ref[row] = (3.0 * square_ref[row] - 2.0 * cube).astype(out_ref.dtype)
+        whole = first_row + row
+        cube = kept(total_ref[row * 64:(row + 1) * 64, :], whole, meta_ref[8 + whole], 512)
+        result[row] = (3.0 * square_ref[whole] - 2.0 * cube).astype(result.dtype)
+    copy = pltpu.make_async_copy(result, out_ref.at[pl.ds(first_row, row_count)], sem)
+    copy.start()
+    copy.wait()
 
 
 def missing_places(index, rows, total_rows, reach):
@@ -416,15 +424,17 @@
         cost_estimate=cost(512),
     )(meta, near_table, *in_hbm(left_near, total, *near_items))
 
-    table_b, square, low = pl.pallas_call(
+    half_rows = row_count // 2
+    table_b, square, low_a, low_b = pl.pallas_call(
         far_kernel,
         out_shape=(
             shape((1536, columns), bf16),
             shape((row_count, block, width), f32),
-            shape((row_count, block, width), bf16),
+            shape((half_rows, block, width), bf16),
+            shape((half_rows, block, width), bf16),
         ),
         in_specs=[smem, smem] + [vmem] * 11,
-        out_specs=(vmem, vmem, vmem),
+        out_specs=(vmem, vmem, vmem, vmem),
         scratch_shapes=[
             pltpu.VMEM((3 * PIECES, row_count, block, width), bf16),
             pltpu.VMEM((rows, columns), f32),
@@ -434,21 +444,30 @@
     )(meta, far_table, *[pltpu.with_memory_space_constraint(v, pltpu.HBM) for v in (left_far, base, za, zb)],
       *far_items[2:7], *[pltpu.with_memory_space_constraint(v, pltpu.HBM) for v in (dd, dd_core)])
 
-    low_x = permuted(low, route["x"])
-    low_core = permuted(low, route["core"])
-    low_far = permuted(low_x, route["core"])
-    return pl.pallas_call(
-        cube_kernel,
-        out_shape=shape((row_count, block, width), bf16),
-        in_specs=[smem] + [vmem] * 8,
-        out_specs=vmem,
-        scratch_shapes=[
-            pltpu.VMEM((ka_count, row_count, block, width), bf16),
-            pltpu.VMEM((rows, depth), bf16),
-            pltpu.VMEM((rows, columns), f32),
-        ],
-        compiler_params=small,
-    )(meta, low, low_core, low_x, low_far, table_own, table_near, table_b, square)
+    lows = (low_a, low_b)
+    by_x = [permuted(low, route["x"]) for low in lows]
+    by_partner = [permuted(low, route["core"]) for low in lows]
+    by_both = [permuted(low, route["core"]) for low in by_x]
+    out = ()
+    for part in range(2):
+        out = (pl.pallas_call(
+            functools.partial(cube_kernel, part),
+            out_shape=pltpu.HBM((row_count, block, width), bf16),
+            in_specs=[smem] + [vmem] * 8 + [hbm] * part,
+            out_specs=hbm,
+            scratch_shapes=[
+                pltpu.VMEM((ka_count, half_rows, block, width), bf16),
+                pltpu.VMEM((rows // 2, depth), bf16),
+                pltpu.VMEM((rows // 2, columns), f32),
+                pltpu.VMEM((half_rows, block, width), bf16),
+                pltpu.SemaphoreType.DMA,
+            ],
+            input_output_aliases={9: 0} if part else {},
+            compiler_params=small,
+            cost_estimate=cost(1280),
+        )(meta, lows[part], by_partner[part], by_x[part], by_both[part],
+          table_own, table_near, table_b, square, *out),)
+    return out[0]
 
 
 def solution(mesh):

time: 107 us -> 107 us (level)
  waiting for transfers between devices: 48.2 us -> 44.2 us
  starting transfers between devices: 30.4 us -> 32.6 us
  Pallas kernels: 24.3 us -> 26.4 us
    ppermute x17 -> x20, waiting for transfers between devices: 46.5 us -> 42.6 us  [permuted(): return lax.ppermute(value, ('dom', 'ka'), pairs)]
    ppermute x17 -> x20, starting transfers between devices: 22.4 us -> 24.6 us  [permuted(): return lax.ppermute(value, ('dom', 'ka'), pairs)]
    pallas_call x1 -> x2, Pallas kernels: 6.17 us -> 8.24 us  [per_device(): pl.pallas_call(functools.partial(cube_kernel, part), out_shape=pltpu.HBM(...]
  transfers between devices with their start and end apart: 21 -> 24, of which waited for: 7 -> 7; matrix products, arithmetic and copies ran while one was open for 3% -> 3% of each run, Pallas kernels for 11% -> 15%
where the time goes in v2:
time: 107 us
  waiting for transfers between devices  44.2 us (41%)
  starting transfers between devices  32.6 us (30%)
  Pallas kernels  26.4 us (25%)
  other arithmetic  2.5 us (2%)
    ppermute x20, waiting for transfers between devices, permuted(): return lax.ppermute(value, ('dom', 'ka'), pairs)  42.6 us
    ppermute x20, starting transfers between devices, permuted(): return lax.ppermute(value, ('dom', 'ka'), pairs)  24.6 us
    pallas_call x2, Pallas kernels, per_device(): pl.pallas_call(functools.partial(cube_kernel, part), out_shape=pltpu.HBM(...  8.24 us
    ppermute x4, starting transfers between devices, along(): lax.ppermute(value, 'dom', [(source(d) % dom_count, d) for d in range(dom...  8.01 us
    pallas_call x1, Pallas kernels, per_device(): pl.pallas_call(far_kernel, out_shape=(shape((1536, columns), bf16), shape...  6.63 us
    pallas_call x1, Pallas kernels, per_device(): pl.pallas_call(own_kernel, out_shape=(pltpu.HBM((rows, 512), bf16), pltpu...  6.36 us
    pallas_call x1, Pallas kernels, per_device(): pl.pallas_call(near_kernel, out_shape=(pltpu.HBM((512, columns), bf16), p...  5.16 us
  transfers between devices with their start and end apart: 24, of which 7 were waited for; matrix products, arithmetic and copies ran while one was open for 3% of the time, Pallas kernels for 15%

profile of v2, /device:TPU:0, one launch (start us, length us, event | category | flops | bytes accessed | tf_op | source)
XLA Modules:
  0.0 106.8 jit_solution(7455737861507589969)
XLA Ops:
  0.0 7.0 %collective-permute-start.9 = (bf16[8,64,512]{2,1,0:T(8,128)(2,1)}, bf16[8,64,512]{2,1,0:T(8,128)(2,1)S(1)}, u32[]{:S(2)}, u32[]{:S(2)}) collective-permute-start(bf16[8,64,512]{2,1,0:T(8,128)(2,1)} %refs_0_.1), channel_id=1, source_target_pairs={{0,30},{1,31},{2,4},{3,5},{4,2},{5,3},{6,8},{7,9},{8,6},{9,7},{10,... | collective-permute-start | bytes 1572872 | tf_op jit(solution)/shard_map/ppermute | solution.py:16
  7.0 1.1 %collective-permute-start.3 = (bf16[8,64,512]{2,1,0:T(8,128)(2,1)}, bf16[8,64,512]{2,1,0:T(8,128)(2,1)S(1)}, u32[]{:S(2)}, u32[]{:S(2)}) collective-permute-start(bf16[8,64,512]{2,1,0:T(8,128)(2,1)} %refs_0_.1), channel_id=1, source_target_pairs={{0,24},{1,25},{2,10},{3,11},{4,28},{5,29},{6,14},{7,15},{8,0},{9,1... | collective-permute-start | bytes 1572872 | tf_op jit(solution)/shard_map/ppermute | solution.py:16
  8.1 0.7 collective-permute-start.13
  8.8 1.3 %collective-permute-start.8 = (s32[8,32]{1,0:T(8,128)}, s32[8,32]{1,0:T(8,128)S(1)}, u32[]{:S(2)}, u32[]{:S(2)}) collective-permute-start(s32[8,32]{1,0:T(8,128)} %param.4), channel_id=1, source_target_pairs={{4,0},{0,4},{12,8},{8,12},{20,16},{16,20},{28,24},{24,28},{5,1},{1... | collective-permute-start | bytes 3080 | tf_op jit(solution)/shard_map/ppermute | solution.py:276
  10.1 0.9 convert_reduce_fusion.4
  11.7 1.6 %collective-permute-done.8 = s32[8,32]{1,0:T(8,128)S(1)} collective-permute-done((s32[8,32]{1,0:T(8,128)}, s32[8,32]{1,0:T(8,128)S(1)}, u32[]{:S(2)}, u32[]{:S(2)}) %collective-permute-start.8) | collective-permute-done | bytes 1056 | tf_op jit(solution)/shard_map/ppermute | solution.py:276
  13.3 0.6 collective-permute-start.1
  13.9 6.1 %collective-permute-done.9.refs_2_.refs_7_ = bf16[8,64,512]{2,1,0:T(8,128)(2,1)S(1)} collective-permute-done((bf16[8,64,512]{2,1,0:T(8,128)(2,1)}, bf16[8,64,512]{2,1,0:T(8,128)(2,1)S(1)}, u32[]{:S(2)}, u32[]{:S(2)}) %collective-permute-start.9) | collective-permute-done | bytes 524320 | tf_op jit(solution)/shard_map/ppermute | solution.py:16
  20.1 1.9 %collective-permute-start = (s32[8,32]{1,0:T(8,128)}, s32[8,32]{1,0:T(8,128)S(1)}, u32[]{:S(2)}, u32[]{:S(2)}) collective-permute-start(s32[8,32]{1,0:T(8,128)} %param.4), channel_id=1, source_target_pairs={{28,0},{8,4},{4,8},{16,12},{12,16},{24,20},{20,24},{0,28},{29,1},{... | collective-permute-start | bytes 3080 | tf_op jit(solution)/shard_map/ppermute | solution.py:276
  22.0 8.9 %collective-permute-done.3.refs_0_ = bf16[8,64,512]{2,1,0:T(8,128)(2,1)S(1)} collective-permute-done((bf16[8,64,512]{2,1,0:T(8,128)(2,1)}, bf16[8,64,512]{2,1,0:T(8,128)(2,1)S(1)}, u32[]{:S(2)}, u32[]{:S(2)}) %collective-permute-start.3) | collective-permute-done | bytes 524320 | tf_op jit(solution)/shard_map/ppermute | solution.py:16
  30.9 4.2 %collective-permute-start.2 = (s32[8,32]{1,0:T(8,128)}, s32[8,32]{1,0:T(8,128)S(1)}, u32[]{:S(2)}, u32[]{:S(2)}) collective-permute-start(s32[8,32]{1,0:T(8,128)} %param.4), channel_id=1, source_target_pairs={{8,0},{12,4},{16,8},{20,12},{24,16},{28,20},{0,24},{4,28},{9,1},{1... | collective-permute-start | bytes 3080 | tf_op jit(solution)/shard_map/ppermute | solution.py:276
  35.1 0.5 collective-permute-start.4
  35.5 0.9 broadcast_select_fusion
  36.7 0.8 collective-permute-start.5
  37.5 2.8 %collective-permute-start.10 = (bf16[8,64,512]{2,1,0:T(8,128)(2,1)}, bf16[8,64,512]{2,1,0:T(8,128)(2,1)}, u32[]{:S(2)}, u32[]{:S(2)}) collective-permute-start(bf16[8,64,512]{2,1,0:T(8,128)(2,1)} %refs_0_.1), channel_id=1, source_target_pairs={{0,4},{1,5},{2,6},{3,7},{4,0},{5,1},{6,2},{7,3},{8,12},{9,13},{10,... | collective-permute-start | bytes 1572872 | tf_op jit(solution)/shard_map/ppermute | solution.py:16
  40.5 9.2 %collective-permute-done.4.refs_3_ = bf16[8,64,512]{2,1,0:T(8,128)(2,1)S(1)} collective-permute-done((bf16[8,64,512]{2,1,0:T(8,128)(2,1)S(1)}, bf16[8,64,512]{2,1,0:T(8,128)(2,1)S(1)}, u32[]{:S(2)}, u32[]{:S(2)}) %collective-permute-start.4) | collective-permute-done | bytes 524320 | tf_op jit(solution)/shard_map/ppermute | solution.py:16
  49.7 3.1 %collective-permute-start.12 = (bf16[8,64,512]{2,1,0:T(8,128)(2,1)S(1)}, bf16[8,64,512]{2,1,0:T(8,128)(2,1)}, u32[]{:S(2)}, u32[]{:S(2)}) collective-permute-start(bf16[8,64,512]{2,1,0:T(8,128)(2,1)S(1)} %collective-permute-done.9.refs_2_.refs_7_), channel_id=1, source_target_pairs={{0,1},{3,2},{4,5},{7,6},{8,9},{11,10},{12,13},{15,14},{16,17},{19,... | collective-permute-start | bytes 1572872 | tf_op jit(solution)/shard_map/ppermute | solution.py:16
  53.0 0.2 convert_reduce_fusion.1
  53.3 3.2 %collective-permute-start.11 = (bf16[8,64,512]{2,1,0:T(8,128)(2,1)}, bf16[8,64,512]{2,1,0:T(8,128)(2,1)}, u32[]{:S(2)}, u32[]{:S(2)}) collective-permute-start(bf16[8,64,512]{2,1,0:T(8,128)(2,1)} %collective-permute-done.10.refs_0_), channel_id=1, source_target_pairs={{0,1},{2,3},{5,4},{7,6},{8,9},{10,11},{13,12},{15,14},{16,17},{18,... | collective-permute-start | bytes 1572872 | tf_op jit(solution)/shard_map/ppermute | solution.py:16
  56.5 7.6 %collective-permute-done.16.refs_5_ = bf16[8,64,512]{2,1,0:T(8,128)(2,1)S(1)} collective-permute-done((bf16[8,64,512]{2,1,0:T(8,128)(2,1)S(1)}, bf16[8,64,512]{2,1,0:T(8,128)(2,1)S(1)}, u32[]{:S(2)}, u32[]{:S(2)}) %collective-permute-start.16) | collective-permute-done | bytes 524320 | tf_op jit(solution)/shard_map/ppermute | solution.py:16
  64.2 1.3 %collective-permute-start.17 = (bf16[8,64,512]{2,1,0:T(8,128)(2,1)S(1)}, bf16[8,64,512]{2,1,0:T(8,128)(2,1)S(1)}, u32[]{:S(2)}, u32[]{:S(2)}) collective-permute-start(bf16[8,64,512]{2,1,0:T(8,128)(2,1)S(1)} %collective-permute-done.16.refs_5_), channel_id=1, source_target_pairs={{1,0},{3,2},{4,5},{6,7},{9,8},{11,10},{12,13},{14,15},{17,16},{19,... | collective-permute-start | bytes 1572872 | tf_op jit(solution)/shard_map/ppermute | solution.py:16
  65.6 6.4 %shard_map.37 = (bf16[512,512]{1,0:T(8,128)(2,1)}, bf16[512,1536]{1,0:T(8,128)(2,1)}, bf16[512,1024]{1,0:T(8,128)(2,1)}, f32[512,1024]{1,0:T(8,128)}) custom-call(s32[31]{0:T(128)S(1)} %concatenate.12.meta_ref, s32[19]{0:T(128)S(1)} %concatenate.14.dest_ref, bf16[8,64,512]{2,1,0:T(8,128)(2,1)} %refs_0_.1, ...), custom_call_target="tpu_custom_call" | custom-call | flops 1073741824 | bytes 12582912 | tf_op jit(solution)/shard_map/pallas_call | solution.py:382
  72.0 5.2 %shard_map.38 = (bf16[512,1024]{1,0:T(8,128)(2,1)}, f32[8,64,512]{2,1,0:T(8,128)}) custom-call(s32[31]{0:T(128)S(1)} %concatenate.12.meta_ref, s32[15]{0:T(128)S(1)} %concatenate.15.dest_ref, bf16[512,512]{1,0:T(8,128)(2,1)} %get-tuple-element.26.left_in, f32[512,1024]{1,0:T(8,128)} %get-tuple-element.27.before_in, ...), custom_call_target="tpu_custom_call" | custom-call | flops 1073741824 | bytes 12582912 | tf_op jit(solution)/shard_map/pallas_call | solution.py:407
  77.2 6.6 %shard_map.39 = (bf16[1536,1024]{1,0:T(8,128)(2,1)S(1)}, f32[8,64,512]{2,1,0:T(8,128)S(1)}, bf16[4,64,512]{2,1,0:T(8,128)(2,1)S(1)}, bf16[4,64,512]{2,1,0:T(8,128)(2,1)S(1)}) custom-call(s32[31]{0:T(128)S(1)} %concatenate.12.meta_ref, s32[42]{0:T(128)S(1)} %concatenate.13.dest_ref, bf16[512,1536]{1,0:T(8,128)(2,1)} %get-tuple-element.24.left_ref, ...), custom_call_target="tpu_custom_call" | custom-call | flops 3221225472 | bytes 12582912 | tf_op jit(solution)/shard_map/pallas_call | solution.py:428
  83.8 1.0 collective-permute-start.22
  84.8 1.1 %collective-permute-start.19 = (bf16[4,64,512]{2,1,0:T(8,128)(2,1)S(1)}, bf16[4,64,512]{2,1,0:T(8,128)(2,1)S(1)}, u32[]{:S(2)}, u32[]{:S(2)}) collective-permute-start(bf16[4,64,512]{2,1,0:T(8,128)(2,1)S(1)} %get-tuple-element.31.own_ref), channel_id=1, source_target_pairs={{0,2},{1,3},{2,0},{3,1},{4,6},{5,7},{6,4},{7,5},{8,10},{9,11},{10,... | collective-permute-start | bytes 786440 | tf_op jit(solution)/shard_map/ppermute | solution.py:16
  85.9 0.8 collective-permute-start.21
  86.7 6.0 %collective-permute-done.22.x_ref = bf16[4,64,512]{2,1,0:T(8,128)(2,1)S(1)} collective-permute-done((bf16[4,64,512]{2,1,0:T(8,128)(2,1)S(1)}, bf16[4,64,512]{2,1,0:T(8,128)(2,1)S(1)}, u32[]{:S(2)}, u32[]{:S(2)}) %collective-permute-start.22) | collective-permute-done | bytes 262176 | tf_op jit(solution)/shard_map/ppermute | solution.py:16
  92.7 0.9 collective-permute-start.23
  93.6 4.7 %collective-permute-done.19.x_ref = bf16[4,64,512]{2,1,0:T(8,128)(2,1)S(1)} collective-permute-done((bf16[4,64,512]{2,1,0:T(8,128)(2,1)S(1)}, bf16[4,64,512]{2,1,0:T(8,128)(2,1)S(1)}, u32[]{:S(2)}, u32[]{:S(2)}) %collective-permute-start.19) | collective-permute-done | bytes 262176 | tf_op jit(solution)/shard_map/ppermute | solution.py:16
  98.6 4.1 %shard_map.40.refs_0_ = bf16[8,64,512]{2,1,0:T(8,128)(2,1)} custom-call(s32[31]{0:T(128)S(1)} %concatenate.12.meta_ref, bf16[4,64,512]{2,1,0:T(8,128)(2,1)S(1)} %get-tuple-element.36.own_ref, bf16[4,64,512]{2,1,0:T(8,128)(2,1)S(1)} %collective-permute-done.21.core_ref, bf16[4,64,512]{2,1,0:T(8,128)(2,1)S(1)} %collective-permute-done.22.x_ref, ...), custom_call_target="tpu_custom_call" | custom-call | flops 2684354560 | bytes 12582912 | tf_op jit(solution)/shard_map/pallas_call | solution.py:453
  102.7 4.1 %shard_map.41 = bf16[8,64,512]{2,1,0:T(8,128)(2,1)} custom-call(s32[31]{0:T(128)S(1)} %concatenate.12.meta_ref, bf16[4,64,512]{2,1,0:T(8,128)(2,1)S(1)} %get-tuple-element.31.own_ref, bf16[4,64,512]{2,1,0:T(8,128)(2,1)S(1)} %collective-permute-done.18.core_ref, ...), custom_call_target="tpu_custom_call", output_to_operand_aliasing={{}: (9, {})} | custom-call | flops 2684354560 | bytes 12582912 | tf_op jit(solution)/shard_map/pallas_call | solution.py:453
  (50 shorter events, 1.4 us)
Async XLA Ops:
  0.0 20.1 %collective-permute-start.9 = (bf16[8,64,512]{2,1,0:T(8,128)(2,1)}, bf16[8,64,512]{2,1,0:T(8,128)(2,1)S(1)}, u32[]{:S(2)}, u32[]{:S(2)}) collective-permute-start(bf16[8,64,512]{2,1,0:T(8,128)(2,1)} %refs_0_.1), channel_id=1, source_target_pairs={{0,30},{1,31},{2,4},{3,5},{4,2},{5,3},{6,8},{7,9},{8,6},{9,7},{10,... | collective-permute-start | bytes 1572872 | tf_op jit(solution)/shard_map/ppermute | solution.py:16
  7.0 33.4 %collective-permute-start.6 = (bf16[8,64,512]{2,1,0:T(8,128)(2,1)}, bf16[8,64,512]{2,1,0:T(8,128)(2,1)}, u32[]{:S(2)}, u32[]{:S(2)}) collective-permute-start(bf16[8,64,512]{2,1,0:T(8,128)(2,1)} %refs_0_.1), channel_id=1, source_target_pairs={{0,2},{1,3},{2,0},{3,1},{4,6},{5,7},{6,4},{7,5},{8,10},{9,11},{10,... | collective-permute-start | bytes 1572872 | tf_op jit(solution)/shard_map/ppermute | solution.py:16
  7.0 23.9 %collective-permute-start.3 = (bf16[8,64,512]{2,1,0:T(8,128)(2,1)}, bf16[8,64,512]{2,1,0:T(8,128)(2,1)S(1)}, u32[]{:S(2)}, u32[]{:S(2)}) collective-permute-start(bf16[8,64,512]{2,1,0:T(8,128)(2,1)} %refs_0_.1), channel_id=1, source_target_pairs={{0,24},{1,25},{2,10},{3,11},{4,28},{5,29},{6,14},{7,15},{8,0},{9,1... | collective-permute-start | bytes 1572872 | tf_op jit(solution)/shard_map/ppermute | solution.py:16
  8.1 27.0 %collective-permute-start.13 = (bf16[8,64,512]{2,1,0:T(8,128)(2,1)}, bf16[8,64,512]{2,1,0:T(8,128)(2,1)S(1)}, u32[]{:S(2)}, u32[]{:S(2)}) collective-permute-start(bf16[8,64,512]{2,1,0:T(8,128)(2,1)} %refs_0_.1), channel_id=1, source_target_pairs={{1,9},{2,26},{3,27},{4,12},{5,13},{6,30},{9,17},{10,2},{11,3},{12,... | collective-permute-start | bytes 1572872 | tf_op jit(solution)/shard_map/ppermute | solution.py:16
  8.8 4.6 %collective-permute-start.8 = (s32[8,32]{1,0:T(8,128)}, s32[8,32]{1,0:T(8,128)S(1)}, u32[]{:S(2)}, u32[]{:S(2)}) collective-permute-start(s32[8,32]{1,0:T(8,128)} %param.4), channel_id=1, source_target_pairs={{4,0},{0,4},{12,8},{8,12},{20,16},{16,20},{28,24},{24,28},{5,1},{1... | collective-permute-start | bytes 3080 | tf_op jit(solution)/shard_map/ppermute | solution.py:276
  13.3 23.3 %collective-permute-start.1 = (s32[8,32]{1,0:T(8,128)}, s32[8,32]{1,0:T(8,128)S(1)}, u32[]{:S(2)}, u32[]{:S(2)}) collective-permute-start(s32[8,32]{1,0:T(8,128)} %param.4), channel_id=1, source_target_pairs={{24,0},{28,4},{0,8},{4,12},{8,16},{12,20},{16,24},{20,28},{25,1},{... | collective-permute-start | bytes 3080 | tf_op jit(solution)/shard_map/ppermute | solution.py:276
  20.1 51.9 %copy-start.2 = (bf16[8,64,512]{2,1,0:T(8,128)(2,1)}, bf16[8,64,512]{2,1,0:T(8,128)(2,1)S(1)}, u32[]{:S(2)}) copy-start(bf16[8,64,512]{2,1,0:T(8,128)(2,1)S(1)} %collective-permute-done.9.refs_2_.refs_7_) | copy-start | bytes 1572868
  20.1 17.4 %collective-permute-start = (s32[8,32]{1,0:T(8,128)}, s32[8,32]{1,0:T(8,128)S(1)}, u32[]{:S(2)}, u32[]{:S(2)}) collective-permute-start(s32[8,32]{1,0:T(8,128)} %param.4), channel_id=1, source_target_pairs={{28,0},{8,4},{4,8},{16,12},{12,16},{24,20},{20,24},{0,28},{29,1},{... | collective-permute-start | bytes 3080 | tf_op jit(solution)/shard_map/ppermute | solution.py:276
  30.9 22.4 %copy-start.3 = (bf16[8,64,512]{2,1,0:T(8,128)(2,1)}, bf16[8,64,512]{2,1,0:T(8,128)(2,1)S(1)}, u32[]{:S(2)}) copy-start(bf16[8,64,512]{2,1,0:T(8,128)(2,1)S(1)} %collective-permute-done.3.refs_0_) | copy-start | bytes 1572868
  30.9 9.3 %collective-permute-start.2 = (s32[8,32]{1,0:T(8,128)}, s32[8,32]{1,0:T(8,128)S(1)}, u32[]{:S(2)}, u32[]{:S(2)}) collective-permute-start(s32[8,32]{1,0:T(8,128)} %param.4), channel_id=1, source_target_pairs={{8,0},{12,4},{16,8},{20,12},{24,16},{28,20},{0,24},{4,28},{9,1},{1... | collective-permute-start | bytes 3080 | tf_op jit(solution)/shard_map/ppermute | solution.py:276
  35.1 5.2 %copy-start.4 = (bf16[8,64,512]{2,1,0:T(8,128)(2,1)}, bf16[8,64,512]{2,1,0:T(8,128)(2,1)S(1)}, u32[]{:S(2)}) copy-start(bf16[8,64,512]{2,1,0:T(8,128)(2,1)S(1)} %collective-permute-done.13.refs_1_) | copy-start | bytes 1572868
  35.1 14.6 %collective-permute-start.4 = (bf16[8,64,512]{2,1,0:T(8,128)(2,1)S(1)}, bf16[8,64,512]{2,1,0:T(8,128)(2,1)S(1)}, u32[]{:S(2)}, u32[]{:S(2)}) collective-permute-start(bf16[8,64,512]{2,1,0:T(8,128)(2,1)S(1)} %collective-permute-done.3.refs_0_), channel_id=1, source_target_pairs={{0,2},{1,3},{2,0},{3,1},{4,6},{5,7},{6,4},{7,5},{8,10},{9,11},{10,... | collective-permute-start | bytes 1572872 | tf_op jit(solution)/shard_map/ppermute | solution.py:16
  36.7 16.6 %collective-permute-start.5 = (bf16[8,64,512]{2,1,0:T(8,128)(2,1)}, bf16[8,64,512]{2,1,0:T(8,128)(2,1)}, u32[]{:S(2)}, u32[]{:S(2)}) collective-permute-start(bf16[8,64,512]{2,1,0:T(8,128)(2,1)} %refs_0_.1), channel_id=1, source_target_pairs={{0,1},{1,0},{2,3},{3,2},{4,5},{5,4},{6,7},{7,6},{8,9},{9,8},{10,11... | collective-permute-start | bytes 1572872 | tf_op jit(solution)/shard_map/ppermute | solution.py:16
  37.5 15.9 %collective-permute-start.10 = (bf16[8,64,512]{2,1,0:T(8,128)(2,1)}, bf16[8,64,512]{2,1,0:T(8,128)(2,1)}, u32[]{:S(2)}, u32[]{:S(2)}) collective-permute-start(bf16[8,64,512]{2,1,0:T(8,128)(2,1)} %refs_0_.1), channel_id=1, source_target_pairs={{0,4},{1,5},{2,6},{3,7},{4,0},{5,1},{6,2},{7,3},{8,12},{9,13},{10,... | collective-permute-start | bytes 1572872 | tf_op jit(solution)/shard_map/ppermute | solution.py:16
  40.2 23.9 %collective-permute-start.16 = (bf16[8,64,512]{2,1,0:T(8,128)(2,1)S(1)}, bf16[8,64,512]{2,1,0:T(8,128)(2,1)S(1)}, u32[]{:S(2)}, u32[]{:S(2)}) collective-permute-start(bf16[8,64,512]{2,1,0:T(8,128)(2,1)S(1)} %get-tuple-element.39), channel_id=1, source_target_pairs={{0,4},{1,5},{2,6},{3,7},{4,0},{5,1},{6,2},{7,3},{8,12},{9,13},{10,... | collective-permute-start | bytes 1572872 | tf_op jit(solution)/shard_map/ppermute | solution.py:16
  40.3 16.2 %collective-permute-start.7 = (bf16[8,64,512]{2,1,0:T(8,128)(2,1)}, bf16[8,64,512]{2,1,0:T(8,128)(2,1)}, u32[]{:S(2)}, u32[]{:S(2)}) collective-permute-start(bf16[8,64,512]{2,1,0:T(8,128)(2,1)} %collective-permute-done.6.refs_2_), channel_id=1, source_target_pairs={{0,1},{1,0},{2,3},{3,2},{4,5},{5,4},{6,7},{7,6},{8,9},{9,8},{10,11... | collective-permute-start | bytes 1572872 | tf_op jit(solution)/shard_map/ppermute | solution.py:16
  49.7 22.3 %collective-permute-start.12 = (bf16[8,64,512]{2,1,0:T(8,128)(2,1)S(1)}, bf16[8,64,512]{2,1,0:T(8,128)(2,1)}, u32[]{:S(2)}, u32[]{:S(2)}) collective-permute-start(bf16[8,64,512]{2,1,0:T(8,128)(2,1)S(1)} %collective-permute-done.9.refs_2_.refs_7_), channel_id=1, source_target_pairs={{0,1},{3,2},{4,5},{7,6},{8,9},{11,10},{12,13},{15,14},{16,17},{19,... | collective-permute-start | bytes 1572872 | tf_op jit(solution)/shard_map/ppermute | solution.py:16
  53.2 23.9 %collective-permute-start.14 = (bf16[8,64,512]{2,1,0:T(8,128)(2,1)}, bf16[8,64,512]{2,1,0:T(8,128)(2,1)S(1)}, u32[]{:S(2)}, u32[]{:S(2)}) collective-permute-start(bf16[8,64,512]{2,1,0:T(8,128)(2,1)} %get-tuple-element.40), channel_id=1, source_target_pairs={{0,1},{1,0},{2,3},{3,2},{4,5},{5,4},{6,7},{7,6},{8,9},{9,8},{10,11... | collective-permute-start | bytes 1572872 | tf_op jit(solution)/shard_map/ppermute | solution.py:16
  53.3 18.6 %collective-permute-start.11 = (bf16[8,64,512]{2,1,0:T(8,128)(2,1)}, bf16[8,64,512]{2,1,0:T(8,128)(2,1)}, u32[]{:S(2)}, u32[]{:S(2)}) collective-permute-start(bf16[8,64,512]{2,1,0:T(8,128)(2,1)} %collective-permute-done.10.refs_0_), channel_id=1, source_target_pairs={{0,1},{2,3},{5,4},{7,6},{8,9},{10,11},{13,12},{15,14},{16,17},{18,... | collective-permute-start | bytes 1572872 | tf_op jit(solution)/shard_map/ppermute | solution.py:16
  56.5 20.6 %collective-permute-start.15 = (bf16[8,64,512]{2,1,0:T(8,128)(2,1)S(1)}, bf16[8,64,512]{2,1,0:T(8,128)(2,1)S(1)}, u32[]{:S(2)}, u32[]{:S(2)}) collective-permute-start(bf16[8,64,512]{2,1,0:T(8,128)(2,1)S(1)} %collective-permute-done.4.refs_3_), channel_id=1, source_target_pairs={{0,1},{1,0},{2,3},{3,2},{4,5},{5,4},{6,7},{7,6},{8,9},{9,8},{10,11... | collective-permute-start | bytes 1572872 | tf_op jit(solution)/shard_map/ppermute | solution.py:16
  64.2 13.0 %collective-permute-start.17 = (bf16[8,64,512]{2,1,0:T(8,128)(2,1)S(1)}, bf16[8,64,512]{2,1,0:T(8,128)(2,1)S(1)}, u32[]{:S(2)}, u32[]{:S(2)}) collective-permute-start(bf16[8,64,512]{2,1,0:T(8,128)(2,1)S(1)} %collective-permute-done.16.refs_5_), channel_id=1, source_target_pairs={{1,0},{3,2},{4,5},{6,7},{9,8},{11,10},{12,13},{14,15},{17,16},{19,... | collective-permute-start | bytes 1572872 | tf_op jit(solution)/shard_map/ppermute | solution.py:16
  77.2 21.4 %copy-start = (bf16[512,1024]{1,0:T(8,128)(2,1)S(1)}, bf16[512,1024]{1,0:T(8,128)(2,1)}, u32[]{:S(2)}) copy-start(bf16[512,1024]{1,0:T(8,128)(2,1)} %get-tuple-element.33.table_near) | copy-start | bytes 3145732
  77.2 21.3 %copy-start.1 = (bf16[512,1024]{1,0:T(8,128)(2,1)S(1)}, bf16[512,1024]{1,0:T(8,128)(2,1)}, u32[]{:S(2)}) copy-start(bf16[512,1024]{1,0:T(8,128)(2,1)} %get-tuple-element.32.table_own) | copy-start | bytes 3145732
  83.8 8.9 %collective-permute-start.22 = (bf16[4,64,512]{2,1,0:T(8,128)(2,1)S(1)}, bf16[4,64,512]{2,1,0:T(8,128)(2,1)S(1)}, u32[]{:S(2)}, u32[]{:S(2)}) collective-permute-start(bf16[4,64,512]{2,1,0:T(8,128)(2,1)S(1)} %get-tuple-element.36.own_ref), channel_id=1, source_target_pairs={{0,2},{1,3},{2,0},{3,1},{4,6},{5,7},{6,4},{7,5},{8,10},{9,11},{10,... | collective-permute-start | bytes 786440 | tf_op jit(solution)/shard_map/ppermute | solution.py:16
  84.8 13.5 %collective-permute-start.19 = (bf16[4,64,512]{2,1,0:T(8,128)(2,1)S(1)}, bf16[4,64,512]{2,1,0:T(8,128)(2,1)S(1)}, u32[]{:S(2)}, u32[]{:S(2)}) collective-permute-start(bf16[4,64,512]{2,1,0:T(8,128)(2,1)S(1)} %get-tuple-element.31.own_ref), channel_id=1, source_target_pairs={{0,2},{1,3},{2,0},{3,1},{4,6},{5,7},{6,4},{7,5},{8,10},{9,11},{10,... | collective-permute-start | bytes 786440 | tf_op jit(solution)/shard_map/ppermute | solution.py:16
  85.9 12.6 %collective-permute-start.21 = (bf16[4,64,512]{2,1,0:T(8,128)(2,1)S(1)}, bf16[4,64,512]{2,1,0:T(8,128)(2,1)S(1)}, u32[]{:S(2)}, u32[]{:S(2)}) collective-permute-start(bf16[4,64,512]{2,1,0:T(8,128)(2,1)S(1)} %get-tuple-element.36.own_ref), channel_id=1, source_target_pairs={{0,1},{1,0},{2,3},{3,2},{4,5},{5,4},{6,7},{7,6},{8,9},{9,8},{10,11... | collective-permute-start | bytes 786440 | tf_op jit(solution)/shard_map/ppermute | solution.py:16
  92.7 5.8 %collective-permute-start.23 = (bf16[4,64,512]{2,1,0:T(8,128)(2,1)S(1)}, bf16[4,64,512]{2,1,0:T(8,128)(2,1)S(1)}, u32[]{:S(2)}, u32[]{:S(2)}) collective-permute-start(bf16[4,64,512]{2,1,0:T(8,128)(2,1)S(1)} %collective-permute-done.22.x_ref), channel_id=1, source_target_pairs={{0,1},{1,0},{2,3},{3,2},{4,5},{5,4},{6,7},{7,6},{8,9},{9,8},{10,11... | collective-permute-start | bytes 786440 | tf_op jit(solution)/shard_map/ppermute | solution.py:16
  93.6 9.1 %collective-permute-start.18 = (bf16[4,64,512]{2,1,0:T(8,128)(2,1)S(1)}, bf16[4,64,512]{2,1,0:T(8,128)(2,1)S(1)}, u32[]{:S(2)}, u32[]{:S(2)}) collective-permute-start(bf16[4,64,512]{2,1,0:T(8,128)(2,1)S(1)} %get-tuple-element.31.own_ref), channel_id=1, source_target_pairs={{0,1},{1,0},{2,3},{3,2},{4,5},{5,4},{6,7},{7,6},{8,9},{9,8},{10,11... | collective-permute-start | bytes 786440 | tf_op jit(solution)/shard_map/ppermute | solution.py:16
  98.3 4.4 %collective-permute-start.20 = (bf16[4,64,512]{2,1,0:T(8,128)(2,1)S(1)}, bf16[4,64,512]{2,1,0:T(8,128)(2,1)S(1)}, u32[]{:S(2)}, u32[]{:S(2)}) collective-permute-start(bf16[4,64,512]{2,1,0:T(8,128)(2,1)S(1)} %collective-permute-done.19.x_ref), channel_id=1, source_target_pairs={{0,1},{1,0},{2,3},{3,2},{4,5},{5,4},{6,7},{7,6},{8,9},{9,8},{10,11... | collective-permute-start | bytes 786440 | tf_op jit(solution)/shard_map/ppermute | solution.py:16

commit v3 on v2

--- a/solution.py
+++ b/solution.py
@@ -115,15 +115,8 @@
 
 
 def product(left_ref, table_ref, total_ref, before_ref=None):
-    depth = table_ref.shape[0]
-
-    def step(tile, carry):
-        cols = pl.ds(pl.multiple_of(tile * 256, 256), 256)
-        value = jnp.dot(left_ref[:, :depth], table_ref[:, cols], preferred_element_type=jnp.float32)
-        total_ref[:, cols] = value if before_ref is None else before_ref[:, cols] + value
-        return carry
-
-    lax.fori_loop(0, table_ref.shape[1] // 256, step, 0)
+    value = jnp.dot(left_ref[...], table_ref[...], preferred_element_type=jnp.float32)
+    total_ref[...] = value if before_ref is None else before_ref[...] + value
 
 
 def transfers(pairs, sems):
@@ -205,14 +198,7 @@
             at = window * 512 + row * 64
             table_ref[at:at + 64, :] = spread(blocks, 8 - row, 16, dest_ref[18 + window * 8 + row])
 
-    def step(tile, carry):
-        cols = pl.ds(pl.multiple_of(tile * 256, 256), 256)
-        total_ref[:, cols] = jnp.dot(
-            left_ref[...], table_ref[:, cols], preferred_element_type=jnp.float32
-        )
-        return carry
-
-    lax.fori_loop(0, 4, step, 0)
+    product(left_ref, table_ref, total_ref)
     for row in range(row_count):
         picked = base_ref[row] + kept(total_ref[row * 64:(row + 1) * 64, :], row, meta_ref[8 + row], 512)
         square_ref[row] = picked
@@ -229,16 +215,11 @@
         store[group ^ bits] = ref[...]
     fill_left(left_ref, store, first_row, lambda row: meta_ref[16 + row], lambda window: meta_ref[24 + window])
 
-    def step(tile, carry):
-        cols = pl.ds(pl.multiple_of(tile * 256, 256), 256)
-        total_ref[:, cols] = (
-            jnp.dot(left_ref[:, :512], table_own[:, cols], preferred_element_type=jnp.float32)
-            + jnp.dot(left_ref[:, 512:1024], table_near[:, cols], preferred_element_type=jnp.float32)
-            + jnp.dot(left_ref[:, 1024:], table_b[:, cols], preferred_element_type=jnp.float32)
-        )
-        return carry
-
-    lax.fori_loop(0, 4, step, 0)
+    total_ref[...] = (
+        jnp.dot(left_ref[:, :512], table_own[...], preferred_element_type=jnp.float32)
+        + jnp.dot(left_ref[:, 512:1024], table_near[...], preferred_element_type=jnp.float32)
+        + jnp.dot(left_ref[:, 1024:], table_b[...], preferred_element_type=jnp.float32)
+    )
     for row in range(row_count):
         whole = first_row + row
         cube = kept(total_ref[row * 64:(row + 1) * 64, :], whole, meta_ref[8 + whole], 512)

time: 107 us -> 103 us (0.963)
  Pallas kernels: 26.4 us -> 22.3 us
    pallas_call x2, Pallas kernels: 8.24 us -> 6.59 us  [per_device(): pl.pallas_call(functools.partial(cube_kernel, part), out_shape=pltpu.HBM(...]
    pallas_call x1, Pallas kernels: 6.63 us -> 5.15 us  [per_device(): pl.pallas_call(far_kernel, out_shape=(shape((1536, columns), bf16), shape...]
  transfers between devices with their start and end apart: 24 -> 24, of which waited for: 7 -> 7; matrix products, arithmetic and copies ran while one was open for 3% -> 3% of each run, Pallas kernels for 15% -> 13%
where the time goes in v3:
time: 103 us
  waiting for transfers between devices  44.2 us (43%)
  starting transfers between devices  32.6 us (32%)
  Pallas kernels  22.3 us (22%)
  other arithmetic  2.5 us (2%)
    ppermute x20, waiting for transfers between devices, permuted(): return lax.ppermute(value, ('dom', 'ka'), pairs)  42.6 us
    ppermute x20, starting transfers between devices, permuted(): return lax.ppermute(value, ('dom', 'ka'), pairs)  24.6 us
    ppermute x4, starting transfers between devices, along(): lax.ppermute(value, 'dom', [(source(d) % dom_count, d) for d in range(dom...  8.01 us
    pallas_call x2, Pallas kernels, per_device(): pl.pallas_call(functools.partial(cube_kernel, part), out_shape=pltpu.HBM(...  6.59 us
    pallas_call x1, Pallas kernels, per_device(): pl.pallas_call(own_kernel, out_shape=(pltpu.HBM((rows, 512), bf16), pltpu...  6.21 us
    pallas_call x1, Pallas kernels, per_device(): pl.pallas_call(far_kernel, out_shape=(shape((1536, columns), bf16), shape...  5.15 us
    pallas_call x1, Pallas kernels, per_device(): pl.pallas_call(near_kernel, out_shape=(pltpu.HBM((512, columns), bf16), p...  4.37 us
  transfers between devices with their start and end apart: 24, of which 7 were waited for; matrix products, arithmetic and copies ran while one was open for 3% of the time, Pallas kernels for 13%

profile of v3, /device:TPU:0, one launch (start us, length us, event | category | flops | bytes accessed | tf_op | source)
XLA Modules:
  0.0 102.9 jit_solution(16312938767296703110)
XLA Ops:
  0.0 7.0 %collective-permute-start.9 = (bf16[8,64,512]{2,1,0:T(8,128)(2,1)}, bf16[8,64,512]{2,1,0:T(8,128)(2,1)S(1)}, u32[]{:S(2)}, u32[]{:S(2)}) collective-permute-start(bf16[8,64,512]{2,1,0:T(8,128)(2,1)} %refs_0_.1), channel_id=1, source_target_pairs={{0,30},{1,31},{2,4},{3,5},{4,2},{5,3},{6,8},{7,9},{8,6},{9,7},{10,... | collective-permute-start | bytes 1572872 | tf_op jit(solution)/shard_map/ppermute | solution.py:16
  7.0 1.1 %collective-permute-start.3 = (bf16[8,64,512]{2,1,0:T(8,128)(2,1)}, bf16[8,64,512]{2,1,0:T(8,128)(2,1)S(1)}, u32[]{:S(2)}, u32[]{:S(2)}) collective-permute-start(bf16[8,64,512]{2,1,0:T(8,128)(2,1)} %refs_0_.1), channel_id=1, source_target_pairs={{0,24},{1,25},{2,10},{3,11},{4,28},{5,29},{6,14},{7,15},{8,0},{9,1... | collective-permute-start | bytes 1572872 | tf_op jit(solution)/shard_map/ppermute | solution.py:16
  8.1 0.7 collective-permute-start.13
  8.8 1.3 %collective-permute-start.8 = (s32[8,32]{1,0:T(8,128)}, s32[8,32]{1,0:T(8,128)S(1)}, u32[]{:S(2)}, u32[]{:S(2)}) collective-permute-start(s32[8,32]{1,0:T(8,128)} %param.4), channel_id=1, source_target_pairs={{4,0},{0,4},{12,8},{8,12},{20,16},{16,20},{28,24},{24,28},{5,1},{1... | collective-permute-start | bytes 3080 | tf_op jit(solution)/shard_map/ppermute | solution.py:257
  10.1 0.9 convert_reduce_fusion.4
  11.7 1.6 %collective-permute-done.8 = s32[8,32]{1,0:T(8,128)S(1)} collective-permute-done((s32[8,32]{1,0:T(8,128)}, s32[8,32]{1,0:T(8,128)S(1)}, u32[]{:S(2)}, u32[]{:S(2)}) %collective-permute-start.8) | collective-permute-done | bytes 1056 | tf_op jit(solution)/shard_map/ppermute | solution.py:257
  13.3 0.6 collective-permute-start.1
  13.9 6.1 %collective-permute-done.9.refs_2_.refs_7_ = bf16[8,64,512]{2,1,0:T(8,128)(2,1)S(1)} collective-permute-done((bf16[8,64,512]{2,1,0:T(8,128)(2,1)}, bf16[8,64,512]{2,1,0:T(8,128)(2,1)S(1)}, u32[]{:S(2)}, u32[]{:S(2)}) %collective-permute-start.9) | collective-permute-done | bytes 524320 | tf_op jit(solution)/shard_map/ppermute | solution.py:16
  20.1 1.9 %collective-permute-start = (s32[8,32]{1,0:T(8,128)}, s32[8,32]{1,0:T(8,128)S(1)}, u32[]{:S(2)}, u32[]{:S(2)}) collective-permute-start(s32[8,32]{1,0:T(8,128)} %param.4), channel_id=1, source_target_pairs={{28,0},{8,4},{4,8},{16,12},{12,16},{24,20},{20,24},{0,28},{29,1},{... | collective-permute-start | bytes 3080 | tf_op jit(solution)/shard_map/ppermute | solution.py:257
  22.0 8.9 %collective-permute-done.3.refs_0_ = bf16[8,64,512]{2,1,0:T(8,128)(2,1)S(1)} collective-permute-done((bf16[8,64,512]{2,1,0:T(8,128)(2,1)}, bf16[8,64,512]{2,1,0:T(8,128)(2,1)S(1)}, u32[]{:S(2)}, u32[]{:S(2)}) %collective-permute-start.3) | collective-permute-done | bytes 524320 | tf_op jit(solution)/shard_map/ppermute | solution.py:16
  30.9 4.2 %collective-permute-start.2 = (s32[8,32]{1,0:T(8,128)}, s32[8,32]{1,0:T(8,128)S(1)}, u32[]{:S(2)}, u32[]{:S(2)}) collective-permute-start(s32[8,32]{1,0:T(8,128)} %param.4), channel_id=1, source_target_pairs={{8,0},{12,4},{16,8},{20,12},{24,16},{28,20},{0,24},{4,28},{9,1},{1... | collective-permute-start | bytes 3080 | tf_op jit(solution)/shard_map/ppermute | solution.py:257
  35.1 0.5 collective-permute-start.4
  35.5 0.9 broadcast_select_fusion
  36.7 0.8 collective-permute-start.5
  37.5 2.8 %collective-permute-start.10 = (bf16[8,64,512]{2,1,0:T(8,128)(2,1)}, bf16[8,64,512]{2,1,0:T(8,128)(2,1)}, u32[]{:S(2)}, u32[]{:S(2)}) collective-permute-start(bf16[8,64,512]{2,1,0:T(8,128)(2,1)} %refs_0_.1), channel_id=1, source_target_pairs={{0,4},{1,5},{2,6},{3,7},{4,0},{5,1},{6,2},{7,3},{8,12},{9,13},{10,... | collective-permute-start | bytes 1572872 | tf_op jit(solution)/shard_map/ppermute | solution.py:16
  40.5 9.2 %collective-permute-done.4.refs_3_ = bf16[8,64,512]{2,1,0:T(8,128)(2,1)S(1)} collective-permute-done((bf16[8,64,512]{2,1,0:T(8,128)(2,1)S(1)}, bf16[8,64,512]{2,1,0:T(8,128)(2,1)S(1)}, u32[]{:S(2)}, u32[]{:S(2)}) %collective-permute-start.4) | collective-permute-done | bytes 524320 | tf_op jit(solution)/shard_map/ppermute | solution.py:16
  49.7 3.1 %collective-permute-start.12 = (bf16[8,64,512]{2,1,0:T(8,128)(2,1)S(1)}, bf16[8,64,512]{2,1,0:T(8,128)(2,1)}, u32[]{:S(2)}, u32[]{:S(2)}) collective-permute-start(bf16[8,64,512]{2,1,0:T(8,128)(2,1)S(1)} %collective-permute-done.9.refs_2_.refs_7_), channel_id=1, source_target_pairs={{0,1},{3,2},{4,5},{7,6},{8,9},{11,10},{12,13},{15,14},{16,17},{19,... | collective-permute-start | bytes 1572872 | tf_op jit(solution)/shard_map/ppermute | solution.py:16
  53.0 0.2 convert_reduce_fusion.1
  53.3 3.2 %collective-permute-start.11 = (bf16[8,64,512]{2,1,0:T(8,128)(2,1)}, bf16[8,64,512]{2,1,0:T(8,128)(2,1)}, u32[]{:S(2)}, u32[]{:S(2)}) collective-permute-start(bf16[8,64,512]{2,1,0:T(8,128)(2,1)} %collective-permute-done.10.refs_0_), channel_id=1, source_target_pairs={{0,1},{2,3},{5,4},{7,6},{8,9},{10,11},{13,12},{15,14},{16,17},{18,... | collective-permute-start | bytes 1572872 | tf_op jit(solution)/shard_map/ppermute | solution.py:16
  56.5 7.6 %collective-permute-done.16.refs_5_ = bf16[8,64,512]{2,1,0:T(8,128)(2,1)S(1)} collective-permute-done((bf16[8,64,512]{2,1,0:T(8,128)(2,1)S(1)}, bf16[8,64,512]{2,1,0:T(8,128)(2,1)S(1)}, u32[]{:S(2)}, u32[]{:S(2)}) %collective-permute-start.16) | collective-permute-done | bytes 524320 | tf_op jit(solution)/shard_map/ppermute | solution.py:16
  64.2 1.3 %collective-permute-start.17 = (bf16[8,64,512]{2,1,0:T(8,128)(2,1)S(1)}, bf16[8,64,512]{2,1,0:T(8,128)(2,1)S(1)}, u32[]{:S(2)}, u32[]{:S(2)}) collective-permute-start(bf16[8,64,512]{2,1,0:T(8,128)(2,1)S(1)} %collective-permute-done.16.refs_5_), channel_id=1, source_target_pairs={{1,0},{3,2},{4,5},{6,7},{9,8},{11,10},{12,13},{14,15},{17,16},{19,... | collective-permute-start | bytes 1572872 | tf_op jit(solution)/shard_map/ppermute | solution.py:16
  65.6 6.2 %shard_map.37 = (bf16[512,512]{1,0:T(8,128)(2,1)}, bf16[512,1536]{1,0:T(8,128)(2,1)}, bf16[512,1024]{1,0:T(8,128)(2,1)}, f32[512,1024]{1,0:T(8,128)}) custom-call(s32[31]{0:T(128)S(1)} %concatenate.12.meta_ref, s32[19]{0:T(128)S(1)} %concatenate.14.dest_ref, bf16[8,64,512]{2,1,0:T(8,128)(2,1)} %refs_0_.1, ...), custom_call_target="tpu_custom_call" | custom-call | flops 1073741824 | bytes 12582912 | tf_op jit(solution)/shard_map/pallas_call | solution.py:363
  71.8 4.4 %shard_map.38 = (bf16[512,1024]{1,0:T(8,128)(2,1)}, f32[8,64,512]{2,1,0:T(8,128)}) custom-call(s32[31]{0:T(128)S(1)} %concatenate.12.meta_ref, s32[15]{0:T(128)S(1)} %concatenate.15.dest_ref, bf16[512,512]{1,0:T(8,128)(2,1)} %get-tuple-element.26.left_in, f32[512,1024]{1,0:T(8,128)} %get-tuple-element.27.before_in, ...), custom_call_target="tpu_custom_call" | custom-call | flops 1073741824 | bytes 12582912 | tf_op jit(solution)/shard_map/pallas_call | solution.py:388
  76.3 5.2 %shard_map.39 = (bf16[1536,1024]{1,0:T(8,128)(2,1)S(1)}, f32[8,64,512]{2,1,0:T(8,128)S(1)}, bf16[4,64,512]{2,1,0:T(8,128)(2,1)S(1)}, bf16[4,64,512]{2,1,0:T(8,128)(2,1)S(1)}) custom-call(s32[31]{0:T(128)S(1)} %concatenate.12.meta_ref, s32[42]{0:T(128)S(1)} %concatenate.13.dest_ref, bf16[512,1536]{1,0:T(8,128)(2,1)} %get-tuple-element.24.left_ref, ...), custom_call_target="tpu_custom_call" | custom-call | flops 3221225472 | bytes 12582912 | tf_op jit(solution)/shard_map/pallas_call | solution.py:409
  81.4 1.0 collective-permute-start.22
  82.4 1.1 %collective-permute-start.19 = (bf16[4,64,512]{2,1,0:T(8,128)(2,1)S(1)}, bf16[4,64,512]{2,1,0:T(8,128)(2,1)S(1)}, u32[]{:S(2)}, u32[]{:S(2)}) collective-permute-start(bf16[4,64,512]{2,1,0:T(8,128)(2,1)S(1)} %get-tuple-element.31.own_ref), channel_id=1, source_target_pairs={{0,2},{1,3},{2,0},{3,1},{4,6},{5,7},{6,4},{7,5},{8,10},{9,11},{10,... | collective-permute-start | bytes 786440 | tf_op jit(solution)/shard_map/ppermute | solution.py:16
  83.5 0.8 collective-permute-start.21
  84.3 6.0 %collective-permute-done.22.x_ref = bf16[4,64,512]{2,1,0:T(8,128)(2,1)S(1)} collective-permute-done((bf16[4,64,512]{2,1,0:T(8,128)(2,1)S(1)}, bf16[4,64,512]{2,1,0:T(8,128)(2,1)S(1)}, u32[]{:S(2)}, u32[]{:S(2)}) %collective-permute-start.22) | collective-permute-done | bytes 262176 | tf_op jit(solution)/shard_map/ppermute | solution.py:16
  90.3 0.9 collective-permute-start.23
  91.2 4.7 %collective-permute-done.19.x_ref = bf16[4,64,512]{2,1,0:T(8,128)(2,1)S(1)} collective-permute-done((bf16[4,64,512]{2,1,0:T(8,128)(2,1)S(1)}, bf16[4,64,512]{2,1,0:T(8,128)(2,1)S(1)}, u32[]{:S(2)}, u32[]{:S(2)}) %collective-permute-start.19) | collective-permute-done | bytes 262176 | tf_op jit(solution)/shard_map/ppermute | solution.py:16
  96.1 3.3 %shard_map.40.refs_0_ = bf16[8,64,512]{2,1,0:T(8,128)(2,1)} custom-call(s32[31]{0:T(128)S(1)} %concatenate.12.meta_ref, bf16[4,64,512]{2,1,0:T(8,128)(2,1)S(1)} %get-tuple-element.36.own_ref, bf16[4,64,512]{2,1,0:T(8,128)(2,1)S(1)} %collective-permute-done.21.core_ref, bf16[4,64,512]{2,1,0:T(8,128)(2,1)S(1)} %collective-permute-done.22.x_ref, ...), custom_call_target="tpu_custom_call" | custom-call | flops 2684354560 | bytes 12582912 | tf_op jit(solution)/shard_map/pallas_call | solution.py:434
  99.4 3.3 %shard_map.41 = bf16[8,64,512]{2,1,0:T(8,128)(2,1)} custom-call(s32[31]{0:T(128)S(1)} %concatenate.12.meta_ref, bf16[4,64,512]{2,1,0:T(8,128)(2,1)S(1)} %get-tuple-element.31.own_ref, bf16[4,64,512]{2,1,0:T(8,128)(2,1)S(1)} %collective-permute-done.18.core_ref, ...), custom_call_target="tpu_custom_call", output_to_operand_aliasing={{}: (9, {})} | custom-call | flops 2684354560 | bytes 12582912 | tf_op jit(solution)/shard_map/pallas_call | solution.py:434
  (50 shorter events, 1.4 us)
Async XLA Ops:
  0.0 20.1 %collective-permute-start.9 = (bf16[8,64,512]{2,1,0:T(8,128)(2,1)}, bf16[8,64,512]{2,1,0:T(8,128)(2,1)S(1)}, u32[]{:S(2)}, u32[]{:S(2)}) collective-permute-start(bf16[8,64,512]{2,1,0:T(8,128)(2,1)} %refs_0_.1), channel_id=1, source_target_pairs={{0,30},{1,31},{2,4},{3,5},{4,2},{5,3},{6,8},{7,9},{8,6},{9,7},{10,... | collective-permute-start | bytes 1572872 | tf_op jit(solution)/shard_map/ppermute | solution.py:16
  7.0 33.4 %collective-permute-start.6 = (bf16[8,64,512]{2,1,0:T(8,128)(2,1)}, bf16[8,64,512]{2,1,0:T(8,128)(2,1)}, u32[]{:S(2)}, u32[]{:S(2)}) collective-permute-start(bf16[8,64,512]{2,1,0:T(8,128)(2,1)} %refs_0_.1), channel_id=1, source_target_pairs={{0,2},{1,3},{2,0},{3,1},{4,6},{5,7},{6,4},{7,5},{8,10},{9,11},{10,... | collective-permute-start | bytes 1572872 | tf_op jit(solution)/shard_map/ppermute | solution.py:16
  7.0 23.9 %collective-permute-start.3 = (bf16[8,64,512]{2,1,0:T(8,128)(2,1)}, bf16[8,64,512]{2,1,0:T(8,128)(2,1)S(1)}, u32[]{:S(2)}, u32[]{:S(2)}) collective-permute-start(bf16[8,64,512]{2,1,0:T(8,128)(2,1)} %refs_0_.1), channel_id=1, source_target_pairs={{0,24},{1,25},{2,10},{3,11},{4,28},{5,29},{6,14},{7,15},{8,0},{9,1... | collective-permute-start | bytes 1572872 | tf_op jit(solution)/shard_map/ppermute | solution.py:16
  8.1 27.0 %collective-permute-start.13 = (bf16[8,64,512]{2,1,0:T(8,128)(2,1)}, bf16[8,64,512]{2,1,0:T(8,128)(2,1)S(1)}, u32[]{:S(2)}, u32[]{:S(2)}) collective-permute-start(bf16[8,64,512]{2,1,0:T(8,128)(2,1)} %refs_0_.1), channel_id=1, source_target_pairs={{1,9},{2,26},{3,27},{4,12},{5,13},{6,30},{9,17},{10,2},{11,3},{12,... | collective-permute-start | bytes 1572872 | tf_op jit(solution)/shard_map/ppermute | solution.py:16
  8.8 4.6 %collective-permute-start.8 = (s32[8,32]{1,0:T(8,128)}, s32[8,32]{1,0:T(8,128)S(1)}, u32[]{:S(2)}, u32[]{:S(2)}) collective-permute-start(s32[8,32]{1,0:T(8,128)} %param.4), channel_id=1, source_target_pairs={{4,0},{0,4},{12,8},{8,12},{20,16},{16,20},{28,24},{24,28},{5,1},{1... | collective-permute-start | bytes 3080 | tf_op jit(solution)/shard_map/ppermute | solution.py:257
  13.3 23.3 %collective-permute-start.1 = (s32[8,32]{1,0:T(8,128)}, s32[8,32]{1,0:T(8,128)S(1)}, u32[]{:S(2)}, u32[]{:S(2)}) collective-permute-start(s32[8,32]{1,0:T(8,128)} %param.4), channel_id=1, source_target_pairs={{24,0},{28,4},{0,8},{4,12},{8,16},{12,20},{16,24},{20,28},{25,1},{... | collective-permute-start | bytes 3080 | tf_op jit(solution)/shard_map/ppermute | solution.py:257
  20.1 51.7 %copy-start.2 = (bf16[8,64,512]{2,1,0:T(8,128)(2,1)}, bf16[8,64,512]{2,1,0:T(8,128)(2,1)S(1)}, u32[]{:S(2)}) copy-start(bf16[8,64,512]{2,1,0:T(8,128)(2,1)S(1)} %collective-permute-done.9.refs_2_.refs_7_) | copy-start | bytes 1572868
  20.1 17.4 %collective-permute-start = (s32[8,32]{1,0:T(8,128)}, s32[8,32]{1,0:T(8,128)S(1)}, u32[]{:S(2)}, u32[]{:S(2)}) collective-permute-start(s32[8,32]{1,0:T(8,128)} %param.4), channel_id=1, source_target_pairs={{28,0},{8,4},{4,8},{16,12},{12,16},{24,20},{20,24},{0,28},{29,1},{... | collective-permute-start | bytes 3080 | tf_op jit(solution)/shard_map/ppermute | solution.py:257
  30.9 22.4 %copy-start.3 = (bf16[8,64,512]{2,1,0:T(8,128)(2,1)}, bf16[8,64,512]{2,1,0:T(8,128)(2,1)S(1)}, u32[]{:S(2)}) copy-start(bf16[8,64,512]{2,1,0:T(8,128)(2,1)S(1)} %collective-permute-done.3.refs_0_) | copy-start | bytes 1572868
  30.9 9.3 %collective-permute-start.2 = (s32[8,32]{1,0:T(8,128)}, s32[8,32]{1,0:T(8,128)S(1)}, u32[]{:S(2)}, u32[]{:S(2)}) collective-permute-start(s32[8,32]{1,0:T(8,128)} %param.4), channel_id=1, source_target_pairs={{8,0},{12,4},{16,8},{20,12},{24,16},{28,20},{0,24},{4,28},{9,1},{1... | collective-permute-start | bytes 3080 | tf_op jit(solution)/shard_map/ppermute | solution.py:257
  35.1 5.2 %copy-start.4 = (bf16[8,64,512]{2,1,0:T(8,128)(2,1)}, bf16[8,64,512]{2,1,0:T(8,128)(2,1)S(1)}, u32[]{:S(2)}) copy-start(bf16[8,64,512]{2,1,0:T(8,128)(2,1)S(1)} %collective-permute-done.13.refs_1_) | copy-start | bytes 1572868
  35.1 14.6 %collective-permute-start.4 = (bf16[8,64,512]{2,1,0:T(8,128)(2,1)S(1)}, bf16[8,64,512]{2,1,0:T(8,128)(2,1)S(1)}, u32[]{:S(2)}, u32[]{:S(2)}) collective-permute-start(bf16[8,64,512]{2,1,0:T(8,128)(2,1)S(1)} %collective-permute-done.3.refs_0_), channel_id=1, source_target_pairs={{0,2},{1,3},{2,0},{3,1},{4,6},{5,7},{6,4},{7,5},{8,10},{9,11},{10,... | collective-permute-start | bytes 1572872 | tf_op jit(solution)/shard_map/ppermute | solution.py:16
  36.7 16.6 %collective-permute-start.5 = (bf16[8,64,512]{2,1,0:T(8,128)(2,1)}, bf16[8,64,512]{2,1,0:T(8,128)(2,1)}, u32[]{:S(2)}, u32[]{:S(2)}) collective-permute-start(bf16[8,64,512]{2,1,0:T(8,128)(2,1)} %refs_0_.1), channel_id=1, source_target_pairs={{0,1},{1,0},{2,3},{3,2},{4,5},{5,4},{6,7},{7,6},{8,9},{9,8},{10,11... | collective-permute-start | bytes 1572872 | tf_op jit(solution)/shard_map/ppermute | solution.py:16
  37.5 15.9 %collective-permute-start.10 = (bf16[8,64,512]{2,1,0:T(8,128)(2,1)}, bf16[8,64,512]{2,1,0:T(8,128)(2,1)}, u32[]{:S(2)}, u32[]{:S(2)}) collective-permute-start(bf16[8,64,512]{2,1,0:T(8,128)(2,1)} %refs_0_.1), channel_id=1, source_target_pairs={{0,4},{1,5},{2,6},{3,7},{4,0},{5,1},{6,2},{7,3},{8,12},{9,13},{10,... | collective-permute-start | bytes 1572872 | tf_op jit(solution)/shard_map/ppermute | solution.py:16
  40.2 23.9 %collective-permute-start.16 = (bf16[8,64,512]{2,1,0:T(8,128)(2,1)S(1)}, bf16[8,64,512]{2,1,0:T(8,128)(2,1)S(1)}, u32[]{:S(2)}, u32[]{:S(2)}) collective-permute-start(bf16[8,64,512]{2,1,0:T(8,128)(2,1)S(1)} %get-tuple-element.39), channel_id=1, source_target_pairs={{0,4},{1,5},{2,6},{3,7},{4,0},{5,1},{6,2},{7,3},{8,12},{9,13},{10,... | collective-permute-start | bytes 1572872 | tf_op jit(solution)/shard_map/ppermute | solution.py:16
  40.3 16.2 %collective-permute-start.7 = (bf16[8,64,512]{2,1,0:T(8,128)(2,1)}, bf16[8,64,512]{2,1,0:T(8,128)(2,1)}, u32[]{:S(2)}, u32[]{:S(2)}) collective-permute-start(bf16[8,64,512]{2,1,0:T(8,128)(2,1)} %collective-permute-done.6.refs_2_), channel_id=1, source_target_pairs={{0,1},{1,0},{2,3},{3,2},{4,5},{5,4},{6,7},{7,6},{8,9},{9,8},{10,11... | collective-permute-start | bytes 1572872 | tf_op jit(solution)/shard_map/ppermute | solution.py:16
  49.7 22.1 %collective-permute-start.12 = (bf16[8,64,512]{2,1,0:T(8,128)(2,1)S(1)}, bf16[8,64,512]{2,1,0:T(8,128)(2,1)}, u32[]{:S(2)}, u32[]{:S(2)}) collective-permute-start(bf16[8,64,512]{2,1,0:T(8,128)(2,1)S(1)} %collective-permute-done.9.refs_2_.refs_7_), channel_id=1, source_target_pairs={{0,1},{3,2},{4,5},{7,6},{8,9},{11,10},{12,13},{15,14},{16,17},{19,... | collective-permute-start | bytes 1572872 | tf_op jit(solution)/shard_map/ppermute | solution.py:16
  53.2 23.0 %collective-permute-start.14 = (bf16[8,64,512]{2,1,0:T(8,128)(2,1)}, bf16[8,64,512]{2,1,0:T(8,128)(2,1)S(1)}, u32[]{:S(2)}, u32[]{:S(2)}) collective-permute-start(bf16[8,64,512]{2,1,0:T(8,128)(2,1)} %get-tuple-element.40), channel_id=1, source_target_pairs={{0,1},{1,0},{2,3},{3,2},{4,5},{5,4},{6,7},{7,6},{8,9},{9,8},{10,11... | collective-permute-start | bytes 1572872 | tf_op jit(solution)/shard_map/ppermute | solution.py:16
  53.3 18.5 %collective-permute-start.11 = (bf16[8,64,512]{2,1,0:T(8,128)(2,1)}, bf16[8,64,512]{2,1,0:T(8,128)(2,1)}, u32[]{:S(2)}, u32[]{:S(2)}) collective-permute-start(bf16[8,64,512]{2,1,0:T(8,128)(2,1)} %collective-permute-done.10.refs_0_), channel_id=1, source_target_pairs={{0,1},{2,3},{5,4},{7,6},{8,9},{10,11},{13,12},{15,14},{16,17},{18,... | collective-permute-start | bytes 1572872 | tf_op jit(solution)/shard_map/ppermute | solution.py:16
  56.5 19.7 %collective-permute-start.15 = (bf16[8,64,512]{2,1,0:T(8,128)(2,1)S(1)}, bf16[8,64,512]{2,1,0:T(8,128)(2,1)S(1)}, u32[]{:S(2)}, u32[]{:S(2)}) collective-permute-start(bf16[8,64,512]{2,1,0:T(8,128)(2,1)S(1)} %collective-permute-done.4.refs_3_), channel_id=1, source_target_pairs={{0,1},{1,0},{2,3},{3,2},{4,5},{5,4},{6,7},{7,6},{8,9},{9,8},{10,11... | collective-permute-start | bytes 1572872 | tf_op jit(solution)/shard_map/ppermute | solution.py:16
  64.2 12.1 %collective-permute-start.17 = (bf16[8,64,512]{2,1,0:T(8,128)(2,1)S(1)}, bf16[8,64,512]{2,1,0:T(8,128)(2,1)S(1)}, u32[]{:S(2)}, u32[]{:S(2)}) collective-permute-start(bf16[8,64,512]{2,1,0:T(8,128)(2,1)S(1)} %collective-permute-done.16.refs_5_), channel_id=1, source_target_pairs={{1,0},{3,2},{4,5},{6,7},{9,8},{11,10},{12,13},{14,15},{17,16},{19,... | collective-permute-start | bytes 1572872 | tf_op jit(solution)/shard_map/ppermute | solution.py:16
  76.2 19.9 %copy-start = (bf16[512,1024]{1,0:T(8,128)(2,1)S(1)}, bf16[512,1024]{1,0:T(8,128)(2,1)}, u32[]{:S(2)}) copy-start(bf16[512,1024]{1,0:T(8,128)(2,1)} %get-tuple-element.33.table_near) | copy-start | bytes 3145732
  76.2 19.9 %copy-start.1 = (bf16[512,1024]{1,0:T(8,128)(2,1)S(1)}, bf16[512,1024]{1,0:T(8,128)(2,1)}, u32[]{:S(2)}) copy-start(bf16[512,1024]{1,0:T(8,128)(2,1)} %get-tuple-element.32.table_own) | copy-start | bytes 3145732
  81.4 8.9 %collective-permute-start.22 = (bf16[4,64,512]{2,1,0:T(8,128)(2,1)S(1)}, bf16[4,64,512]{2,1,0:T(8,128)(2,1)S(1)}, u32[]{:S(2)}, u32[]{:S(2)}) collective-permute-start(bf16[4,64,512]{2,1,0:T(8,128)(2,1)S(1)} %get-tuple-element.36.own_ref), channel_id=1, source_target_pairs={{0,2},{1,3},{2,0},{3,1},{4,6},{5,7},{6,4},{7,5},{8,10},{9,11},{10,... | collective-permute-start | bytes 786440 | tf_op jit(solution)/shard_map/ppermute | solution.py:16
  82.4 13.5 %collective-permute-start.19 = (bf16[4,64,512]{2,1,0:T(8,128)(2,1)S(1)}, bf16[4,64,512]{2,1,0:T(8,128)(2,1)S(1)}, u32[]{:S(2)}, u32[]{:S(2)}) collective-permute-start(bf16[4,64,512]{2,1,0:T(8,128)(2,1)S(1)} %get-tuple-element.31.own_ref), channel_id=1, source_target_pairs={{0,2},{1,3},{2,0},{3,1},{4,6},{5,7},{6,4},{7,5},{8,10},{9,11},{10,... | collective-permute-start | bytes 786440 | tf_op jit(solution)/shard_map/ppermute | solution.py:16
  83.5 12.6 %collective-permute-start.21 = (bf16[4,64,512]{2,1,0:T(8,128)(2,1)S(1)}, bf16[4,64,512]{2,1,0:T(8,128)(2,1)S(1)}, u32[]{:S(2)}, u32[]{:S(2)}) collective-permute-start(bf16[4,64,512]{2,1,0:T(8,128)(2,1)S(1)} %get-tuple-element.36.own_ref), channel_id=1, source_target_pairs={{0,1},{1,0},{2,3},{3,2},{4,5},{5,4},{6,7},{7,6},{8,9},{9,8},{10,11... | collective-permute-start | bytes 786440 | tf_op jit(solution)/shard_map/ppermute | solution.py:16
  90.3 5.8 %collective-permute-start.23 = (bf16[4,64,512]{2,1,0:T(8,128)(2,1)S(1)}, bf16[4,64,512]{2,1,0:T(8,128)(2,1)S(1)}, u32[]{:S(2)}, u32[]{:S(2)}) collective-permute-start(bf16[4,64,512]{2,1,0:T(8,128)(2,1)S(1)} %collective-permute-done.22.x_ref), channel_id=1, source_target_pairs={{0,1},{1,0},{2,3},{3,2},{4,5},{5,4},{6,7},{7,6},{8,9},{9,8},{10,11... | collective-permute-start | bytes 786440 | tf_op jit(solution)/shard_map/ppermute | solution.py:16
  91.2 8.2 %collective-permute-start.18 = (bf16[4,64,512]{2,1,0:T(8,128)(2,1)S(1)}, bf16[4,64,512]{2,1,0:T(8,128)(2,1)S(1)}, u32[]{:S(2)}, u32[]{:S(2)}) collective-permute-start(bf16[4,64,512]{2,1,0:T(8,128)(2,1)S(1)} %get-tuple-element.31.own_ref), channel_id=1, source_target_pairs={{0,1},{1,0},{2,3},{3,2},{4,5},{5,4},{6,7},{7,6},{8,9},{9,8},{10,11... | collective-permute-start | bytes 786440 | tf_op jit(solution)/shard_map/ppermute | solution.py:16
  95.9 3.5 %collective-permute-start.20 = (bf16[4,64,512]{2,1,0:T(8,128)(2,1)S(1)}, bf16[4,64,512]{2,1,0:T(8,128)(2,1)S(1)}, u32[]{:S(2)}, u32[]{:S(2)}) collective-permute-start(bf16[4,64,512]{2,1,0:T(8,128)(2,1)S(1)} %collective-permute-done.19.x_ref), channel_id=1, source_target_pairs={{0,1},{1,0},{2,3},{3,2},{4,5},{5,4},{6,7},{7,6},{8,9},{9,8},{10,11... | collective-permute-start | bytes 786440 | tf_op jit(solution)/shard_map/ppermute | solution.py:16

commit v4 on v3

--- a/solution.py
+++ b/solution.py
@@ -68,11 +68,11 @@
             left_ref[row * 64:(row + 1) * 64, at] = dense[:, window * 512:(window + 1) * 512]
 
 
-def collect(store, items, dest, valid):
+def collect(store, items, firsts, dest, valid):
     for number, item in enumerate(items):
         @pl.when(dest(number) >= 0)
         def _():
-            store[dest(number)] = item[...]
+            store[dest(number), firsts[number]:firsts[number] + item.shape[0]] = item[...]
     for place in range(store.shape[0]):
         @pl.when(valid(place) == 0)
         def _():
@@ -128,9 +128,10 @@
 
 def own_kernel(meta_ref, dest_ref, *refs):
     items = refs[:4]
-    left_near_out, left_far_out, table_out, total_out = refs[4:8]
-    left_store, left, left_near, left_far, store, table, total, sems, out_sems = refs[8:]
+    left_near_out, left_far_0, left_far_1, table_out, total_out = refs[4:9]
+    left_store, left, left_near, left_far, store, table, total, sems, out_sems = refs[9:]
     row_count = left_store.shape[1]
+    half = left_far.shape[0] // 2
     copies = transfers([(items[n], left_store.at[dest_ref[4 + n]]) for n in range(4)], sems)
     zero_invalid(store, lambda p: dest_ref[8 + p])
     for copy in copies:
@@ -157,18 +158,20 @@
         def _():
             left_near[rows, :] = dense[:, 512:1024]
             left_far[rows, :512] = dense[:, 1536:2048]
-    outs = transfers([(left_near, left_near_out), (left_far, left_far_out)], out_sems)
+    outs = transfers([(left_near, left_near_out), (left_far.at[pl.ds(0, half)], left_far_0),
+                      (left_far.at[pl.ds(half, half)], left_far_1)], out_sems)
     windows(store, table, 1, lambda at: dest_ref[11 + at])
-    outs += transfers([(table, table_out)], out_sems.at[pl.ds(2, 1)])
+    outs += transfers([(table, table_out)], out_sems.at[pl.ds(3, 1)])
     product(left, table, total)
-    outs += transfers([(total, total_out)], out_sems.at[pl.ds(3, 1)])
+    outs += transfers([(total, total_out)], out_sems.at[pl.ds(4, 1)])
     for copy in outs:
         copy.wait()
 
 
 def near_kernel(meta_ref, dest_ref, left_in, before_in, *refs):
     items = refs[:4]
-    table_out, base_out, store, left, before, table, total, base, sems, in_sems, out_sems = refs[4:]
+    table_out, base_0, base_1, store, left, before, table, total, base, sems, in_sems, out_sems = refs[4:]
+    half = base.shape[0] // 2
     copies = collected(items, store, sems, lambda n: dest_ref[n])
     start_all(copies)
     ins = transfers([(left_in, left), (before_in, before)], in_sems)
@@ -181,29 +184,38 @@
     product(left, table, total, before)
     for row in range(base.shape[0]):
         base[row] = kept(total[row * 64:(row + 1) * 64, :], row, meta_ref[8 + row], 512)
-    outs += transfers([(base, base_out)], out_sems.at[pl.ds(1, 1)])
+    outs += transfers([(base.at[pl.ds(0, half)], base_0), (base.at[pl.ds(half, half)], base_1)], out_sems.at[pl.ds(1, 2)])
     for copy in outs:
         copy.wait()
 
 
 def far_kernel(meta_ref, dest_ref, left_ref, base_ref, *refs):
-    items = refs[:9]
-    table_ref, square_ref, low_a, low_b, store, total_ref = refs[9:]
+    items = refs[:11]
+    table_ref, square_ref, low_ref, store, total_ref = refs[11:]
     row_count = items[0].shape[0]
     half = row_count // 2
-    collect(store, items, lambda n: dest_ref[n], lambda p: dest_ref[9 + p])
+    firsts = (0,) * 7 + (half,) * 2 + (0,) * 2
+    collect(store, items, firsts, lambda n: dest_ref[n], lambda p: dest_ref[11 + p])
     for window in range(3):
         for row in range(row_count):
             blocks = [store[window * PIECES + piece, row] for piece in range(PIECES)]
             at = window * 512 + row * 64
-            table_ref[at:at + 64, :] = spread(blocks, 8 - row, 16, dest_ref[18 + window * 8 + row])
-
+            table_ref[at:at + 64, :] = spread(blocks, 8 - row, 16, dest_ref[20 + window * 8 + row])
+
+    squares(meta_ref, 0, left_ref, base_ref, table_ref, square_ref, low_ref, total_ref)
+
+
+def squares(meta_ref, part, left_ref, base_ref, table_ref, square_ref, low_ref, total_ref):
     product(left_ref, table_ref, total_ref)
-    for row in range(row_count):
-        picked = base_ref[row] + kept(total_ref[row * 64:(row + 1) * 64, :], row, meta_ref[8 + row], 512)
+    for row in range(square_ref.shape[0]):
+        whole = part * square_ref.shape[0] + row
+        picked = base_ref[row] + kept(total_ref[row * 64:(row + 1) * 64, :], whole, meta_ref[8 + whole], 512)
         square_ref[row] = picked
-        low_ref = low_a if row < half else low_b
-        low_ref[row % half] = picked.astype(low_ref.dtype)
+        low_ref[row] = picked.astype(low_ref.dtype)
+
+
+def second_kernel(meta_ref, left_ref, base_ref, table_ref, square_ref, low_ref, total_ref):
+    squares(meta_ref, 1, left_ref, base_ref, table_ref, square_ref, low_ref, total_ref)
 
 
 def cube_kernel(part, meta_ref, own_ref, core_ref, x_ref, far_ref, table_own, table_near, table_b, square_ref, *refs):
@@ -223,7 +235,7 @@
     for row in range(row_count):
         whole = first_row + row
         cube = kept(total_ref[row * 64:(row + 1) * 64, :], whole, meta_ref[8 + whole], 512)
-        result[row] = (3.0 * square_ref[whole] - 2.0 * cube).astype(result.dtype)
+        result[row] = (3.0 * square_ref[row] - 2.0 * cube).astype(result.dtype)
     copy = pltpu.make_async_copy(result, out_ref.at[pl.ds(first_row, row_count)], sem)
     copy.start()
     copy.wait()
@@ -272,13 +284,16 @@
     from_near, dd = lax.optimization_barrier((from_near, dd))
     dd_core = permuted(dd, route["core_dd"])
     bx = permuted(za, route["x"])
-    by_source = jnp.where(same, za, zb)
+    half_rows = row_count // 2
+    by_source = [jnp.where(same, za[first:first + half_rows], zb[first:first + half_rows]) for first in (0, half_rows)]
     z_source = jnp.where((group == 0) | (group == 3), za, zb)
-    by = permuted(by_source, route["y"])
+    by_0 = permuted(by_source[0], route["y"])
+    by_1 = permuted(by_source[1], route["y"])
     z_core = permuted(z_source, route["core"])
     from_far, from_before, from_after, bx = lax.optimization_barrier((from_far, from_before, from_after, bx))
     bx_core = permuted(bx, route["core"])
-    by_core = permuted(by, route["core_by"])
+    by_0_core = permuted(by_0, route["core_by"])
+    by_1_core = permuted(by_1, route["core_by"])
 
     place = {0: missing(col_index, 0), "near": missing(from_near, near), "far": missing(from_far, -near),
              -2: missing(from_before, -2), 2: missing(from_after, 2)}
@@ -323,7 +338,7 @@
         + valid_of(near),
         [threshold(near, "near")],
     )
-    far_items = (za, zb, z_core, bx, bx_core, by, by_core, dd, dd_core)
+    far_items = (za, zb, z_core, bx, bx_core, by_0, by_0_core, by_1, by_1_core, dd, dd_core)
     far_dest = dest_of(
         [
             (-2 * sign, group, yes),
@@ -333,6 +348,8 @@
             (2 * sign, group ^ 3, yes),
             (-near, group, yes),
             (-near, group ^ 1, yes),
+            (-near, group, yes),
+            (-near, group ^ 1, yes),
             (-near, group ^ 2, same),
             (-near, group ^ 3, same),
         ],
@@ -360,16 +377,17 @@
         return [pltpu.with_memory_space_constraint(value, pltpu.HBM) for value in values]
 
     dma = pltpu.SemaphoreType.DMA
-    left_near, left_far, table_own, total = pl.pallas_call(
+    left_near, left_far_0, left_far_1, table_own, total = pl.pallas_call(
         own_kernel,
         out_shape=(
             pltpu.HBM((rows, 512), bf16),
-            pltpu.HBM((rows, 1536), bf16),
+            pltpu.HBM((rows // 2, 1536), bf16),
+            pltpu.HBM((rows // 2, 1536), bf16),
             pltpu.HBM((512, columns), bf16),
             pltpu.HBM((rows, columns), f32),
         ),
         in_specs=[smem, smem] + [hbm] * 4,
-        out_specs=(hbm,) * 4,
+        out_specs=(hbm,) * 5,
         scratch_shapes=[
             pltpu.VMEM((ka_count,) + shards, bf16),
             pltpu.VMEM((rows, 512), bf16),
@@ -379,17 +397,21 @@
             pltpu.VMEM((512, columns), bf16),
             pltpu.VMEM((rows, columns), f32),
             dma((4,)),
-            dma((4,)),
+            dma((5,)),
         ],
         compiler_params=small,
         cost_estimate=cost(512),
     )(meta, own_table, *in_hbm(*own_items))
 
-    table_near, base = pl.pallas_call(
+    table_near, base_0, base_1 = pl.pallas_call(
         near_kernel,
-        out_shape=(pltpu.HBM((512, columns), bf16), pltpu.HBM(shards, f32)),
+        out_shape=(
+            pltpu.HBM((512, columns), bf16),
+            pltpu.HBM((row_count // 2, block, width), f32),
+            pltpu.HBM((row_count // 2, block, width), f32),
+        ),
         in_specs=[smem, smem] + [hbm] * 6,
-        out_specs=(hbm, hbm),
+        out_specs=(hbm, hbm, hbm),
         scratch_shapes=[
             pltpu.VMEM((PIECES,) + shards, bf16),
             pltpu.VMEM((rows, 512), bf16),
@@ -399,33 +421,34 @@
             pltpu.VMEM(shards, f32),
             dma((4,)),
             dma((2,)),
-            dma((2,)),
+            dma((3,)),
         ],
         compiler_params=small,
         cost_estimate=cost(512),
     )(meta, near_table, *in_hbm(left_near, total, *near_items))
 
     half_rows = row_count // 2
-    table_b, square, low_a, low_b = pl.pallas_call(
+    half_shape = (half_rows, block, width)
+    table_b, square_0, low_0 = pl.pallas_call(
         far_kernel,
-        out_shape=(
-            shape((1536, columns), bf16),
-            shape((row_count, block, width), f32),
-            shape((half_rows, block, width), bf16),
-            shape((half_rows, block, width), bf16),
-        ),
-        in_specs=[smem, smem] + [vmem] * 11,
-        out_specs=(vmem, vmem, vmem, vmem),
-        scratch_shapes=[
-            pltpu.VMEM((3 * PIECES, row_count, block, width), bf16),
-            pltpu.VMEM((rows, columns), f32),
-        ],
+        out_shape=(shape((1536, columns), bf16), shape(half_shape, f32), shape(half_shape, bf16)),
+        in_specs=[smem, smem] + [vmem] * 13,
+        out_specs=(vmem, vmem, vmem),
+        scratch_shapes=[pltpu.VMEM((3 * PIECES, row_count, block, width), bf16), pltpu.VMEM((rows // 2, columns), f32)],
         compiler_params=small,
         cost_estimate=cost(1536),
-    )(meta, far_table, *[pltpu.with_memory_space_constraint(v, pltpu.HBM) for v in (left_far, base, za, zb)],
-      *far_items[2:7], *[pltpu.with_memory_space_constraint(v, pltpu.HBM) for v in (dd, dd_core)])
-
-    lows = (low_a, low_b)
+    )(meta, far_table, *in_hbm(left_far_0, base_0, za, zb), *far_items[2:9], *in_hbm(dd, dd_core))
+    square_1, low_1 = pl.pallas_call(
+        second_kernel,
+        out_shape=(shape(half_shape, f32), shape(half_shape, bf16)),
+        in_specs=[smem] + [vmem] * 3,
+        out_specs=(vmem, vmem),
+        scratch_shapes=[pltpu.VMEM((rows // 2, columns), f32)],
+        compiler_params=small,
+        cost_estimate=cost(768),
+    )(meta, *in_hbm(left_far_1, base_1), table_b)
+
+    lows, square = (low_0, low_1), (square_0, square_1)
     by_x = [permuted(low, route["x"]) for low in lows]
     by_partner = [permuted(low, route["core"]) for low in lows]
     by_both = [permuted(low, route["core"]) for low in by_x]
@@ -447,7 +470,7 @@
             compiler_params=small,
             cost_estimate=cost(1280),
         )(meta, lows[part], by_partner[part], by_x[part], by_both[part],
-          table_own, table_near, table_b, square, *out),)
+          table_own, table_near, table_b, square[part], *out),)
     return out[0]
 
 

time: 103 us -> 98.6 us (0.957)
  waiting for transfers between devices: 44.2 us -> 35.4 us
  starting transfers between devices: 32.6 us -> 35.9 us
  Pallas kernels: 22.3 us -> 23.5 us
    ppermute x20 -> x22, waiting for transfers between devices: 42.6 us -> 30.2 us  [permuted(): return lax.ppermute(value, ('dom', 'ka'), pairs)]
    ppermute x20 -> x22, starting transfers between devices: 24.6 us -> 29.3 us  [permuted(): return lax.ppermute(value, ('dom', 'ka'), pairs)]
    ppermute x4, waiting for transfers between devices: 1.62 us -> 5.2 us  [along(): lax.ppermute(value, 'dom', [(source(d) % dom_count, d) for d in range(dom...]
    pallas_call x0 -> x1, Pallas kernels: none -> 2.42 us  [per_device(): pl.pallas_call(second_kernel, out_shape=(shape(half_shape, f32), shape(ha...]
    ppermute x4, starting transfers between devices: 8.01 us -> 6.6 us  [along(): lax.ppermute(value, 'dom', [(source(d) % dom_count, d) for d in range(dom...]
    pallas_call x1, Pallas kernels: 5.15 us -> 3.88 us  [per_device(): pl.pallas_call(far_kernel, out_shape=(shape((1536, columns), bf16), shape...]
  transfers between devices with their start and end apart: 24 -> 26, of which waited for: 7 -> 7; matrix products, arithmetic and copies ran while one was open for 3% -> 3% of each run, Pallas kernels for 13% -> 16%
where the time goes in v4:
time: 98.6 us; the launch traced here: 98.3 us
  starting transfers between devices  35.9 us (36%)
  waiting for transfers between devices  35.4 us (36%)
  Pallas kernels  23.5 us (24%)
  other arithmetic  2.61 us (3%)
    ppermute x22, waiting for transfers between devices, permuted(): return lax.ppermute(value, ('dom', 'ka'), pairs)  30.2 us
    ppermute x22, starting transfers between devices, permuted(): return lax.ppermute(value, ('dom', 'ka'), pairs)  29.3 us
    pallas_call x2, Pallas kernels, per_device(): pl.pallas_call(functools.partial(cube_kernel, part), out_shape=pltpu.HBM(...  6.68 us
    ppermute x4, starting transfers between devices, along(): lax.ppermute(value, 'dom', [(source(d) % dom_count, d) for d in range(dom...  6.6 us
    pallas_call x1, Pallas kernels, per_device(): pl.pallas_call(own_kernel, out_shape=(pltpu.HBM((rows, 512), bf16), pltpu...  6.13 us
    ppermute x4, waiting for transfers between devices, along(): lax.ppermute(value, 'dom', [(source(d) % dom_count, d) for d in range(dom...  5.2 us
    pallas_call x1, Pallas kernels, per_device(): pl.pallas_call(near_kernel, out_shape=(pltpu.HBM((512, columns), bf16), p...  4.36 us
    pallas_call x1, Pallas kernels, per_device(): pl.pallas_call(far_kernel, out_shape=(shape((1536, columns), bf16), shape...  3.88 us
  transfers between devices with their start and end apart: 26, of which 7 were waited for; matrix products, arithmetic and copies ran while one was open for 3% of the time, Pallas kernels for 16%

profile of v4, /device:TPU:0, one launch (start us, length us, event | category | flops | bytes accessed | tf_op | source)
XLA Modules:
  0.0 98.3 jit_solution(9152420708685578137)
XLA Ops:
  0.0 6.0 %collective-permute-start.8 = (s32[8,32]{1,0:T(8,128)}, s32[8,32]{1,0:T(8,128)S(1)}, u32[]{:S(2)}, u32[]{:S(2)}) collective-permute-start(s32[8,32]{1,0:T(8,128)} %param.4), channel_id=1, source_target_pairs={{28,0},{8,4},{4,8},{16,12},{12,16},{24,20},{20,24},{0,28},{29,1},{... | collective-permute-start | bytes 3080 | tf_op jit(solution)/shard_map/ppermute | solution.py:269
  6.0 2.8 %collective-permute-start.4 = (bf16[8,64,512]{2,1,0:T(8,128)(2,1)}, bf16[8,64,512]{2,1,0:T(8,128)(2,1)}, u32[]{:S(2)}, u32[]{:S(2)}) collective-permute-start(bf16[8,64,512]{2,1,0:T(8,128)(2,1)} %refs_0_.1), channel_id=1, source_target_pairs={{0,30},{1,31},{2,4},{3,5},{4,2},{5,3},{6,8},{7,9},{8,6},{9,7},{10,... | collective-permute-start | bytes 1572872 | tf_op jit(solution)/shard_map/ppermute | solution.py:16
  8.9 0.7 collective-permute-start.13
  9.6 0.5 collective-permute-start.11
  10.3 0.9 convert_reduce_fusion.4
  11.4 0.5 collective-permute-start.10
  11.9 12.9 %collective-permute-done.4.refs_2_.refs_9_ = bf16[8,64,512]{2,1,0:T(8,128)(2,1)} collective-permute-done((bf16[8,64,512]{2,1,0:T(8,128)(2,1)}, bf16[8,64,512]{2,1,0:T(8,128)(2,1)}, u32[]{:S(2)}, u32[]{:S(2)}) %collective-permute-start.4) | collective-permute-done | bytes 524320 | tf_op jit(solution)/shard_map/ppermute | solution.py:16
  24.9 10.9 %collective-permute-start.1 = (bf16[8,64,512]{2,1,0:T(8,128)(2,1)}, bf16[8,64,512]{2,1,0:T(8,128)(2,1)}, u32[]{:S(2)}, u32[]{:S(2)}) collective-permute-start(bf16[8,64,512]{2,1,0:T(8,128)(2,1)} %refs_0_.1), channel_id=1, source_target_pairs={{0,2},{1,3},{2,0},{3,1},{4,6},{5,7},{6,4},{7,5},{8,10},{9,11},{10,... | collective-permute-start | bytes 1572872 | tf_op jit(solution)/shard_map/ppermute | solution.py:16
  35.7 2.9 %collective-permute-done.11.refs_0_ = bf16[8,64,512]{2,1,0:T(8,128)(2,1)S(1)} collective-permute-done((bf16[8,64,512]{2,1,0:T(8,128)(2,1)}, bf16[8,64,512]{2,1,0:T(8,128)(2,1)S(1)}, u32[]{:S(2)}, u32[]{:S(2)}) %collective-permute-start.11) | collective-permute-done | bytes 524320 | tf_op jit(solution)/shard_map/ppermute | solution.py:16
  38.6 1.0 broadcast_select_fusion
  40.1 5.2 %collective-permute-done.9 = s32[8,32]{1,0:T(8,128)S(1)} collective-permute-done((s32[8,32]{1,0:T(8,128)S(1)}, s32[8,32]{1,0:T(8,128)S(1)}, u32[]{:S(2)}, u32[]{:S(2)}) %collective-permute-start.9) | collective-permute-done | bytes 1056 | tf_op jit(solution)/shard_map/ppermute | solution.py:269
  45.3 2.6 %collective-permute-start.18 = (bf16[4,64,512]{2,1,0:T(8,128)(2,1)S(1)}, bf16[4,64,512]{2,1,0:T(8,128)(2,1)S(1)}, u32[]{:S(2)}, u32[]{:S(2)}) collective-permute-start(bf16[4,64,512]{2,1,0:T(8,128)(2,1)S(1)} %get-tuple-element.45), channel_id=1, source_target_pairs={{0,4},{1,5},{2,6},{3,7},{4,0},{5,1},{6,2},{7,3},{8,12},{9,13},{10,... | collective-permute-start | bytes 786440 | tf_op jit(solution)/shard_map/ppermute | solution.py:16
  47.9 0.6 collective-permute-done.1.refs_2_
  48.5 1.3 %collective-permute-start.6 = (bf16[8,64,512]{2,1,0:T(8,128)(2,1)}, bf16[8,64,512]{2,1,0:T(8,128)(2,1)S(1)}, u32[]{:S(2)}, u32[]{:S(2)}) collective-permute-start(bf16[8,64,512]{2,1,0:T(8,128)(2,1)} %collective-permute-done.5.refs_0_), channel_id=1, source_target_pairs={{0,1},{2,3},{5,4},{7,6},{8,9},{10,11},{13,12},{15,14},{16,17},{18,... | collective-permute-start | bytes 1572872 | tf_op jit(solution)/shard_map/ppermute | solution.py:16
  49.9 5.4 %collective-permute-done.12.refs_3_ = bf16[8,64,512]{2,1,0:T(8,128)(2,1)S(1)} collective-permute-done((bf16[8,64,512]{2,1,0:T(8,128)(2,1)S(1)}, bf16[8,64,512]{2,1,0:T(8,128)(2,1)S(1)}, u32[]{:S(2)}, u32[]{:S(2)}) %collective-permute-start.12) | collective-permute-done | bytes 524320 | tf_op jit(solution)/shard_map/ppermute | solution.py:16
  55.3 0.2 convert_reduce_fusion
  55.7 3.3 %collective-permute-start.7 = (bf16[8,64,512]{2,1,0:T(8,128)(2,1)}, bf16[8,64,512]{2,1,0:T(8,128)(2,1)}, u32[]{:S(2)}, u32[]{:S(2)}) collective-permute-start(bf16[8,64,512]{2,1,0:T(8,128)(2,1)} %collective-permute-done.4.refs_2_.refs_9_), channel_id=1, source_target_pairs={{0,1},{3,2},{4,5},{7,6},{8,9},{11,10},{12,13},{15,14},{16,17},{19,... | collective-permute-start | bytes 1572872 | tf_op jit(solution)/shard_map/ppermute | solution.py:16
  59.0 0.5 collective-permute-start.15
  59.5 1.3 %collective-permute-start.19 = (bf16[4,64,512]{2,1,0:T(8,128)(2,1)S(1)}, bf16[4,64,512]{2,1,0:T(8,128)(2,1)S(1)}, u32[]{:S(2)}, u32[]{:S(2)}) collective-permute-start(bf16[4,64,512]{2,1,0:T(8,128)(2,1)S(1)} %collective-permute-done.18.refs_7_), channel_id=1, source_target_pairs={{1,0},{3,2},{4,5},{6,7},{9,8},{11,10},{12,13},{14,15},{17,16},{19,... | collective-permute-start | bytes 786440 | tf_op jit(solution)/shard_map/ppermute | solution.py:16
  60.8 1.3 %collective-permute-start.17 = (bf16[4,64,512]{2,1,0:T(8,128)(2,1)S(1)}, bf16[4,64,512]{2,1,0:T(8,128)(2,1)S(1)}, u32[]{:S(2)}, u32[]{:S(2)}) collective-permute-start(bf16[4,64,512]{2,1,0:T(8,128)(2,1)S(1)} %collective-permute-done.16.refs_5_), channel_id=1, source_target_pairs={{1,0},{3,2},{4,5},{6,7},{9,8},{11,10},{12,13},{14,15},{17,16},{19,... | collective-permute-start | bytes 786440 | tf_op jit(solution)/shard_map/ppermute | solution.py:16
  62.3 6.1 %shard_map.37 = (bf16[512,512]{1,0:T(8,128)(2,1)}, bf16[256,1536]{1,0:T(8,128)(2,1)}, bf16[256,1536]{1,0:T(8,128)(2,1)}, bf16[512,1024]{1,0:T(8,128)(2,1)}, f32[512,1024]{1,0:T(8,128)}) custom-call(s32[31]{0:T(128)S(1)} %concatenate.12.meta_ref, s32[19]{0:T(128)S(1)} %concatenate.13.dest_ref, bf16[8,64,512]{2,1,0:T(8,128)(2,1)} %refs_0_.1, ...), custom_call_target="tpu_custom_call" | custom-call | flops 1073741824 | bytes 12582912 | tf_op jit(solution)/shard_map/pallas_call | solution.py:380
  68.4 4.4 %shard_map.38 = (bf16[512,1024]{1,0:T(8,128)(2,1)}, f32[4,64,512]{2,1,0:T(8,128)}, f32[4,64,512]{2,1,0:T(8,128)}) custom-call(s32[31]{0:T(128)S(1)} %concatenate.12.meta_ref, s32[15]{0:T(128)S(1)} %concatenate.14.dest_ref, bf16[512,512]{1,0:T(8,128)(2,1)} %get-tuple-element.26.left_in, f32[512,1024]{1,0:T(8,128)} %get-tuple-element.27.before_in, ...), custom_call_target="tpu_custom_call" | custom-call | flops 1073741824 | bytes 12582912 | tf_op jit(solution)/shard_map/pallas_call | solution.py:406
  72.8 3.9 %shard_map.39 = (bf16[1536,1024]{1,0:T(8,128)(2,1)S(1)}, f32[4,64,512]{2,1,0:T(8,128)S(1)}, bf16[4,64,512]{2,1,0:T(8,128)(2,1)S(1)}) custom-call(s32[31]{0:T(128)S(1)} %concatenate.12.meta_ref, s32[44]{0:T(128)S(1)} %concatenate.15.dest_ref, bf16[256,1536]{1,0:T(8,128)(2,1)} %get-tuple-element.33.left_ref, f32[4,64,512]{2,1,0:T(8,128)} %get-tuple-element.34.base_ref, ...), custom_call_target="tpu_custom_call" | custom-call | flops 3221225472 | bytes 12582912 | tf_op jit(solution)/shard_map/pallas_call | solution.py:432
  76.7 1.3 %collective-permute-start.24 = (bf16[4,64,512]{2,1,0:T(8,128)(2,1)S(1)}, bf16[4,64,512]{2,1,0:T(8,128)(2,1)S(1)}, u32[]{:S(2)}, u32[]{:S(2)}) collective-permute-start(bf16[4,64,512]{2,1,0:T(8,128)(2,1)S(1)} %get-tuple-element.41.own_ref), channel_id=1, source_target_pairs={{0,2},{1,3},{2,0},{3,1},{4,6},{5,7},{6,4},{7,5},{8,10},{9,11},{10,... | collective-permute-start | bytes 786440 | tf_op jit(solution)/shard_map/ppermute | solution.py:16
  78.1 2.4 %shard_map.40 = (f32[4,64,512]{2,1,0:T(8,128)S(1)}, bf16[4,64,512]{2,1,0:T(8,128)(2,1)S(1)}) custom-call(s32[31]{0:T(128)S(1)} %concatenate.12.meta_ref, bf16[256,1536]{1,0:T(8,128)(2,1)} %get-tuple-element.24.left_ref, f32[4,64,512]{2,1,0:T(8,128)} %get-tuple-element.29.base_ref, bf16[1536,1024]{1,0:T(8,128)(2,1)S(1)} %get-tuple-element.36.table_ref.table_b), custom_call_target="tpu_custom_call" | custom-call | flops 1610612736 | bytes 12582912 | tf_op jit(solution)/shard_map/pallas_call | solution.py:441
  80.5 0.8 collective-permute-start.21
  81.3 0.8 collective-permute-start.23
  82.1 3.5 %collective-permute-done.24.x_ref = bf16[4,64,512]{2,1,0:T(8,128)(2,1)S(1)} collective-permute-done((bf16[4,64,512]{2,1,0:T(8,128)(2,1)S(1)}, bf16[4,64,512]{2,1,0:T(8,128)(2,1)S(1)}, u32[]{:S(2)}, u32[]{:S(2)}) %collective-permute-start.24) | collective-permute-done | bytes 262176 | tf_op jit(solution)/shard_map/ppermute | solution.py:16
  85.6 0.9 collective-permute-start.25
  86.5 4.8 %collective-permute-done.21.x_ref = bf16[4,64,512]{2,1,0:T(8,128)(2,1)S(1)} collective-permute-done((bf16[4,64,512]{2,1,0:T(8,128)(2,1)S(1)}, bf16[4,64,512]{2,1,0:T(8,128)(2,1)S(1)}, u32[]{:S(2)}, u32[]{:S(2)}) %collective-permute-start.21) | collective-permute-done | bytes 262176 | tf_op jit(solution)/shard_map/ppermute | solution.py:16
  91.5 3.3 %shard_map.41.refs_0_ = bf16[8,64,512]{2,1,0:T(8,128)(2,1)} custom-call(s32[31]{0:T(128)S(1)} %concatenate.12.meta_ref, bf16[4,64,512]{2,1,0:T(8,128)(2,1)S(1)} %get-tuple-element.41.own_ref, bf16[4,64,512]{2,1,0:T(8,128)(2,1)S(1)} %collective-permute-done.23.core_ref, bf16[4,64,512]{2,1,0:T(8,128)(2,1)S(1)} %collective-permute-done.24.x_ref, ...), custom_call_target="tpu_custom_call" | custom-call | flops 2684354560 | bytes 12582912 | tf_op jit(solution)/shard_map/pallas_call | solution.py:457
  94.8 3.4 %shard_map.42 = bf16[8,64,512]{2,1,0:T(8,128)(2,1)} custom-call(s32[31]{0:T(128)S(1)} %concatenate.12.meta_ref, bf16[4,64,512]{2,1,0:T(8,128)(2,1)S(1)} %get-tuple-element.37.own_ref, bf16[4,64,512]{2,1,0:T(8,128)(2,1)S(1)} %collective-permute-done.20.core_ref, ...), custom_call_target="tpu_custom_call", output_to_operand_aliasing={{}: (9, {})} | custom-call | flops 2684354560 | bytes 12582912 | tf_op jit(solution)/shard_map/pallas_call | solution.py:457
  (60 shorter events, 1.3 us)
Async XLA Ops:
  0.0 39.9 %copy-start.5 = (s32[8,32]{1,0:T(8,128)S(1)}, s32[8,32]{1,0:T(8,128)}, u32[]{:S(2)}) copy-start(s32[8,32]{1,0:T(8,128)} %param.4) | copy-start | bytes 3076
  0.0 39.9 %collective-permute-start.8 = (s32[8,32]{1,0:T(8,128)}, s32[8,32]{1,0:T(8,128)S(1)}, u32[]{:S(2)}, u32[]{:S(2)}) collective-permute-start(s32[8,32]{1,0:T(8,128)} %param.4), channel_id=1, source_target_pairs={{28,0},{8,4},{4,8},{16,12},{12,16},{24,20},{20,24},{0,28},{29,1},{... | collective-permute-start | bytes 3080 | tf_op jit(solution)/shard_map/ppermute | solution.py:269
  6.0 5.3 %collective-permute-start.3 = (s32[8,32]{1,0:T(8,128)}, s32[8,32]{1,0:T(8,128)S(1)}, u32[]{:S(2)}, u32[]{:S(2)}) collective-permute-start(s32[8,32]{1,0:T(8,128)} %param.4), channel_id=1, source_target_pairs={{4,0},{0,4},{12,8},{8,12},{20,16},{16,20},{28,24},{24,28},{5,1},{1... | collective-permute-start | bytes 3080 | tf_op jit(solution)/shard_map/ppermute | solution.py:269
  6.0 18.8 %collective-permute-start.4 = (bf16[8,64,512]{2,1,0:T(8,128)(2,1)}, bf16[8,64,512]{2,1,0:T(8,128)(2,1)}, u32[]{:S(2)}, u32[]{:S(2)}) collective-permute-start(bf16[8,64,512]{2,1,0:T(8,128)(2,1)} %refs_0_.1), channel_id=1, source_target_pairs={{0,30},{1,31},{2,4},{3,5},{4,2},{5,3},{6,8},{7,9},{8,6},{9,7},{10,... | collective-permute-start | bytes 1572872 | tf_op jit(solution)/shard_map/ppermute | solution.py:16
  8.9 16.0 %collective-permute-start.13 = (bf16[8,64,512]{2,1,0:T(8,128)(2,1)}, bf16[8,64,512]{2,1,0:T(8,128)(2,1)S(1)}, u32[]{:S(2)}, u32[]{:S(2)}) collective-permute-start(bf16[8,64,512]{2,1,0:T(8,128)(2,1)} %refs_0_.1), channel_id=1, source_target_pairs={{1,9},{2,26},{3,27},{4,12},{5,13},{6,30},{9,17},{10,2},{11,3},{12,... | collective-permute-start | bytes 1572872 | tf_op jit(solution)/shard_map/ppermute | solution.py:16
  9.6 29.1 %collective-permute-start.11 = (bf16[8,64,512]{2,1,0:T(8,128)(2,1)}, bf16[8,64,512]{2,1,0:T(8,128)(2,1)S(1)}, u32[]{:S(2)}, u32[]{:S(2)}) collective-permute-start(bf16[8,64,512]{2,1,0:T(8,128)(2,1)} %refs_0_.1), channel_id=1, source_target_pairs={{0,24},{1,25},{2,10},{3,11},{4,28},{5,29},{6,14},{7,15},{8,0},{9,1... | collective-permute-start | bytes 1572872 | tf_op jit(solution)/shard_map/ppermute | solution.py:16
  11.4 28.5 %collective-permute-start.10 = (s32[8,32]{1,0:T(8,128)}, s32[8,32]{1,0:T(8,128)S(1)}, u32[]{:S(2)}, u32[]{:S(2)}) collective-permute-start(s32[8,32]{1,0:T(8,128)} %param.4), channel_id=1, source_target_pairs={{8,0},{12,4},{16,8},{20,12},{24,16},{28,20},{0,24},{4,28},{9,1},{1... | collective-permute-start | bytes 3080 | tf_op jit(solution)/shard_map/ppermute | solution.py:269
  24.8 23.1 %collective-permute-start.5 = (bf16[8,64,512]{2,1,0:T(8,128)(2,1)}, bf16[8,64,512]{2,1,0:T(8,128)(2,1)}, u32[]{:S(2)}, u32[]{:S(2)}) collective-permute-start(bf16[8,64,512]{2,1,0:T(8,128)(2,1)} %refs_0_.1), channel_id=1, source_target_pairs={{0,4},{1,5},{2,6},{3,7},{4,0},{5,1},{6,2},{7,3},{8,12},{9,13},{10,... | collective-permute-start | bytes 1572872 | tf_op jit(solution)/shard_map/ppermute | solution.py:16
  24.9 43.6 %copy-start.2 = (bf16[8,64,512]{2,1,0:T(8,128)(2,1)}, bf16[8,64,512]{2,1,0:T(8,128)(2,1)S(1)}, u32[]{:S(2)}) copy-start(bf16[8,64,512]{2,1,0:T(8,128)(2,1)S(1)} %collective-permute-done.13.refs_1_) | copy-start | bytes 1572868
  24.9 23.7 %collective-permute-start.1 = (bf16[8,64,512]{2,1,0:T(8,128)(2,1)}, bf16[8,64,512]{2,1,0:T(8,128)(2,1)}, u32[]{:S(2)}, u32[]{:S(2)}) collective-permute-start(bf16[8,64,512]{2,1,0:T(8,128)(2,1)} %refs_0_.1), channel_id=1, source_target_pairs={{0,2},{1,3},{2,0},{3,1},{4,6},{5,7},{6,4},{7,5},{8,10},{9,11},{10,... | collective-permute-start | bytes 1572872 | tf_op jit(solution)/shard_map/ppermute | solution.py:16
  38.6 20.9 %copy-start.3 = (bf16[8,64,512]{2,1,0:T(8,128)(2,1)}, bf16[8,64,512]{2,1,0:T(8,128)(2,1)S(1)}, u32[]{:S(2)}) copy-start(bf16[8,64,512]{2,1,0:T(8,128)(2,1)S(1)} %collective-permute-done.11.refs_0_) | copy-start | bytes 1572868
  38.6 16.6 %collective-permute-start.12 = (bf16[8,64,512]{2,1,0:T(8,128)(2,1)S(1)}, bf16[8,64,512]{2,1,0:T(8,128)(2,1)S(1)}, u32[]{:S(2)}, u32[]{:S(2)}) collective-permute-start(bf16[8,64,512]{2,1,0:T(8,128)(2,1)S(1)} %collective-permute-done.11.refs_0_), channel_id=1, source_target_pairs={{0,2},{1,3},{2,0},{3,1},{4,6},{5,7},{6,4},{7,5},{8,10},{9,11},{10,... | collective-permute-start | bytes 1572872 | tf_op jit(solution)/shard_map/ppermute | solution.py:16
  39.9 5.5 %collective-permute-start.9 = (s32[8,32]{1,0:T(8,128)S(1)}, s32[8,32]{1,0:T(8,128)S(1)}, u32[]{:S(2)}, u32[]{:S(2)}) collective-permute-start(s32[8,32]{1,0:T(8,128)S(1)} %copy-done.5), channel_id=1, source_target_pairs={{24,0},{28,4},{0,8},{4,12},{8,16},{12,20},{16,24},{20,28},{25,1},{... | collective-permute-start | bytes 3080 | tf_op jit(solution)/shard_map/ppermute | solution.py:269
  39.9 15.7 %collective-permute-start = (bf16[8,64,512]{2,1,0:T(8,128)(2,1)}, bf16[8,64,512]{2,1,0:T(8,128)(2,1)}, u32[]{:S(2)}, u32[]{:S(2)}) collective-permute-start(bf16[8,64,512]{2,1,0:T(8,128)(2,1)} %refs_0_.1), channel_id=1, source_target_pairs={{0,1},{1,0},{2,3},{3,2},{4,5},{5,4},{6,7},{7,6},{8,9},{9,8},{10,11... | collective-permute-start | bytes 1572872 | tf_op jit(solution)/shard_map/ppermute | solution.py:16
  45.3 13.6 %collective-permute-start.18 = (bf16[4,64,512]{2,1,0:T(8,128)(2,1)S(1)}, bf16[4,64,512]{2,1,0:T(8,128)(2,1)S(1)}, u32[]{:S(2)}, u32[]{:S(2)}) collective-permute-start(bf16[4,64,512]{2,1,0:T(8,128)(2,1)S(1)} %get-tuple-element.45), channel_id=1, source_target_pairs={{0,4},{1,5},{2,6},{3,7},{4,0},{5,1},{6,2},{7,3},{8,12},{9,13},{10,... | collective-permute-start | bytes 786440 | tf_op jit(solution)/shard_map/ppermute | solution.py:16
  47.9 11.1 %collective-permute-start.16 = (bf16[4,64,512]{2,1,0:T(8,128)(2,1)S(1)}, bf16[4,64,512]{2,1,0:T(8,128)(2,1)S(1)}, u32[]{:S(2)}, u32[]{:S(2)}) collective-permute-start(bf16[4,64,512]{2,1,0:T(8,128)(2,1)S(1)} %get-tuple-element.46), channel_id=1, source_target_pairs={{0,4},{1,5},{2,6},{3,7},{4,0},{5,1},{6,2},{7,3},{8,12},{9,13},{10,... | collective-permute-start | bytes 786440 | tf_op jit(solution)/shard_map/ppermute | solution.py:16
  48.5 11.0 %collective-permute-start.6 = (bf16[8,64,512]{2,1,0:T(8,128)(2,1)}, bf16[8,64,512]{2,1,0:T(8,128)(2,1)S(1)}, u32[]{:S(2)}, u32[]{:S(2)}) collective-permute-start(bf16[8,64,512]{2,1,0:T(8,128)(2,1)} %collective-permute-done.5.refs_0_), channel_id=1, source_target_pairs={{0,1},{2,3},{5,4},{7,6},{8,9},{10,11},{13,12},{15,14},{16,17},{18,... | collective-permute-start | bytes 1572872 | tf_op jit(solution)/shard_map/ppermute | solution.py:16
  55.3 5.6 %collective-permute-start.2 = (bf16[8,64,512]{2,1,0:T(8,128)(2,1)}, bf16[8,64,512]{2,1,0:T(8,128)(2,1)S(1)}, u32[]{:S(2)}, u32[]{:S(2)}) collective-permute-start(bf16[8,64,512]{2,1,0:T(8,128)(2,1)} %collective-permute-done.1.refs_2_), channel_id=1, source_target_pairs={{0,1},{1,0},{2,3},{3,2},{4,5},{5,4},{6,7},{7,6},{8,9},{9,8},{10,11... | collective-permute-start | bytes 1572872 | tf_op jit(solution)/shard_map/ppermute | solution.py:16
  55.7 12.7 %collective-permute-start.7 = (bf16[8,64,512]{2,1,0:T(8,128)(2,1)}, bf16[8,64,512]{2,1,0:T(8,128)(2,1)}, u32[]{:S(2)}, u32[]{:S(2)}) collective-permute-start(bf16[8,64,512]{2,1,0:T(8,128)(2,1)} %collective-permute-done.4.refs_2_.refs_9_), channel_id=1, source_target_pairs={{0,1},{3,2},{4,5},{7,6},{8,9},{11,10},{12,13},{15,14},{16,17},{19,... | collective-permute-start | bytes 1572872 | tf_op jit(solution)/shard_map/ppermute | solution.py:16
  59.0 13.8 %collective-permute-start.14 = (bf16[8,64,512]{2,1,0:T(8,128)(2,1)}, bf16[8,64,512]{2,1,0:T(8,128)(2,1)S(1)}, u32[]{:S(2)}, u32[]{:S(2)}) collective-permute-start(bf16[8,64,512]{2,1,0:T(8,128)(2,1)} %broadcast_select_fusion), channel_id=1, source_target_pairs={{0,1},{1,0},{2,3},{3,2},{4,5},{5,4},{6,7},{7,6},{8,9},{9,8},{10,11... | collective-permute-start | bytes 1572872 | tf_op jit(solution)/shard_map/ppermute | solution.py:16
  59.0 13.8 %collective-permute-start.15 = (bf16[8,64,512]{2,1,0:T(8,128)(2,1)S(1)}, bf16[8,64,512]{2,1,0:T(8,128)(2,1)S(1)}, u32[]{:S(2)}, u32[]{:S(2)}) collective-permute-start(bf16[8,64,512]{2,1,0:T(8,128)(2,1)S(1)} %collective-permute-done.12.refs_3_), channel_id=1, source_target_pairs={{0,1},{1,0},{2,3},{3,2},{4,5},{5,4},{6,7},{7,6},{8,9},{9,8},{10,11... | collective-permute-start | bytes 1572872 | tf_op jit(solution)/shard_map/ppermute | solution.py:16
  59.5 2.6 %copy-start.4 = (bf16[8,64,512]{2,1,0:T(8,128)(2,1)}, bf16[8,64,512]{2,1,0:T(8,128)(2,1)S(1)}, u32[]{:S(2)}) copy-start(bf16[8,64,512]{2,1,0:T(8,128)(2,1)S(1)} %collective-permute-done.6.refs_1_) | copy-start | bytes 1572868
  59.5 13.3 %collective-permute-start.19 = (bf16[4,64,512]{2,1,0:T(8,128)(2,1)S(1)}, bf16[4,64,512]{2,1,0:T(8,128)(2,1)S(1)}, u32[]{:S(2)}, u32[]{:S(2)}) collective-permute-start(bf16[4,64,512]{2,1,0:T(8,128)(2,1)S(1)} %collective-permute-done.18.refs_7_), channel_id=1, source_target_pairs={{1,0},{3,2},{4,5},{6,7},{9,8},{11,10},{12,13},{14,15},{17,16},{19,... | collective-permute-start | bytes 786440 | tf_op jit(solution)/shard_map/ppermute | solution.py:16
  60.8 12.0 %collective-permute-start.17 = (bf16[4,64,512]{2,1,0:T(8,128)(2,1)S(1)}, bf16[4,64,512]{2,1,0:T(8,128)(2,1)S(1)}, u32[]{:S(2)}, u32[]{:S(2)}) collective-permute-start(bf16[4,64,512]{2,1,0:T(8,128)(2,1)S(1)} %collective-permute-done.16.refs_5_), channel_id=1, source_target_pairs={{1,0},{3,2},{4,5},{6,7},{9,8},{11,10},{12,13},{14,15},{17,16},{19,... | collective-permute-start | bytes 786440 | tf_op jit(solution)/shard_map/ppermute | solution.py:16
  76.7 14.7 %copy-start = (bf16[512,1024]{1,0:T(8,128)(2,1)S(1)}, bf16[512,1024]{1,0:T(8,128)(2,1)}, u32[]{:S(2)}) copy-start(bf16[512,1024]{1,0:T(8,128)(2,1)} %get-tuple-element.39.table_near) | copy-start | bytes 3145732
  76.7 14.7 %copy-start.1 = (bf16[512,1024]{1,0:T(8,128)(2,1)S(1)}, bf16[512,1024]{1,0:T(8,128)(2,1)}, u32[]{:S(2)}) copy-start(bf16[512,1024]{1,0:T(8,128)(2,1)} %get-tuple-element.38.table_own) | copy-start | bytes 3145732
  76.7 8.9 %collective-permute-start.24 = (bf16[4,64,512]{2,1,0:T(8,128)(2,1)S(1)}, bf16[4,64,512]{2,1,0:T(8,128)(2,1)S(1)}, u32[]{:S(2)}, u32[]{:S(2)}) collective-permute-start(bf16[4,64,512]{2,1,0:T(8,128)(2,1)S(1)} %get-tuple-element.41.own_ref), channel_id=1, source_target_pairs={{0,2},{1,3},{2,0},{3,1},{4,6},{5,7},{6,4},{7,5},{8,10},{9,11},{10,... | collective-permute-start | bytes 786440 | tf_op jit(solution)/shard_map/ppermute | solution.py:16
  80.5 10.7 %collective-permute-start.21 = (bf16[4,64,512]{2,1,0:T(8,128)(2,1)S(1)}, bf16[4,64,512]{2,1,0:T(8,128)(2,1)S(1)}, u32[]{:S(2)}, u32[]{:S(2)}) collective-permute-start(bf16[4,64,512]{2,1,0:T(8,128)(2,1)S(1)} %get-tuple-element.37.own_ref), channel_id=1, source_target_pairs={{0,2},{1,3},{2,0},{3,1},{4,6},{5,7},{6,4},{7,5},{8,10},{9,11},{10,... | collective-permute-start | bytes 786440 | tf_op jit(solution)/shard_map/ppermute | solution.py:16
  81.3 10.1 %collective-permute-start.23 = (bf16[4,64,512]{2,1,0:T(8,128)(2,1)S(1)}, bf16[4,64,512]{2,1,0:T(8,128)(2,1)S(1)}, u32[]{:S(2)}, u32[]{:S(2)}) collective-permute-start(bf16[4,64,512]{2,1,0:T(8,128)(2,1)S(1)} %get-tuple-element.41.own_ref), channel_id=1, source_target_pairs={{0,1},{1,0},{2,3},{3,2},{4,5},{5,4},{6,7},{7,6},{8,9},{9,8},{10,11... | collective-permute-start | bytes 786440 | tf_op jit(solution)/shard_map/ppermute | solution.py:16
  85.6 5.8 %collective-permute-start.25 = (bf16[4,64,512]{2,1,0:T(8,128)(2,1)S(1)}, bf16[4,64,512]{2,1,0:T(8,128)(2,1)S(1)}, u32[]{:S(2)}, u32[]{:S(2)}) collective-permute-start(bf16[4,64,512]{2,1,0:T(8,128)(2,1)S(1)} %collective-permute-done.24.x_ref), channel_id=1, source_target_pairs={{0,1},{1,0},{2,3},{3,2},{4,5},{5,4},{6,7},{7,6},{8,9},{9,8},{10,11... | collective-permute-start | bytes 786440 | tf_op jit(solution)/shard_map/ppermute | solution.py:16
  86.5 8.3 %collective-permute-start.20 = (bf16[4,64,512]{2,1,0:T(8,128)(2,1)S(1)}, bf16[4,64,512]{2,1,0:T(8,128)(2,1)S(1)}, u32[]{:S(2)}, u32[]{:S(2)}) collective-permute-start(bf16[4,64,512]{2,1,0:T(8,128)(2,1)S(1)} %get-tuple-element.37.own_ref), channel_id=1, source_target_pairs={{0,1},{1,0},{2,3},{3,2},{4,5},{5,4},{6,7},{7,6},{8,9},{9,8},{10,11... | collective-permute-start | bytes 786440 | tf_op jit(solution)/shard_map/ppermute | solution.py:16
  91.2 3.5 %collective-permute-start.22 = (bf16[4,64,512]{2,1,0:T(8,128)(2,1)S(1)}, bf16[4,64,512]{2,1,0:T(8,128)(2,1)S(1)}, u32[]{:S(2)}, u32[]{:S(2)}) collective-permute-start(bf16[4,64,512]{2,1,0:T(8,128)(2,1)S(1)} %collective-permute-done.21.x_ref), channel_id=1, source_target_pairs={{0,1},{1,0},{2,3},{3,2},{4,5},{5,4},{6,7},{7,6},{8,9},{9,8},{10,11... | collective-permute-start | bytes 786440 | tf_op jit(solution)/shard_map/ppermute | solution.py:16
  (1 other events, 1.3 us)

commit v5 on v4

--- a/solution.py
+++ b/solution.py
@@ -191,11 +191,15 @@
 
 def far_kernel(meta_ref, dest_ref, left_ref, base_ref, *refs):
     items = refs[:11]
-    table_ref, square_ref, low_ref, store, total_ref = refs[11:]
+    table_ref, square_ref, low_ref, store, total_ref, sems = refs[11:]
     row_count = items[0].shape[0]
     half = row_count // 2
-    firsts = (0,) * 7 + (half,) * 2 + (0,) * 2
-    collect(store, items, firsts, lambda n: dest_ref[n], lambda p: dest_ref[11 + p])
+    early = (0, 1, 9, 10)
+    copies = collected([items[n] for n in early], store, sems, lambda n: dest_ref[early[n]])
+    start_all(copies)
+    firsts = (0,) * 5 + (half,) * 2
+    collect(store, items[2:9], firsts, lambda n: dest_ref[2 + n], lambda p: dest_ref[11 + p])
+    wait_all(copies)
     for window in range(3):
         for row in range(row_count):
             blocks = [store[window * PIECES + piece, row] for piece in range(PIECES)]
@@ -323,7 +327,6 @@
     ).astype(jnp.int32)
 
     yes = jnp.bool_(True)
-    own_items = (own, own_core, ox, ox_core)
     own_table = table_of(
         dest_of([(0, group ^ bits, yes) for bits in range(4)], lambda delta: 0)
         + [group ^ bits for bits in range(4)] + valid_of(0),
@@ -368,7 +371,7 @@
     shape = jax.ShapeDtypeStruct
     bf16, f32 = jnp.bfloat16, jnp.float32
 
-    small = pltpu.CompilerParams(vmem_limit_bytes=28 << 20)
+    small = pltpu.CompilerParams(vmem_limit_bytes=22 << 20)
 
     def cost(k):
         return pl.CostEstimate(flops=2 * rows * k * columns * 2, bytes_accessed=12 << 20, transcendentals=0)
@@ -401,7 +404,7 @@
         ],
         compiler_params=small,
         cost_estimate=cost(512),
-    )(meta, own_table, *in_hbm(*own_items))
+    )(meta, own_table, *in_hbm(own), own_core, *in_hbm(ox), ox_core)
 
     table_near, base_0, base_1 = pl.pallas_call(
         near_kernel,
@@ -432,9 +435,13 @@
     table_b, square_0, low_0 = pl.pallas_call(
         far_kernel,
         out_shape=(shape((1536, columns), bf16), shape(half_shape, f32), shape(half_shape, bf16)),
-        in_specs=[smem, smem] + [vmem] * 13,
+        in_specs=[smem, smem, vmem, vmem, hbm, hbm] + [vmem] * 7 + [hbm, hbm],
         out_specs=(vmem, vmem, vmem),
-        scratch_shapes=[pltpu.VMEM((3 * PIECES, row_count, block, width), bf16), pltpu.VMEM((rows // 2, columns), f32)],
+        scratch_shapes=[
+            pltpu.VMEM((3 * PIECES, row_count, block, width), bf16),
+            pltpu.VMEM((rows // 2, columns), f32),
+            dma((4,)),
+        ],
         compiler_params=small,
         cost_estimate=cost(1536),
     )(meta, far_table, *in_hbm(left_far_0, base_0, za, zb), *far_items[2:9], *in_hbm(dd, dd_core))

time: 98.6 us -> 98.4 us (level)
  waiting for transfers between devices: 35.4 us -> 32 us
  starting transfers between devices: 35.9 us -> 39.2 us
    ppermute x22, waiting for transfers between devices: 30.2 us -> 26.8 us  [permuted(): return lax.ppermute(value, ('dom', 'ka'), pairs)]
    ppermute x22, starting transfers between devices: 29.3 us -> 32.6 us  [permuted(): return lax.ppermute(value, ('dom', 'ka'), pairs)]
where the time goes in v5:
time: 98.4 us; the launch traced here: 98 us
  starting transfers between devices  39.2 us (40%)
  waiting for transfers between devices  32 us (33%)
  Pallas kernels  23.2 us (24%)
  other arithmetic  2.61 us (3%)
    ppermute x22, starting transfers between devices, permuted(): return lax.ppermute(value, ('dom', 'ka'), pairs)  32.6 us
    ppermute x22, waiting for transfers between devices, permuted(): return lax.ppermute(value, ('dom', 'ka'), pairs)  26.8 us
    pallas_call x2, Pallas kernels, per_device(): pl.pallas_call(functools.partial(cube_kernel, part), out_shape=pltpu.HBM(...  6.68 us
    ppermute x4, starting transfers between devices, along(): lax.ppermute(value, 'dom', [(source(d) % dom_count, d) for d in range(dom...  6.6 us
    pallas_call x1, Pallas kernels, per_device(): pl.pallas_call(own_kernel, out_shape=(pltpu.HBM((rows, 512), bf16), pltpu...  5.9 us
    ppermute x4, waiting for transfers between devices, along(): lax.ppermute(value, 'dom', [(source(d) % dom_count, d) for d in range(dom...  5.19 us
    pallas_call x1, Pallas kernels, per_device(): pl.pallas_call(near_kernel, out_shape=(pltpu.HBM((512, columns), bf16), p...  4.39 us
    pallas_call x1, Pallas kernels, per_device(): pl.pallas_call(far_kernel, out_shape=(shape((1536, columns), bf16), shape...  3.78 us
  transfers between devices with their start and end apart: 26, of which 7 were waited for; matrix products, arithmetic and copies ran while one was open for 3% of the time, Pallas kernels for 16%

profile of v5, /device:TPU:0, one launch (start us, length us, event | category | flops | bytes accessed | tf_op | source)
XLA Modules:
  0.0 98.0 jit_solution(10010913621633293574)
XLA Ops:
  0.0 6.0 %collective-permute-start.8 = (s32[8,32]{1,0:T(8,128)}, s32[8,32]{1,0:T(8,128)S(1)}, u32[]{:S(2)}, u32[]{:S(2)}) collective-permute-start(s32[8,32]{1,0:T(8,128)} %param.4), channel_id=1, source_target_pairs={{28,0},{8,4},{4,8},{16,12},{12,16},{24,20},{20,24},{0,28},{29,1},{... | collective-permute-start | bytes 3080 | tf_op jit(solution)/shard_map/ppermute | solution.py:273
  6.0 2.8 %collective-permute-start.4 = (bf16[8,64,512]{2,1,0:T(8,128)(2,1)}, bf16[8,64,512]{2,1,0:T(8,128)(2,1)}, u32[]{:S(2)}, u32[]{:S(2)}) collective-permute-start(bf16[8,64,512]{2,1,0:T(8,128)(2,1)} %refs_0_.1), channel_id=1, source_target_pairs={{0,30},{1,31},{2,4},{3,5},{4,2},{5,3},{6,8},{7,9},{8,6},{9,7},{10,... | collective-permute-start | bytes 1572872 | tf_op jit(solution)/shard_map/ppermute | solution.py:16
  8.9 0.7 collective-permute-start.13
  9.6 0.5 collective-permute-start.11
  10.3 0.9 convert_reduce_fusion.4
  11.4 0.5 collective-permute-start.10
  11.9 12.9 %collective-permute-done.4.refs_2_.refs_9_ = bf16[8,64,512]{2,1,0:T(8,128)(2,1)} collective-permute-done((bf16[8,64,512]{2,1,0:T(8,128)(2,1)}, bf16[8,64,512]{2,1,0:T(8,128)(2,1)}, u32[]{:S(2)}, u32[]{:S(2)}) %collective-permute-start.4) | collective-permute-done | bytes 524320 | tf_op jit(solution)/shard_map/ppermute | solution.py:16
  24.9 10.9 %collective-permute-start.1 = (bf16[8,64,512]{2,1,0:T(8,128)(2,1)}, bf16[8,64,512]{2,1,0:T(8,128)(2,1)}, u32[]{:S(2)}, u32[]{:S(2)}) collective-permute-start(bf16[8,64,512]{2,1,0:T(8,128)(2,1)} %refs_0_.1), channel_id=1, source_target_pairs={{0,2},{1,3},{2,0},{3,1},{4,6},{5,7},{6,4},{7,5},{8,10},{9,11},{10,... | collective-permute-start | bytes 1572872 | tf_op jit(solution)/shard_map/ppermute | solution.py:16
  35.7 2.9 %collective-permute-done.11.refs_0_ = bf16[8,64,512]{2,1,0:T(8,128)(2,1)S(1)} collective-permute-done((bf16[8,64,512]{2,1,0:T(8,128)(2,1)}, bf16[8,64,512]{2,1,0:T(8,128)(2,1)S(1)}, u32[]{:S(2)}, u32[]{:S(2)}) %collective-permute-start.11) | collective-permute-done | bytes 524320 | tf_op jit(solution)/shard_map/ppermute | solution.py:16
  38.6 1.0 broadcast_select_fusion
  40.1 5.2 %collective-permute-done.9 = s32[8,32]{1,0:T(8,128)S(1)} collective-permute-done((s32[8,32]{1,0:T(8,128)S(1)}, s32[8,32]{1,0:T(8,128)S(1)}, u32[]{:S(2)}, u32[]{:S(2)}) %collective-permute-start.9) | collective-permute-done | bytes 1056 | tf_op jit(solution)/shard_map/ppermute | solution.py:273
  45.3 2.6 %collective-permute-start.18 = (bf16[4,64,512]{2,1,0:T(8,128)(2,1)S(1)}, bf16[4,64,512]{2,1,0:T(8,128)(2,1)S(1)}, u32[]{:S(2)}, u32[]{:S(2)}) collective-permute-start(bf16[4,64,512]{2,1,0:T(8,128)(2,1)S(1)} %get-tuple-element.45), channel_id=1, source_target_pairs={{0,4},{1,5},{2,6},{3,7},{4,0},{5,1},{6,2},{7,3},{8,12},{9,13},{10,... | collective-permute-start | bytes 786440 | tf_op jit(solution)/shard_map/ppermute | solution.py:16
  47.9 0.6 collective-permute-done.1.refs_2_
  48.5 1.3 %collective-permute-start.6 = (bf16[8,64,512]{2,1,0:T(8,128)(2,1)}, bf16[8,64,512]{2,1,0:T(8,128)(2,1)S(1)}, u32[]{:S(2)}, u32[]{:S(2)}) collective-permute-start(bf16[8,64,512]{2,1,0:T(8,128)(2,1)} %collective-permute-done.5.refs_0_), channel_id=1, source_target_pairs={{0,1},{2,3},{5,4},{7,6},{8,9},{10,11},{13,12},{15,14},{16,17},{18,... | collective-permute-start | bytes 1572872 | tf_op jit(solution)/shard_map/ppermute | solution.py:16
  49.9 5.4 %collective-permute-done.12.refs_3_ = bf16[8,64,512]{2,1,0:T(8,128)(2,1)S(1)} collective-permute-done((bf16[8,64,512]{2,1,0:T(8,128)(2,1)S(1)}, bf16[8,64,512]{2,1,0:T(8,128)(2,1)S(1)}, u32[]{:S(2)}, u32[]{:S(2)}) %collective-permute-start.12) | collective-permute-done | bytes 524320 | tf_op jit(solution)/shard_map/ppermute | solution.py:16
  55.7 3.3 %collective-permute-start.7 = (bf16[8,64,512]{2,1,0:T(8,128)(2,1)}, bf16[8,64,512]{2,1,0:T(8,128)(2,1)}, u32[]{:S(2)}, u32[]{:S(2)}) collective-permute-start(bf16[8,64,512]{2,1,0:T(8,128)(2,1)} %collective-permute-done.4.refs_2_.refs_9_), channel_id=1, source_target_pairs={{0,1},{3,2},{4,5},{7,6},{8,9},{11,10},{12,13},{15,14},{16,17},{19,... | collective-permute-start | bytes 1572872 | tf_op jit(solution)/shard_map/ppermute | solution.py:16
  59.0 0.5 collective-permute-start.15
  59.5 1.3 %collective-permute-start.19 = (bf16[4,64,512]{2,1,0:T(8,128)(2,1)S(1)}, bf16[4,64,512]{2,1,0:T(8,128)(2,1)S(1)}, u32[]{:S(2)}, u32[]{:S(2)}) collective-permute-start(bf16[4,64,512]{2,1,0:T(8,128)(2,1)S(1)} %collective-permute-done.18.refs_7_), channel_id=1, source_target_pairs={{1,0},{3,2},{4,5},{6,7},{9,8},{11,10},{12,13},{14,15},{17,16},{19,... | collective-permute-start | bytes 786440 | tf_op jit(solution)/shard_map/ppermute | solution.py:16
  60.8 1.3 %collective-permute-start.17 = (bf16[4,64,512]{2,1,0:T(8,128)(2,1)S(1)}, bf16[4,64,512]{2,1,0:T(8,128)(2,1)}, u32[]{:S(2)}, u32[]{:S(2)}) collective-permute-start(bf16[4,64,512]{2,1,0:T(8,128)(2,1)S(1)} %collective-permute-done.16.refs_5_), channel_id=1, source_target_pairs={{1,0},{3,2},{4,5},{6,7},{9,8},{11,10},{12,13},{14,15},{17,16},{19,... | collective-permute-start | bytes 786440 | tf_op jit(solution)/shard_map/ppermute | solution.py:16
  62.2 5.9 %shard_map.37 = (bf16[512,512]{1,0:T(8,128)(2,1)}, bf16[256,1536]{1,0:T(8,128)(2,1)}, bf16[256,1536]{1,0:T(8,128)(2,1)}, bf16[512,1024]{1,0:T(8,128)(2,1)}, f32[512,1024]{1,0:T(8,128)}) custom-call(s32[31]{0:T(128)S(1)} %concatenate.12.meta_ref, s32[19]{0:T(128)S(1)} %concatenate.13.dest_ref, bf16[8,64,512]{2,1,0:T(8,128)(2,1)} %refs_0_.1, ...), custom_call_target="tpu_custom_call" | custom-call | flops 1073741824 | bytes 12582912 | tf_op jit(solution)/shard_map/pallas_call | solution.py:383
  68.2 4.4 %shard_map.38 = (bf16[512,1024]{1,0:T(8,128)(2,1)}, f32[4,64,512]{2,1,0:T(8,128)}, f32[4,64,512]{2,1,0:T(8,128)}) custom-call(s32[31]{0:T(128)S(1)} %concatenate.12.meta_ref, s32[15]{0:T(128)S(1)} %concatenate.14.dest_ref, bf16[512,512]{1,0:T(8,128)(2,1)} %get-tuple-element.26.left_in, f32[512,1024]{1,0:T(8,128)} %get-tuple-element.27.before_in, ...), custom_call_target="tpu_custom_call" | custom-call | flops 1073741824 | bytes 12582912 | tf_op jit(solution)/shard_map/pallas_call | solution.py:409
  72.6 3.8 %shard_map.39 = (bf16[1536,1024]{1,0:T(8,128)(2,1)S(1)}, f32[4,64,512]{2,1,0:T(8,128)S(1)}, bf16[4,64,512]{2,1,0:T(8,128)(2,1)S(1)}) custom-call(s32[31]{0:T(128)S(1)} %concatenate.12.meta_ref, s32[44]{0:T(128)S(1)} %concatenate.15.dest_ref, bf16[256,1536]{1,0:T(8,128)(2,1)} %get-tuple-element.33.left_ref, f32[4,64,512]{2,1,0:T(8,128)} %get-tuple-element.34.base_ref, ...), custom_call_target="tpu_custom_call" | custom-call | flops 3221225472 | bytes 12582912 | tf_op jit(solution)/shard_map/pallas_call | solution.py:435
  76.4 0.9 collective-permute-start.24
  77.3 2.4 %shard_map.40 = (f32[4,64,512]{2,1,0:T(8,128)S(1)}, bf16[4,64,512]{2,1,0:T(8,128)(2,1)S(1)}) custom-call(s32[31]{0:T(128)S(1)} %concatenate.12.meta_ref, bf16[256,1536]{1,0:T(8,128)(2,1)} %get-tuple-element.24.left_ref, f32[4,64,512]{2,1,0:T(8,128)} %get-tuple-element.29.base_ref, bf16[1536,1024]{1,0:T(8,128)(2,1)S(1)} %get-tuple-element.36.table_ref.table_b), custom_call_target="tpu_custom_call" | custom-call | flops 1610612736 | bytes 12582912 | tf_op jit(solution)/shard_map/pallas_call | solution.py:448
  79.7 1.3 %collective-permute-start.21 = (bf16[4,64,512]{2,1,0:T(8,128)(2,1)S(1)}, bf16[4,64,512]{2,1,0:T(8,128)(2,1)S(1)}, u32[]{:S(2)}, u32[]{:S(2)}) collective-permute-start(bf16[4,64,512]{2,1,0:T(8,128)(2,1)S(1)} %get-tuple-element.37.own_ref), channel_id=1, source_target_pairs={{0,2},{1,3},{2,0},{3,1},{4,6},{5,7},{6,4},{7,5},{8,10},{9,11},{10,... | collective-permute-start | bytes 786440 | tf_op jit(solution)/shard_map/ppermute | solution.py:16
  81.0 1.6 %collective-permute-start.23 = (bf16[4,64,512]{2,1,0:T(8,128)(2,1)S(1)}, bf16[4,64,512]{2,1,0:T(8,128)(2,1)S(1)}, u32[]{:S(2)}, u32[]{:S(2)}) collective-permute-start(bf16[4,64,512]{2,1,0:T(8,128)(2,1)S(1)} %get-tuple-element.41.own_ref), channel_id=1, source_target_pairs={{0,1},{1,0},{2,3},{3,2},{4,5},{5,4},{6,7},{7,6},{8,9},{9,8},{10,11... | collective-permute-start | bytes 786440 | tf_op jit(solution)/shard_map/ppermute | solution.py:16
  82.6 1.8 %collective-permute-done.24.x_ref = bf16[4,64,512]{2,1,0:T(8,128)(2,1)S(1)} collective-permute-done((bf16[4,64,512]{2,1,0:T(8,128)(2,1)S(1)}, bf16[4,64,512]{2,1,0:T(8,128)(2,1)S(1)}, u32[]{:S(2)}, u32[]{:S(2)}) %collective-permute-start.24) | collective-permute-done | bytes 262176 | tf_op jit(solution)/shard_map/ppermute | solution.py:16
  84.5 2.5 %collective-permute-start.25 = (bf16[4,64,512]{2,1,0:T(8,128)(2,1)S(1)}, bf16[4,64,512]{2,1,0:T(8,128)(2,1)S(1)}, u32[]{:S(2)}, u32[]{:S(2)}) collective-permute-start(bf16[4,64,512]{2,1,0:T(8,128)(2,1)S(1)} %collective-permute-done.24.x_ref), channel_id=1, source_target_pairs={{0,1},{1,0},{2,3},{3,2},{4,5},{5,4},{6,7},{7,6},{8,9},{9,8},{10,11... | collective-permute-start | bytes 786440 | tf_op jit(solution)/shard_map/ppermute | solution.py:16
  87.0 3.1 %collective-permute-done.21.x_ref = bf16[4,64,512]{2,1,0:T(8,128)(2,1)S(1)} collective-permute-done((bf16[4,64,512]{2,1,0:T(8,128)(2,1)S(1)}, bf16[4,64,512]{2,1,0:T(8,128)(2,1)S(1)}, u32[]{:S(2)}, u32[]{:S(2)}) %collective-permute-start.21) | collective-permute-done | bytes 262176 | tf_op jit(solution)/shard_map/ppermute | solution.py:16
  90.1 1.0 %collective-permute-start.22 = (bf16[4,64,512]{2,1,0:T(8,128)(2,1)S(1)}, bf16[4,64,512]{2,1,0:T(8,128)(2,1)S(1)}, u32[]{:S(2)}, u32[]{:S(2)}) collective-permute-start(bf16[4,64,512]{2,1,0:T(8,128)(2,1)S(1)} %collective-permute-done.21.x_ref), channel_id=1, source_target_pairs={{0,1},{1,0},{2,3},{3,2},{4,5},{5,4},{6,7},{7,6},{8,9},{9,8},{10,11... | collective-permute-start | bytes 786440 | tf_op jit(solution)/shard_map/ppermute | solution.py:16
  91.1 3.3 %shard_map.41.refs_0_ = bf16[8,64,512]{2,1,0:T(8,128)(2,1)} custom-call(s32[31]{0:T(128)S(1)} %concatenate.12.meta_ref, bf16[4,64,512]{2,1,0:T(8,128)(2,1)S(1)} %get-tuple-element.41.own_ref, bf16[4,64,512]{2,1,0:T(8,128)(2,1)S(1)} %collective-permute-done.23.core_ref, bf16[4,64,512]{2,1,0:T(8,128)(2,1)S(1)} %collective-permute-done.24.x_ref, ...), custom_call_target="tpu_custom_call" | custom-call | flops 2684354560 | bytes 12582912 | tf_op jit(solution)/shard_map/pallas_call | solution.py:464
  94.5 3.4 %shard_map.42 = bf16[8,64,512]{2,1,0:T(8,128)(2,1)} custom-call(s32[31]{0:T(128)S(1)} %concatenate.12.meta_ref, bf16[4,64,512]{2,1,0:T(8,128)(2,1)S(1)} %get-tuple-element.37.own_ref, bf16[4,64,512]{2,1,0:T(8,128)(2,1)S(1)} %collective-permute-done.20.core_ref, ...), custom_call_target="tpu_custom_call", output_to_operand_aliasing={{}: (9, {})} | custom-call | flops 2684354560 | bytes 12582912 | tf_op jit(solution)/shard_map/pallas_call | solution.py:464
  (58 shorter events, 1.3 us)
Async XLA Ops:
  0.0 39.9 %copy-start.5 = (s32[8,32]{1,0:T(8,128)S(1)}, s32[8,32]{1,0:T(8,128)}, u32[]{:S(2)}) copy-start(s32[8,32]{1,0:T(8,128)} %param.4) | copy-start | bytes 3076
  0.0 39.9 %collective-permute-start.8 = (s32[8,32]{1,0:T(8,128)}, s32[8,32]{1,0:T(8,128)S(1)}, u32[]{:S(2)}, u32[]{:S(2)}) collective-permute-start(s32[8,32]{1,0:T(8,128)} %param.4), channel_id=1, source_target_pairs={{28,0},{8,4},{4,8},{16,12},{12,16},{24,20},{20,24},{0,28},{29,1},{... | collective-permute-start | bytes 3080 | tf_op jit(solution)/shard_map/ppermute | solution.py:273
  6.0 5.3 %collective-permute-start.3 = (s32[8,32]{1,0:T(8,128)}, s32[8,32]{1,0:T(8,128)S(1)}, u32[]{:S(2)}, u32[]{:S(2)}) collective-permute-start(s32[8,32]{1,0:T(8,128)} %param.4), channel_id=1, source_target_pairs={{4,0},{0,4},{12,8},{8,12},{20,16},{16,20},{28,24},{24,28},{5,1},{1... | collective-permute-start | bytes 3080 | tf_op jit(solution)/shard_map/ppermute | solution.py:273
  6.0 18.8 %collective-permute-start.4 = (bf16[8,64,512]{2,1,0:T(8,128)(2,1)}, bf16[8,64,512]{2,1,0:T(8,128)(2,1)}, u32[]{:S(2)}, u32[]{:S(2)}) collective-permute-start(bf16[8,64,512]{2,1,0:T(8,128)(2,1)} %refs_0_.1), channel_id=1, source_target_pairs={{0,30},{1,31},{2,4},{3,5},{4,2},{5,3},{6,8},{7,9},{8,6},{9,7},{10,... | collective-permute-start | bytes 1572872 | tf_op jit(solution)/shard_map/ppermute | solution.py:16
  8.9 16.0 %collective-permute-start.13 = (bf16[8,64,512]{2,1,0:T(8,128)(2,1)}, bf16[8,64,512]{2,1,0:T(8,128)(2,1)S(1)}, u32[]{:S(2)}, u32[]{:S(2)}) collective-permute-start(bf16[8,64,512]{2,1,0:T(8,128)(2,1)} %refs_0_.1), channel_id=1, source_target_pairs={{1,9},{2,26},{3,27},{4,12},{5,13},{6,30},{9,17},{10,2},{11,3},{12,... | collective-permute-start | bytes 1572872 | tf_op jit(solution)/shard_map/ppermute | solution.py:16
  9.6 29.1 %collective-permute-start.11 = (bf16[8,64,512]{2,1,0:T(8,128)(2,1)}, bf16[8,64,512]{2,1,0:T(8,128)(2,1)S(1)}, u32[]{:S(2)}, u32[]{:S(2)}) collective-permute-start(bf16[8,64,512]{2,1,0:T(8,128)(2,1)} %refs_0_.1), channel_id=1, source_target_pairs={{0,24},{1,25},{2,10},{3,11},{4,28},{5,29},{6,14},{7,15},{8,0},{9,1... | collective-permute-start | bytes 1572872 | tf_op jit(solution)/shard_map/ppermute | solution.py:16
  11.4 28.6 %collective-permute-start.10 = (s32[8,32]{1,0:T(8,128)}, s32[8,32]{1,0:T(8,128)S(1)}, u32[]{:S(2)}, u32[]{:S(2)}) collective-permute-start(s32[8,32]{1,0:T(8,128)} %param.4), channel_id=1, source_target_pairs={{8,0},{12,4},{16,8},{20,12},{24,16},{28,20},{0,24},{4,28},{9,1},{1... | collective-permute-start | bytes 3080 | tf_op jit(solution)/shard_map/ppermute | solution.py:273
  24.8 23.1 %collective-permute-start.5 = (bf16[8,64,512]{2,1,0:T(8,128)(2,1)}, bf16[8,64,512]{2,1,0:T(8,128)(2,1)}, u32[]{:S(2)}, u32[]{:S(2)}) collective-permute-start(bf16[8,64,512]{2,1,0:T(8,128)(2,1)} %refs_0_.1), channel_id=1, source_target_pairs={{0,4},{1,5},{2,6},{3,7},{4,0},{5,1},{6,2},{7,3},{8,12},{9,13},{10,... | collective-permute-start | bytes 1572872 | tf_op jit(solution)/shard_map/ppermute | solution.py:16
  24.9 15.1 %copy-start.2 = (bf16[8,64,512]{2,1,0:T(8,128)(2,1)}, bf16[8,64,512]{2,1,0:T(8,128)(2,1)S(1)}, u32[]{:S(2)}) copy-start(bf16[8,64,512]{2,1,0:T(8,128)(2,1)S(1)} %collective-permute-done.13.refs_1_) | copy-start | bytes 1572868
  24.9 23.7 %collective-permute-start.1 = (bf16[8,64,512]{2,1,0:T(8,128)(2,1)}, bf16[8,64,512]{2,1,0:T(8,128)(2,1)}, u32[]{:S(2)}, u32[]{:S(2)}) collective-permute-start(bf16[8,64,512]{2,1,0:T(8,128)(2,1)} %refs_0_.1), channel_id=1, source_target_pairs={{0,2},{1,3},{2,0},{3,1},{4,6},{5,7},{6,4},{7,5},{8,10},{9,11},{10,... | collective-permute-start | bytes 1572872 | tf_op jit(solution)/shard_map/ppermute | solution.py:16
  38.6 20.3 %copy-start.3 = (bf16[8,64,512]{2,1,0:T(8,128)(2,1)}, bf16[8,64,512]{2,1,0:T(8,128)(2,1)S(1)}, u32[]{:S(2)}) copy-start(bf16[8,64,512]{2,1,0:T(8,128)(2,1)S(1)} %collective-permute-done.11.refs_0_) | copy-start | bytes 1572868
  38.6 16.6 %collective-permute-start.12 = (bf16[8,64,512]{2,1,0:T(8,128)(2,1)S(1)}, bf16[8,64,512]{2,1,0:T(8,128)(2,1)S(1)}, u32[]{:S(2)}, u32[]{:S(2)}) collective-permute-start(bf16[8,64,512]{2,1,0:T(8,128)(2,1)S(1)} %collective-permute-done.11.refs_0_), channel_id=1, source_target_pairs={{0,2},{1,3},{2,0},{3,1},{4,6},{5,7},{6,4},{7,5},{8,10},{9,11},{10,... | collective-permute-start | bytes 1572872 | tf_op jit(solution)/shard_map/ppermute | solution.py:16
  39.9 5.5 %collective-permute-start.9 = (s32[8,32]{1,0:T(8,128)S(1)}, s32[8,32]{1,0:T(8,128)S(1)}, u32[]{:S(2)}, u32[]{:S(2)}) collective-permute-start(s32[8,32]{1,0:T(8,128)S(1)} %copy-done.5), channel_id=1, source_target_pairs={{24,0},{28,4},{0,8},{4,12},{8,16},{12,20},{16,24},{20,28},{25,1},{... | collective-permute-start | bytes 3080 | tf_op jit(solution)/shard_map/ppermute | solution.py:273
  40.0 15.7 %collective-permute-start = (bf16[8,64,512]{2,1,0:T(8,128)(2,1)}, bf16[8,64,512]{2,1,0:T(8,128)(2,1)S(1)}, u32[]{:S(2)}, u32[]{:S(2)}) collective-permute-start(bf16[8,64,512]{2,1,0:T(8,128)(2,1)} %refs_0_.1), channel_id=1, source_target_pairs={{0,1},{1,0},{2,3},{3,2},{4,5},{5,4},{6,7},{7,6},{8,9},{9,8},{10,11... | collective-permute-start | bytes 1572872 | tf_op jit(solution)/shard_map/ppermute | solution.py:16
  45.3 13.6 %collective-permute-start.18 = (bf16[4,64,512]{2,1,0:T(8,128)(2,1)S(1)}, bf16[4,64,512]{2,1,0:T(8,128)(2,1)S(1)}, u32[]{:S(2)}, u32[]{:S(2)}) collective-permute-start(bf16[4,64,512]{2,1,0:T(8,128)(2,1)S(1)} %get-tuple-element.45), channel_id=1, source_target_pairs={{0,4},{1,5},{2,6},{3,7},{4,0},{5,1},{6,2},{7,3},{8,12},{9,13},{10,... | collective-permute-start | bytes 786440 | tf_op jit(solution)/shard_map/ppermute | solution.py:16
  47.9 11.1 %collective-permute-start.16 = (bf16[4,64,512]{2,1,0:T(8,128)(2,1)S(1)}, bf16[4,64,512]{2,1,0:T(8,128)(2,1)S(1)}, u32[]{:S(2)}, u32[]{:S(2)}) collective-permute-start(bf16[4,64,512]{2,1,0:T(8,128)(2,1)S(1)} %get-tuple-element.46), channel_id=1, source_target_pairs={{0,4},{1,5},{2,6},{3,7},{4,0},{5,1},{6,2},{7,3},{8,12},{9,13},{10,... | collective-permute-start | bytes 786440 | tf_op jit(solution)/shard_map/ppermute | solution.py:16
  48.5 11.0 %collective-permute-start.6 = (bf16[8,64,512]{2,1,0:T(8,128)(2,1)}, bf16[8,64,512]{2,1,0:T(8,128)(2,1)S(1)}, u32[]{:S(2)}, u32[]{:S(2)}) collective-permute-start(bf16[8,64,512]{2,1,0:T(8,128)(2,1)} %collective-permute-done.5.refs_0_), channel_id=1, source_target_pairs={{0,1},{2,3},{5,4},{7,6},{8,9},{10,11},{13,12},{15,14},{16,17},{18,... | collective-permute-start | bytes 1572872 | tf_op jit(solution)/shard_map/ppermute | solution.py:16
  55.3 5.6 %collective-permute-start.2 = (bf16[8,64,512]{2,1,0:T(8,128)(2,1)}, bf16[8,64,512]{2,1,0:T(8,128)(2,1)S(1)}, u32[]{:S(2)}, u32[]{:S(2)}) collective-permute-start(bf16[8,64,512]{2,1,0:T(8,128)(2,1)} %collective-permute-done.1.refs_2_), channel_id=1, source_target_pairs={{0,1},{1,0},{2,3},{3,2},{4,5},{5,4},{6,7},{7,6},{8,9},{9,8},{10,11... | collective-permute-start | bytes 1572872 | tf_op jit(solution)/shard_map/ppermute | solution.py:16
  55.7 12.5 %collective-permute-start.7 = (bf16[8,64,512]{2,1,0:T(8,128)(2,1)}, bf16[8,64,512]{2,1,0:T(8,128)(2,1)}, u32[]{:S(2)}, u32[]{:S(2)}) collective-permute-start(bf16[8,64,512]{2,1,0:T(8,128)(2,1)} %collective-permute-done.4.refs_2_.refs_9_), channel_id=1, source_target_pairs={{0,1},{3,2},{4,5},{7,6},{8,9},{11,10},{12,13},{15,14},{16,17},{19,... | collective-permute-start | bytes 1572872 | tf_op jit(solution)/shard_map/ppermute | solution.py:16
  59.0 13.6 %collective-permute-start.14 = (bf16[8,64,512]{2,1,0:T(8,128)(2,1)}, bf16[8,64,512]{2,1,0:T(8,128)(2,1)S(1)}, u32[]{:S(2)}, u32[]{:S(2)}) collective-permute-start(bf16[8,64,512]{2,1,0:T(8,128)(2,1)} %broadcast_select_fusion), channel_id=1, source_target_pairs={{0,1},{1,0},{2,3},{3,2},{4,5},{5,4},{6,7},{7,6},{8,9},{9,8},{10,11... | collective-permute-start | bytes 1572872 | tf_op jit(solution)/shard_map/ppermute | solution.py:16
  59.0 13.6 %collective-permute-start.15 = (bf16[8,64,512]{2,1,0:T(8,128)(2,1)S(1)}, bf16[8,64,512]{2,1,0:T(8,128)(2,1)S(1)}, u32[]{:S(2)}, u32[]{:S(2)}) collective-permute-start(bf16[8,64,512]{2,1,0:T(8,128)(2,1)S(1)} %collective-permute-done.12.refs_3_), channel_id=1, source_target_pairs={{0,1},{1,0},{2,3},{3,2},{4,5},{5,4},{6,7},{7,6},{8,9},{9,8},{10,11... | collective-permute-start | bytes 1572872 | tf_op jit(solution)/shard_map/ppermute | solution.py:16
  59.5 2.6 %copy-start.4 = (bf16[8,64,512]{2,1,0:T(8,128)(2,1)}, bf16[8,64,512]{2,1,0:T(8,128)(2,1)S(1)}, u32[]{:S(2)}) copy-start(bf16[8,64,512]{2,1,0:T(8,128)(2,1)S(1)} %collective-permute-done.6.refs_1_) | copy-start | bytes 1572868
  59.5 13.1 %collective-permute-start.19 = (bf16[4,64,512]{2,1,0:T(8,128)(2,1)S(1)}, bf16[4,64,512]{2,1,0:T(8,128)(2,1)S(1)}, u32[]{:S(2)}, u32[]{:S(2)}) collective-permute-start(bf16[4,64,512]{2,1,0:T(8,128)(2,1)S(1)} %collective-permute-done.18.refs_7_), channel_id=1, source_target_pairs={{1,0},{3,2},{4,5},{6,7},{9,8},{11,10},{12,13},{14,15},{17,16},{19,... | collective-permute-start | bytes 786440 | tf_op jit(solution)/shard_map/ppermute | solution.py:16
  60.8 11.8 %collective-permute-start.17 = (bf16[4,64,512]{2,1,0:T(8,128)(2,1)S(1)}, bf16[4,64,512]{2,1,0:T(8,128)(2,1)}, u32[]{:S(2)}, u32[]{:S(2)}) collective-permute-start(bf16[4,64,512]{2,1,0:T(8,128)(2,1)S(1)} %collective-permute-done.16.refs_5_), channel_id=1, source_target_pairs={{1,0},{3,2},{4,5},{6,7},{9,8},{11,10},{12,13},{14,15},{17,16},{19,... | collective-permute-start | bytes 786440 | tf_op jit(solution)/shard_map/ppermute | solution.py:16
  76.4 14.7 %copy-start = (bf16[512,1024]{1,0:T(8,128)(2,1)S(1)}, bf16[512,1024]{1,0:T(8,128)(2,1)}, u32[]{:S(2)}) copy-start(bf16[512,1024]{1,0:T(8,128)(2,1)} %get-tuple-element.39.table_near) | copy-start | bytes 3145732
  76.4 14.7 %copy-start.1 = (bf16[512,1024]{1,0:T(8,128)(2,1)S(1)}, bf16[512,1024]{1,0:T(8,128)(2,1)}, u32[]{:S(2)}) copy-start(bf16[512,1024]{1,0:T(8,128)(2,1)} %get-tuple-element.38.table_own) | copy-start | bytes 3145732
  76.4 8.0 %collective-permute-start.24 = (bf16[4,64,512]{2,1,0:T(8,128)(2,1)S(1)}, bf16[4,64,512]{2,1,0:T(8,128)(2,1)S(1)}, u32[]{:S(2)}, u32[]{:S(2)}) collective-permute-start(bf16[4,64,512]{2,1,0:T(8,128)(2,1)S(1)} %get-tuple-element.41.own_ref), channel_id=1, source_target_pairs={{0,2},{1,3},{2,0},{3,1},{4,6},{5,7},{6,4},{7,5},{8,10},{9,11},{10,... | collective-permute-start | bytes 786440 | tf_op jit(solution)/shard_map/ppermute | solution.py:16
  79.7 10.3 %collective-permute-start.21 = (bf16[4,64,512]{2,1,0:T(8,128)(2,1)S(1)}, bf16[4,64,512]{2,1,0:T(8,128)(2,1)S(1)}, u32[]{:S(2)}, u32[]{:S(2)}) collective-permute-start(bf16[4,64,512]{2,1,0:T(8,128)(2,1)S(1)} %get-tuple-element.37.own_ref), channel_id=1, source_target_pairs={{0,2},{1,3},{2,0},{3,1},{4,6},{5,7},{6,4},{7,5},{8,10},{9,11},{10,... | collective-permute-start | bytes 786440 | tf_op jit(solution)/shard_map/ppermute | solution.py:16
  81.0 10.1 %collective-permute-start.23 = (bf16[4,64,512]{2,1,0:T(8,128)(2,1)S(1)}, bf16[4,64,512]{2,1,0:T(8,128)(2,1)S(1)}, u32[]{:S(2)}, u32[]{:S(2)}) collective-permute-start(bf16[4,64,512]{2,1,0:T(8,128)(2,1)S(1)} %get-tuple-element.41.own_ref), channel_id=1, source_target_pairs={{0,1},{1,0},{2,3},{3,2},{4,5},{5,4},{6,7},{7,6},{8,9},{9,8},{10,11... | collective-permute-start | bytes 786440 | tf_op jit(solution)/shard_map/ppermute | solution.py:16
  84.5 6.7 %collective-permute-start.25 = (bf16[4,64,512]{2,1,0:T(8,128)(2,1)S(1)}, bf16[4,64,512]{2,1,0:T(8,128)(2,1)S(1)}, u32[]{:S(2)}, u32[]{:S(2)}) collective-permute-start(bf16[4,64,512]{2,1,0:T(8,128)(2,1)S(1)} %collective-permute-done.24.x_ref), channel_id=1, source_target_pairs={{0,1},{1,0},{2,3},{3,2},{4,5},{5,4},{6,7},{7,6},{8,9},{9,8},{10,11... | collective-permute-start | bytes 786440 | tf_op jit(solution)/shard_map/ppermute | solution.py:16
  87.0 7.5 %collective-permute-start.20 = (bf16[4,64,512]{2,1,0:T(8,128)(2,1)S(1)}, bf16[4,64,512]{2,1,0:T(8,128)(2,1)S(1)}, u32[]{:S(2)}, u32[]{:S(2)}) collective-permute-start(bf16[4,64,512]{2,1,0:T(8,128)(2,1)S(1)} %get-tuple-element.37.own_ref), channel_id=1, source_target_pairs={{0,1},{1,0},{2,3},{3,2},{4,5},{5,4},{6,7},{7,6},{8,9},{9,8},{10,11... | collective-permute-start | bytes 786440 | tf_op jit(solution)/shard_map/ppermute | solution.py:16
  90.1 4.4 %collective-permute-start.22 = (bf16[4,64,512]{2,1,0:T(8,128)(2,1)S(1)}, bf16[4,64,512]{2,1,0:T(8,128)(2,1)S(1)}, u32[]{:S(2)}, u32[]{:S(2)}) collective-permute-start(bf16[4,64,512]{2,1,0:T(8,128)(2,1)S(1)} %collective-permute-done.21.x_ref), channel_id=1, source_target_pairs={{0,1},{1,0},{2,3},{3,2},{4,5},{5,4},{6,7},{7,6},{8,9},{9,8},{10,11... | collective-permute-start | bytes 786440 | tf_op jit(solution)/shard_map/ppermute | solution.py:16
